TPU v7x, 32 devices: a whole 2x2x4 slice. The times are simulated.
32 devices in a mesh: rep: 4 (over y, x), fsdp: 8 (over z, core).
Axes of the slice: x: 2, y: 2, z: 4, core: 2. Of those that a mesh axis runs over, the one named last changes fastest.
Arguments:
- global_views: bfloat16 [320, 14, 14, 1024], P(('rep', 'fsdp')), may hold values from -6 to 6
- local_views: bfloat16 [640, 6, 6, 1024], P(('rep', 'fsdp')), may hold values from -6 to 6
- live_images: int32 [32], P(('rep', 'fsdp')), may hold values from 1 to 5, as said below
- first_reduce: bfloat16 [1024, 256], P(None, 'fsdp'), may hold values from -0.1875 to 0.1875
- first_spatial: bfloat16 [2304, 256], P(None, 'fsdp'), may hold values from -0.125 to 0.125
- first_expand: bfloat16 [256, 1024], P(None, 'fsdp'), may hold values from -0.375 to 0.375
- first_norms: bfloat16 [2, 1536], P(None, 'fsdp'), may hold values from 0.3984375 to 1.3984375
- second_reduce: bfloat16 [1024, 512], P(None, 'fsdp'), may hold values from -0.1875 to 0.1875
- second_spatial: bfloat16 [4608, 512], P(None, 'fsdp'), may hold values from -0.09375 to 0.09375
- second_expand: bfloat16 [512, 2048], P(None, 'fsdp'), may hold values from -0.25 to 0.25
- second_short: bfloat16 [1024, 2048], P(None, 'fsdp'), may hold values from -0.1875 to 0.1875
- second_norms: bfloat16 [2, 5120], P(None, 'fsdp'), may hold values from 0.3984375 to 1.3984375
- global_cotan: bfloat16 [320, 7, 7, 2048], P(('rep', 'fsdp')), may hold values from -6 to 6
- local_cotan: bfloat16 [640, 3, 3, 2048], P(('rep', 'fsdp')), may hold values from -6 to 6
Outputs:
- first_global: bfloat16 [320, 14, 14, 1024], P(('rep', 'fsdp'))
- first_local: bfloat16 [640, 6, 6, 1024], P(('rep', 'fsdp'))
- second_global: bfloat16 [320, 7, 7, 2048], P(('rep', 'fsdp'))
- second_local: bfloat16 [640, 3, 3, 2048], P(('rep', 'fsdp'))
- global_grad: float32 [320, 14, 14, 1024], P(('rep', 'fsdp'))
- local_grad: float32 [640, 6, 6, 1024], P(('rep', 'fsdp'))
- grad_first_reduce: float32 [1024, 256], P(None, 'fsdp')
- grad_first_spatial: float32 [2304, 256], P(None, 'fsdp')
- grad_first_expand: float32 [256, 1024], P(None, 'fsdp')
- grad_first_norms: float32 [2, 1536], P(None, 'fsdp')
- grad_second_reduce: float32 [1024, 512], P(None, 'fsdp')
- grad_second_spatial: float32 [4608, 512], P(None, 'fsdp')
- grad_second_expand: float32 [512, 2048], P(None, 'fsdp')
- grad_second_short: float32 [1024, 2048], P(None, 'fsdp')
- grad_second_norms: float32 [2, 5120], P(None, 'fsdp')
- pooled_std: float32 [], replicated
Inputs may be any that keep to these rules, and one draw needn't show every extreme that they name: `live_images`: A device with n live images holds their 2 n global and 4 n local views in its first slots; some device holds 5 images.
All inputs are finite; a program needn't handle non-finite values.
Results may differ from a plain program's by a relative error of at most 0.025.
Values may be sent and summed in bfloat16 or wider, within the bound.
A program may use at most 320 MiB of HBM per device.

v0:
```python
import jax
import jax.numpy as jnp
from jax import lax
from jax.sharding import PartitionSpec as P

EPSILON = 1e-05


def for_sending(x):
    return jax.tree.map(lambda a: a.astype(jnp.bfloat16) if a.dtype == jnp.float32 else a, x)


def sigmoid_linear(values):
    return values * jax.nn.sigmoid(values)


def silu_slope(values):
    sigmoid = jax.nn.sigmoid(values)
    return sigmoid * (1.0 + values * (1.0 - sigmoid))


def patches(feature, stride):
    padded = jnp.pad(feature, ((0, 0), (1, 1), (1, 1), (0, 0)))
    batch_views = feature.shape[0]
    out_rows = (feature.shape[1] - 1) // stride + 1
    out_cols = (feature.shape[2] - 1) // stride + 1
    pieces = []
    for shift_row in range(3):
        for shift_col in range(3):
            pieces.append(
                lax.slice(
                    padded,
                    (0, shift_row, shift_col, 0),
                    (
                        batch_views,
                        shift_row + stride * (out_rows - 1) + 1,
                        shift_col + stride * (out_cols - 1) + 1,
                        feature.shape[3],
                    ),
                    (1, stride, stride, 1),
                )
            )
    return jnp.concatenate(pieces, axis=3)


def unfold_back(grad_cols, like_shape, stride):
    blank = jnp.zeros(like_shape, jnp.float32)
    unused, pullback = jax.vjp(lambda tensor: patches(tensor, stride), blank)
    return pullback(grad_cols)[0]


def project(operand, weight):
    return jnp.dot(operand, weight, preferred_element_type=jnp.float32)


def weight_grad(lefts, rights):
    total = jnp.einsum("vhwc,vhwd->cd", lefts[0], rights[0], preferred_element_type=jnp.float32)
    return total + jnp.einsum(
        "vhwc,vhwd->cd", lefts[1], rights[1], preferred_element_type=jnp.float32
    )


def collect(params):
    return jax.tree.map(
        lambda part, own: part.astype(own.dtype),
        lax.all_gather(for_sending(params), "fsdp", axis=1, tiled=True),
        params,
    )


def combine_grads(gradients):
    shards = jax.tree.map(
        lambda part: part.astype(jnp.float32),
        lax.psum_scatter(for_sending(gradients), "fsdp", scatter_dimension=1, tiled=True),
    )
    return jax.tree.map(lambda part: part.astype(jnp.float32), lax.psum(for_sending(shards), "rep"))


def batch_norm(entries, live_mask, view_totals, extras):
    members = list(extras)
    for conv_pair, norm_params in entries:
        first_sums = []
        second_sums = []
        for resolution in range(2):
            weighted = conv_pair[resolution] * live_mask[resolution][:, None, None, None]
            first_sums.append(jnp.sum(weighted, axis=(0, 1, 2)))
            second_sums.append(jnp.sum(weighted * conv_pair[resolution], axis=(0, 1, 2)))
        members.append(jnp.stack(first_sums))
        members.append(jnp.stack(second_sums))
    summed = lax.psum(tuple(members), ("rep", "fsdp"))
    offset = len(extras)
    if offset:
        view_totals = summed[0]
    results = []
    for position, (conv_pair, norm_params) in enumerate(entries):
        first = summed[offset + 2 * position]
        second = summed[offset + 2 * position + 1]
        normed = []
        stored = []
        for resolution in range(2):
            conv_out = conv_pair[resolution]
            pixels = view_totals[resolution] * (conv_out.shape[1] * conv_out.shape[2])
            center = first[resolution] / pixels
            spread = second[resolution] / pixels - center * center
            inv_std = lax.rsqrt(spread + EPSILON)
            scaled = (conv_out - center) * inv_std
            normed.append(
                norm_params[0].astype(jnp.float32) * scaled + norm_params[1].astype(jnp.float32)
            )
            stored.append((scaled, inv_std))
        results.append((normed, stored))
    return (results, view_totals)


def norm_back(entries, live_mask, view_totals):
    members = []
    for grad_pair, stored, norm_params in entries:
        first_sums = []
        second_sums = []
        for resolution in range(2):
            first_sums.append(jnp.sum(grad_pair[resolution], axis=(0, 1, 2)))
            second_sums.append(
                jnp.sum(grad_pair[resolution] * stored[resolution][0], axis=(0, 1, 2))
            )
        members.append(jnp.stack(first_sums))
        members.append(jnp.stack(second_sums))
    summed = lax.psum(tuple(members), ("rep", "fsdp"))
    results = []
    for position, (grad_pair, stored, norm_params) in enumerate(entries):
        first = summed[2 * position]
        second = summed[2 * position + 1]
        back = []
        for resolution in range(2):
            scaled, inv_std = stored[resolution]
            pixels = view_totals[resolution] * (scaled.shape[1] * scaled.shape[2])
            core = (
                grad_pair[resolution]
                - first[resolution] / pixels
                - scaled * (second[resolution] / pixels)
            )
            factor = norm_params[0].astype(jnp.float32) * inv_std
            back.append(core * factor * live_mask[resolution][:, None, None, None])
        param_grad = jnp.stack([jnp.sum(second, axis=0), jnp.sum(first, axis=0)])
        results.append((back, param_grad))
    return results


def to_low(pair):
    return [item.astype(jnp.bfloat16) for item in pair]


def body(
    global_views,
    local_views,
    live_images,
    first_reduce,
    first_spatial,
    first_expand,
    first_norms,
    second_reduce,
    second_spatial,
    second_expand,
    second_short,
    second_norms,
    global_cotan,
    local_cotan,
):
    live_count = live_images[0]
    live_mask = [
        (jnp.arange(global_views.shape[0]) // 2 < live_count).astype(jnp.float32),
        (jnp.arange(local_views.shape[0]) // 4 < live_count).astype(jnp.float32),
    ]
    view_counts = jnp.stack([2 * live_count, 4 * live_count]).astype(jnp.float32)
    sources = [global_views, local_views]
    first_set = collect((first_reduce, first_spatial, first_expand, first_norms))
    mid_first = first_set[0].shape[1]
    results, view_totals = batch_norm(
        [([project(item, first_set[0]) for item in sources], first_set[3][:, :mid_first])],
        live_mask,
        None,
        (view_counts,),
    )
    normed_a, stored_a = results[0]
    act_a = to_low([sigmoid_linear(item) for item in normed_a])
    patch_a = [patches(item, 1) for item in act_a]
    results, unused = batch_norm(
        [
            (
                [project(item, first_set[1]) for item in patch_a],
                first_set[3][:, mid_first : 2 * mid_first],
            )
        ],
        live_mask,
        view_totals,
        (),
    )
    normed_b, stored_b = results[0]
    act_b = to_low([sigmoid_linear(item) for item in normed_b])
    results, unused = batch_norm(
        [([project(item, first_set[2]) for item in act_b], first_set[3][:, 2 * mid_first :])],
        live_mask,
        view_totals,
        (),
    )
    normed_c, stored_c = results[0]
    joined_a = [
        normed_c[resolution] + sources[resolution].astype(jnp.float32) for resolution in range(2)
    ]
    hidden = [sigmoid_linear(item) for item in joined_a]
    hidden_low = to_low(hidden)
    first_out = [
        (hidden[resolution] * live_mask[resolution][:, None, None, None]).astype(jnp.bfloat16)
        for resolution in range(2)
    ]
    second_set = collect((second_reduce, second_spatial, second_expand, second_short, second_norms))
    mid_second = second_set[0].shape[1]
    width_out = second_set[2].shape[1]
    results, unused = batch_norm(
        [([project(item, second_set[0]) for item in hidden_low], second_set[4][:, :mid_second])],
        live_mask,
        view_totals,
        (),
    )
    normed_d, stored_d = results[0]
    act_d = to_low([sigmoid_linear(item) for item in normed_d])
    patch_d = [patches(item, 2) for item in act_d]
    results, unused = batch_norm(
        [
            (
                [project(item, second_set[1]) for item in patch_d],
                second_set[4][:, mid_second : 2 * mid_second],
            )
        ],
        live_mask,
        view_totals,
        (),
    )
    normed_e, stored_e = results[0]
    act_e = to_low([sigmoid_linear(item) for item in normed_e])
    subsample = [item[:, ::2, ::2, :] for item in hidden_low]
    results, unused = batch_norm(
        [
            (
                [project(item, second_set[2]) for item in act_e],
                second_set[4][:, 2 * mid_second : 2 * mid_second + width_out],
            ),
            (
                [project(item, second_set[3]) for item in subsample],
                second_set[4][:, 2 * mid_second + width_out :],
            ),
        ],
        live_mask,
        view_totals,
        (),
    )
    normed_f, stored_f = results[0]
    normed_s, stored_s = results[1]
    joined_b = [normed_f[resolution] + normed_s[resolution] for resolution in range(2)]
    block_out = [
        sigmoid_linear(joined_b[resolution]) * live_mask[resolution][:, None, None, None]
        for resolution in range(2)
    ]
    second_out = to_low(block_out)
    pooled_first = jnp.zeros((width_out,), jnp.float32)
    pooled_second = jnp.zeros((width_out,), jnp.float32)
    for resolution in range(2):
        pooled = jnp.mean(block_out[resolution], axis=(1, 2))
        normed_pool = pooled * lax.rsqrt(jnp.mean(pooled * pooled, axis=1, keepdims=True) + 1e-06)
        weighted = normed_pool * live_mask[resolution][:, None]
        pooled_first = pooled_first + jnp.sum(weighted, axis=0)
        pooled_second = pooled_second + jnp.sum(weighted * normed_pool, axis=0)
    pooled_sums = lax.psum((pooled_first, pooled_second), ("rep", "fsdp"))
    total_views = view_totals[0] + view_totals[1]
    center = pooled_sums[0] / total_views
    spread = pooled_sums[1] / total_views - center * center
    pooled_std = jnp.mean(jnp.sqrt(spread + 1e-06))
    second_back = collect(
        (second_reduce, second_spatial, second_expand, second_short, second_norms)
    )
    cotans = [global_cotan, local_cotan]
    grad_joined = [
        cotans[resolution].astype(jnp.float32)
        * live_mask[resolution][:, None, None, None]
        * silu_slope(joined_b[resolution])
        for resolution in range(2)
    ]
    results = norm_back(
        [
            (grad_joined, stored_f, second_back[4][:, 2 * mid_second : 2 * mid_second + width_out]),
            (grad_joined, stored_s, second_back[4][:, 2 * mid_second + width_out :]),
        ],
        live_mask,
        view_totals,
    )
    low_f = to_low(results[0][0])
    low_s = to_low(results[1][0])
    norm_grad_f = results[0][1]
    norm_grad_s = results[1][1]
    wgrad_f = weight_grad(act_e, low_f)
    wgrad_s = weight_grad(subsample, low_s)
    back_e = [
        project(low_f[resolution], second_back[2].T) * silu_slope(normed_e[resolution])
        for resolution in range(2)
    ]
    results = norm_back(
        [(back_e, stored_e, second_back[4][:, mid_second : 2 * mid_second])], live_mask, view_totals
    )
    low_e = to_low(results[0][0])
    norm_grad_e = results[0][1]
    wgrad_e = weight_grad(patch_d, low_e)
    back_d = [
        unfold_back(project(low_e[resolution], second_back[1].T), act_d[resolution].shape, 2)
        * silu_slope(normed_d[resolution])
        for resolution in range(2)
    ]
    results = norm_back(
        [(back_d, stored_d, second_back[4][:, :mid_second])], live_mask, view_totals
    )
    low_d = to_low(results[0][0])
    norm_grad_d = results[0][1]
    wgrad_d = weight_grad(hidden_low, low_d)
    back_hidden = []
    for resolution in range(2):
        through_reduce = project(low_d[resolution], second_back[0].T)
        through_short = project(low_s[resolution], second_back[3].T)
        back_hidden.append(through_reduce.at[:, ::2, ::2, :].add(through_short))
    second_grads = combine_grads((wgrad_d, wgrad_e, wgrad_f, wgrad_s))
    first_back = collect((first_reduce, first_spatial, first_expand, first_norms))
    back_joined = [
        back_hidden[resolution] * silu_slope(joined_a[resolution]) for resolution in range(2)
    ]
    results = norm_back(
        [(back_joined, stored_c, first_back[3][:, 2 * mid_first :])], live_mask, view_totals
    )
    low_c = to_low(results[0][0])
    norm_grad_c = results[0][1]
    wgrad_c = weight_grad(act_b, low_c)
    back_b = [
        project(low_c[resolution], first_back[2].T) * silu_slope(normed_b[resolution])
        for resolution in range(2)
    ]
    results = norm_back(
        [(back_b, stored_b, first_back[3][:, mid_first : 2 * mid_first])], live_mask, view_totals
    )
    low_b = to_low(results[0][0])
    norm_grad_b = results[0][1]
    wgrad_b = weight_grad(patch_a, low_b)
    back_a = [
        unfold_back(project(low_b[resolution], first_back[1].T), act_a[resolution].shape, 1)
        * silu_slope(normed_a[resolution])
        for resolution in range(2)
    ]
    results = norm_back([(back_a, stored_a, first_back[3][:, :mid_first])], live_mask, view_totals)
    low_a = to_low(results[0][0])
    norm_grad_a = results[0][1]
    wgrad_a = weight_grad(sources, low_a)
    input_grads = [
        back_joined[resolution] + project(low_a[resolution], first_back[0].T)
        for resolution in range(2)
    ]
    first_grads = combine_grads((wgrad_a, wgrad_b, wgrad_c))
    first_width = first_norms.shape[1]
    second_width = second_norms.shape[1]
    first_norm_full = jnp.concatenate([norm_grad_a, norm_grad_b, norm_grad_c], axis=1)
    second_norm_full = jnp.concatenate([norm_grad_d, norm_grad_e, norm_grad_f, norm_grad_s], axis=1)
    shard_index = lax.axis_index("fsdp")
    first_norm_grad = lax.dynamic_slice_in_dim(
        first_norm_full, shard_index * first_width, first_width, 1
    )
    second_norm_grad = lax.dynamic_slice_in_dim(
        second_norm_full, shard_index * second_width, second_width, 1
    )
    return (
        first_out[0],
        first_out[1],
        second_out[0],
        second_out[1],
        input_grads[0],
        input_grads[1],
        first_grads[0],
        first_grads[1],
        first_grads[2],
        first_norm_grad,
        second_grads[0],
        second_grads[1],
        second_grads[2],
        second_grads[3],
        second_norm_grad,
        pooled_std,
    )


def solution(mesh):
    return jax.shard_map(
        body,
        mesh=mesh,
        in_specs=(
            P(("rep", "fsdp"), None, None, None),
            P(("rep", "fsdp"), None, None, None),
            P(("rep", "fsdp")),
            P(None, "fsdp"),
            P(None, "fsdp"),
            P(None, "fsdp"),
            P(None, "fsdp"),
            P(None, "fsdp"),
            P(None, "fsdp"),
            P(None, "fsdp"),
            P(None, "fsdp"),
            P(None, "fsdp"),
            P(("rep", "fsdp"), None, None, None),
            P(("rep", "fsdp"), None, None, None),
        ),
        out_specs=(
            P(("rep", "fsdp"), None, None, None),
            P(("rep", "fsdp"), None, None, None),
            P(("rep", "fsdp"), None, None, None),
            P(("rep", "fsdp"), None, None, None),
            P(("rep", "fsdp"), None, None, None),
            P(("rep", "fsdp"), None, None, None),
            P(None, "fsdp"),
            P(None, "fsdp"),
            P(None, "fsdp"),
            P(None, "fsdp"),
            P(None, "fsdp"),
            P(None, "fsdp"),
            P(None, "fsdp"),
            P(None, "fsdp"),
            P(None, "fsdp"),
            P(),
        ),
        check_vma=False,
    )
```

profile of v0, /device:TPU:0, one launch (start us, length us, event | category | flops | bytes accessed | tf_op | source)
XLA Modules:
  0.0 1873.9 jit_solution(3062614227000472145)
XLA Ops:
  11.8 13.7 all-gather
  26.2 14.0 all_gather.40
  42.1 16.9 all_gather.37
  59.0 14.7 all_gather.39
  78.7 43.7 %all-reduce.51 = (f32[2,256]{1,0:T(2,128)S(1)}, f32[2]{0:T(128)S(1)}, f32[2,256]{1,0:T(2,128)S(1)}) all-reduce(f32[2,256]{1,0:T(2,128)S(1)} %pad_maximum_fusion.20, f32[2]{0:T(128)S(1)} %add_convert_fusion, f32[2,256]{1,0:T(2,128)S(1)} %pad_maximum_fusion.19), channel_id=1, replica_groups=mesh['rep'=4,'fsdp'=8] {'rep','fsdp'}, use_global_device_ids=true, to_apply=%region_6.7 | all-reduce | flops 1026 | bytes 8208 | tf_op jit(solution)/shard_map/psum | solution.py:90
  142.8 8.4 multiply_reduce_fusion.10
  151.2 40.1 %all-reduce.50 = (f32[2,256]{1,0:T(2,128)S(1)}, f32[2,256]{1,0:T(2,128)S(1)}) all-reduce(f32[2,256]{1,0:T(2,128)S(1)} %pad_maximum_fusion.22, f32[2,256]{1,0:T(2,128)S(1)} %pad_maximum_fusion.21), channel_id=1, replica_groups=mesh['rep'=4,'fsdp'=8] {'rep','fsdp'}, use_global_device_ids=true, to_apply=%region_12.13 | all-reduce | flops 1024 | bytes 8192 | tf_op jit(solution)/shard_map/psum | solution.py:90
  200.6 41.5 %all-reduce.49 = (f32[2,1024]{1,0:T(2,128)}, f32[2,1024]{1,0:T(2,128)}) all-reduce(f32[2,1024]{1,0:T(2,128)} %pad_maximum_fusion.8, f32[2,1024]{1,0:T(2,128)} %pad_maximum_fusion.7), channel_id=1, replica_groups=mesh['rep'=4,'fsdp'=8] {'rep','fsdp'}, use_global_device_ids=true, to_apply=%region_18.19 | all-reduce | flops 4096 | bytes 32768 | tf_op jit(solution)/shard_map/psum | solution.py:90
  249.7 8.6 fusion.199
  267.3 39.9 %all-reduce.48 = (f32[2,512]{1,0:T(2,128)S(1)}, f32[2,512]{1,0:T(2,128)S(1)}) all-reduce(f32[2,512]{1,0:T(2,128)S(1)} %pad_maximum_fusion.12, f32[2,512]{1,0:T(2,128)S(1)} %pad_maximum_fusion.11), channel_id=1, replica_groups=mesh['rep'=4,'fsdp'=8] {'rep','fsdp'}, use_global_device_ids=true, to_apply=%region_24.25 | all-reduce | flops 2048 | bytes 16384 | tf_op jit(solution)/shard_map/psum | solution.py:90
  314.7 21.5 %slice.458 = bf16[10,7,7,512]{3,2,1,0:T(8,128)(2,1)} slice(bf16[10,16,16,512]{3,2,1,0:T(8,128)(2,1)S(1)} %pad.146), slice={[0:10:1], [2:15:2], [0:13:2], [0:512:1]} | slice | bytes 1003520 | tf_op jit(solution)/shard_map/slice | solution.py:31
  336.1 21.5 %slice.457 = bf16[10,7,7,512]{3,2,1,0:T(8,128)(2,1)} slice(bf16[10,16,16,512]{3,2,1,0:T(8,128)(2,1)S(1)} %pad.146), slice={[0:10:1], [1:14:2], [2:15:2], [0:512:1]} | slice | bytes 1003520 | tf_op jit(solution)/shard_map/slice | solution.py:31
  357.7 21.4 %slice.456 = bf16[10,7,7,512]{3,2,1,0:T(8,128)(2,1)} slice(bf16[10,16,16,512]{3,2,1,0:T(8,128)(2,1)S(1)} %pad.146), slice={[0:10:1], [1:14:2], [1:14:2], [0:512:1]} | slice | bytes 1003520 | tf_op jit(solution)/shard_map/slice | solution.py:31
  379.1 21.5 %slice.455 = bf16[10,7,7,512]{3,2,1,0:T(8,128)(2,1)} slice(bf16[10,16,16,512]{3,2,1,0:T(8,128)(2,1)S(1)} %pad.146), slice={[0:10:1], [1:14:2], [0:13:2], [0:512:1]} | slice | bytes 1003520 | tf_op jit(solution)/shard_map/slice | solution.py:31
  400.6 21.6 %slice.454 = bf16[10,7,7,512]{3,2,1,0:T(8,128)(2,1)} slice(bf16[10,16,16,512]{3,2,1,0:T(8,128)(2,1)S(1)} %pad.146), slice={[0:10:1], [0:13:2], [2:15:2], [0:512:1]} | slice | bytes 1003520 | tf_op jit(solution)/shard_map/slice | solution.py:31
  422.2 21.6 %slice.453 = bf16[10,7,7,512]{3,2,1,0:T(8,128)(2,1)} slice(bf16[10,16,16,512]{3,2,1,0:T(8,128)(2,1)S(1)} %pad.146), slice={[0:10:1], [0:13:2], [1:14:2], [0:512:1]} | slice | bytes 1003520 | tf_op jit(solution)/shard_map/slice | solution.py:31
  443.8 21.6 %slice.452 = bf16[10,7,7,512]{3,2,1,0:T(8,128)(2,1)} slice(bf16[10,16,16,512]{3,2,1,0:T(8,128)(2,1)S(1)} %pad.146), slice={[0:10:1], [0:13:2], [0:13:2], [0:512:1]} | slice | bytes 1003520 | tf_op jit(solution)/shard_map/slice | solution.py:31
  481.2 35.1 %slice.481 = bf16[10,7,7,1024]{3,2,1,0:T(8,128)(2,1)} slice(bf16[10,14,14,1024]{3,2,1,0:T(8,128)(2,1)} %get-tuple-element.127), slice={[0:10:1], [0:14:2], [0:14:2], [0:1024:1]} | slice | bytes 2007040 | tf_op jit(solution)/shard_map/slice | solution.py:240
  533.9 8.6 multiply_reduce_fusion.20
  542.5 41.4 %all-reduce.47 = (f32[2,512]{1,0:T(2,128)S(1)}, f32[2,512]{1,0:T(2,128)S(1)}) all-reduce(f32[2,512]{1,0:T(2,128)S(1)} %pad_maximum_fusion.14, f32[2,512]{1,0:T(2,128)S(1)} %pad_maximum_fusion.13), channel_id=1, replica_groups=mesh['rep'=4,'fsdp'=8] {'rep','fsdp'}, use_global_device_ids=true, to_apply=%region_30.31 | all-reduce | flops 2048 | bytes 16384 | tf_op jit(solution)/shard_map/psum | solution.py:90
  596.6 118.0 %all-reduce.56.cloned.1.call-done = (f32[2,2048]{1,0:T(2,128)}, f32[2,2048]{1,0:T(2,128)}, f32[2,2048]{1,0:T(2,128)}, f32[2,2048]{1,0:T(2,128)}) async-done(((f32[2,2048]{1,0:T(2,128)}, f32[2,2048]{1,0:T(2,128)}, f32[2,2048]{1,0:T(2,128)}, f32[2,2048]{1,0:T(2,128)}), (f32[2,2048]{1,0:T(2,128)}, f32[2,2048]{1,0:T(2,128)}, f32[2,2048]{1,0:T(2,128)}, f32[2,2048]{1,0:T(2,128)})) %all-reduce.56.cloned.1.call-update) | async-done | bytes 65552 | tf_op jit(solution)/shard_map/psum | solution.py:90
  722.9 8.5 multiply_reduce_fusion.6
  731.4 41.4 %all-reduce.45 = (f32[2,2048]{1,0:T(2,128)S(1)}, f32[2,2048]{1,0:T(2,128)S(1)}) all-reduce(f32[2,2048]{1,0:T(2,128)S(1)} %pad_maximum_fusion.5, f32[2,2048]{1,0:T(2,128)S(1)} %pad_maximum_fusion.4), channel_id=1, replica_groups=mesh['rep'=4,'fsdp'=8] {'rep','fsdp'}, use_global_device_ids=true, to_apply=%region_48.49 | all-reduce | flops 8192 | bytes 65536 | tf_op jit(solution)/shard_map/psum | solution.py:127
  787.1 40.0 %all-reduce.44 = (f32[2,512]{1,0:T(2,128)S(1)}, f32[2,512]{1,0:T(2,128)S(1)}) all-reduce(f32[2,512]{1,0:T(2,128)S(1)} %pad_maximum_fusion.16, f32[2,512]{1,0:T(2,128)S(1)} %pad_maximum_fusion.15), channel_id=1, replica_groups=mesh['rep'=4,'fsdp'=8] {'rep','fsdp'}, use_global_device_ids=true, to_apply=%region_54.55 | all-reduce | flops 2048 | bytes 16384 | tf_op jit(solution)/shard_map/psum | solution.py:127
  833.2 6.4 pad.267
  843.9 6.4 pad.546
  850.3 6.4 pad.547
  865.7 6.9 pad.159
  893.8 34.3 %pad.149 = f32[10,16,16,512]{3,2,1,0:T(8,128)} pad(f32[10,7,7,512]{3,2,1,0:T(8,128)} %get-tuple-element.140, f32[]{:T(128)} %constant.46.clone.1), padding=0_0_0x2_1_1x1_2_1x0_0_0 | pad | bytes 6246404 | tf_op jit(solution)/shard_map/transpose(jvp())/pad | solution.py:31
  928.1 33.9 %pad.544 = f32[10,14,15,512]{3,2,1,0:T(8,128)} pad(f32[10,7,7,512]{3,2,1,0:T(8,128)} %get-tuple-element.144, f32[]{:T(128)} %constant.46.clone.1), padding=0_0_0x0_1_1x0_2_1x0_0_0 | pad | bytes 5304324
  962.0 33.9 %pad.260 = f32[10,14,14,512]{3,2,1,0:T(8,128)} pad(f32[10,7,7,512]{3,2,1,0:T(8,128)} %get-tuple-element.145, f32[]{:T(128)} %constant.46.clone.1), padding=0_0_0x0_1_1x0_1_1x0_0_0 | pad | bytes 5017604 | tf_op jit(solution)/shard_map/transpose(jvp(jit(_pad)))/pad | solution.py:23
  995.8 34.0 %pad.259 = f32[10,14,14,512]{3,2,1,0:T(8,128)} pad(f32[10,7,7,512]{3,2,1,0:T(8,128)} %get-tuple-element.146, f32[]{:T(128)} %constant.46.clone.1), padding=0_0_0x0_1_1x1_0_1x0_0_0 | pad | bytes 5017604 | tf_op jit(solution)/shard_map/transpose(jvp(jit(_pad)))/pad | solution.py:23
  1029.9 34.1 %pad.541 = f32[10,15,15,512]{3,2,1,0:T(8,128)} pad(f32[10,7,7,512]{3,2,1,0:T(8,128)} %get-tuple-element.141, f32[]{:T(128)} %constant.46.clone.1), padding=0_0_0x0_2_1x0_2_1x0_0_0 | pad | bytes 5611524
  1063.9 34.1 %pad.542 = f32[10,15,14,512]{3,2,1,0:T(8,128)} pad(f32[10,7,7,512]{3,2,1,0:T(8,128)} %get-tuple-element.142, f32[]{:T(128)} %constant.46.clone.1), padding=0_0_0x0_2_1x0_1_1x0_0_0 | pad | bytes 5304324
  1098.0 33.9 %pad.543 = f32[10,15,14,512]{3,2,1,0:T(8,128)} pad(f32[10,7,7,512]{3,2,1,0:T(8,128)} %get-tuple-element.143, f32[]{:T(128)} %constant.46.clone.1), padding=0_0_0x0_2_1x1_0_1x0_0_0 | pad | bytes 5304324
  1132.0 34.3 %pad.150 = f32[10,16,16,512]{3,2,1,0:T(8,128)} pad(f32[10,7,7,512]{3,2,1,0:T(8,128)} %get-tuple-element.147, f32[]{:T(128)} %constant.46.clone.1), padding=0_0_0x2_1_1x0_3_1x0_0_0 | pad | bytes 6246404 | tf_op jit(solution)/shard_map/transpose(jvp())/pad | solution.py:31
  1166.3 34.2 %pad.148 = f32[10,16,16,512]{3,2,1,0:T(8,128)} pad(f32[10,7,7,512]{3,2,1,0:T(8,128)} %get-tuple-element.148, f32[]{:T(128)} %constant.46.clone.1), padding=0_0_0x2_1_1x2_1_1x0_0_0 | pad | bytes 6246404 | tf_op jit(solution)/shard_map/transpose(jvp())/pad | solution.py:31
  1200.5 6.8 add_add_fusion.2
  1207.3 8.4 add_add_fusion
  1215.7 7.3 fusion.188
  1223.0 14.0 fusion.184
  1237.1 41.0 %all-reduce.43 = (f32[2,512]{1,0:T(2,128)S(1)}, f32[2,512]{1,0:T(2,128)S(1)}, f32[2,2048]{1,0:T(2,128)S(1)}) all-reduce(f32[2,512]{1,0:T(2,128)S(1)} %pad_maximum_fusion.18, f32[2,512]{1,0:T(2,128)S(1)} %pad_maximum_fusion.17, f32[2,2048]{1,0:T(2,128)S(1)} %pad_maximum_fusion.6), channel_id=1, replica_groups=mesh['rep'=4,'fsdp'=8] {'rep','fsdp'}, use_global_device_ids=true, to_apply=%region_60.61 | all-reduce | flops 6144 | bytes 49152 | tf_op jit(solution)/shard_map/psum | solution.py:127
  1301.5 6.5 fusion.185
  1311.7 7.0 fusion.47
  1318.6 12.1 scatter_fusion
  1330.8 15.2 fusion.183
  1346.0 40.1 %all-reduce.42 = (f32[2,1024]{1,0:T(2,128)S(1)}, f32[2,1024]{1,0:T(2,128)S(1)}) all-reduce(f32[2,1024]{1,0:T(2,128)S(1)} %pad_maximum_fusion.10, f32[2,1024]{1,0:T(2,128)S(1)} %pad_maximum_fusion.9), channel_id=1, replica_groups=mesh['rep'=4,'fsdp'=8] {'rep','fsdp'}, use_global_device_ids=true, to_apply=%region_71.72 | all-reduce | flops 4096 | bytes 32768 | tf_op jit(solution)/shard_map/psum | solution.py:127
  1386.2 13.3 multiply_convert_fusion
  1413.3 40.9 %all-reduce.41 = (f32[2,256]{1,0:T(2,128)S(1)}, f32[2,256]{1,0:T(2,128)S(1)}) all-reduce(f32[2,256]{1,0:T(2,128)S(1)} %pad_maximum_fusion.24, f32[2,256]{1,0:T(2,128)S(1)} %pad_maximum_fusion.23), channel_id=1, replica_groups=mesh['rep'=4,'fsdp'=8] {'rep','fsdp'}, use_global_device_ids=true, to_apply=%region_77.78 | all-reduce | flops 1024 | bytes 8192 | tf_op jit(solution)/shard_map/psum | solution.py:127
  1462.0 8.4 fusion.99
  1470.4 12.1 fusion.203
  1495.1 40.4 %all-reduce.40 = (f32[2,256]{1,0:T(2,128)S(1)}, f32[2,256]{1,0:T(2,128)S(1)}, f32[2048]{0:T(1024)}, f32[2048]{0:T(1024)}) all-reduce(f32[2,256]{1,0:T(2,128)S(1)} %pad_maximum_fusion.26, f32[2,256]{1,0:T(2,128)S(1)} %pad_maximum_fusion.25, f32[2048]{0:T(1024)S(1)} %add.693, ...), channel_id=1, replica_groups=mesh['rep'=4,'fsdp'=8] {'rep','fsdp'}, use_global_device_ids=true, to_apply=%region_83.84 | all-reduce | flops 5120 | bytes 40960 | tf_op jit(solution)/shard_map/psum | solution.py:127
  1546.2 6.1 fusion.55
  1552.4 6.1 fusion.40
  1565.8 6.9 fusion.31
  1572.7 6.0 fusion.143
  1578.7 9.9 fusion.5
  1602.4 6.5 reduce-scatter.14.cloned.1.call-done
  1608.9 34.0 %reduce-scatter.12.cloned.1.call-done = bf16[2304,32]{0,1:T(8,128)(2,1)} async-done(((bf16[2304,256]{0,1:T(8,128)(2,1)}), bf16[2304,32]{0,1:T(8,128)(2,1)}) %reduce-scatter.12.cloned.1.call-update) | async-done | bytes 147472 | tf_op jit(solution)/shard_map/reduce_scatter | solution.py:74
  1642.9 36.7 %reduce-scatter.18.cloned.1.call-done = bf16[512,256]{1,0:T(8,128)(2,1)} async-done(((bf16[512,2048]{1,0:T(8,128)(2,1)}), bf16[512,256]{1,0:T(8,128)(2,1)}) %reduce-scatter.18.cloned.1.call-update) | async-done | bytes 262160 | tf_op jit(solution)/shard_map/reduce_scatter | solution.py:74
  1679.6 50.9 %reduce-scatter.20.cloned.1.call-done = bf16[1024,256]{1,0:T(8,128)(2,1)} async-done(((bf16[1024,2048]{1,0:T(8,128)(2,1)}), bf16[1024,256]{1,0:T(8,128)(2,1)}) %reduce-scatter.20.cloned.1.call-update) | async-done | bytes 524304 | tf_op jit(solution)/shard_map/reduce_scatter | solution.py:74
  1730.6 56.0 %reduce-scatter.16.cloned.1.call-done = bf16[4608,64]{0,1:T(8,128)(2,1)} async-done(((bf16[4608,512]{0,1:T(8,128)(2,1)}), bf16[4608,64]{0,1:T(8,128)(2,1)}) %reduce-scatter.16.cloned.1.call-update) | async-done | bytes 589840 | tf_op jit(solution)/shard_map/reduce_scatter | solution.py:74
  1810.7 9.0 convolution_add_fusion
  1819.7 35.7 %all-reduce.58.cloned.1.call-done = (bf16[1024,32]{0,1:T(8,128)(2,1)}, bf16[2304,32]{0,1:T(8,128)(2,1)}, bf16[256,128]{1,0:T(8,128)(2,1)}, bf16[1024,64]{0,1:T(8...) async-done(((bf16[1024,32]{0,1:T(8,128)(2,1)}, bf16[2304,32]{0,1:T(8,128)(2,1)}, bf16[256,128]{1,0:T(8,128)(2,1)}, ...) | async-done | bytes 1785872 | tf_op jit(solution)/shard_map/psum | solution.py:76
  (663 shorter events, 295.2 us)
Async XLA Ops:
  7.2 51.8 %copy-start.106 = (bf16[256,128]{1,0:T(8,128)(2,1)S(1)}, bf16[256,128]{1,0:T(8,128)(2,1)}, u32[]{:S(2)}) copy-start(bf16[256,128]{1,0:T(8,128)(2,1)} %param.19) | copy-start | bytes 196612
  7.2 66.6 %copy-start.23 = (bf16[20,6,6,1024]{3,0,2,1:T(8,128)(2,1)S(1)}, bf16[20,6,6,1024]{3,0,2,1:T(8,128)(2,1)}, u32[]{:S(2)}) copy-start(bf16[20,6,6,1024]{3,0,2,1:T(8,128)(2,1)} %param.15) | copy-start | bytes 4423684
  7.2 130.8 %all-gather.7.cloned.1.call-start = ((), (), s32[]{:S(2)}) async-start(), calls=%async_computation.7 | async-start | bytes 1327104 | tf_op jit(solution)/shard_map/all_gather | solution.py:66
  7.9 250.3 %all-gather.9.cloned.1.call-start = ((), (), s32[]{:S(2)}) async-start(), calls=%async_computation.8 | async-start | bytes 1179648 | tf_op jit(solution)/shard_map/all_gather | solution.py:66
  8.7 510.6 %all-gather.15.cloned.1.call-start = ((), (), s32[]{:S(2)}) async-start(), calls=%async_computation.11 | async-start | bytes 4718592 | tf_op jit(solution)/shard_map/all_gather | solution.py:66
  9.4 519.6 %all-gather.11.cloned.1.call-start = ((), (), s32[]{:S(2)}) async-start(), calls=%async_computation.9 | async-start | bytes 5308416 | tf_op jit(solution)/shard_map/all_gather | solution.py:66
  10.0 574.1 %all-gather.13.cloned.1.call-start = ((), (), s32[]{:S(2)}) async-start(), calls=%async_computation.10 | async-start | bytes 2359296 | tf_op jit(solution)/shard_map/all_gather | solution.py:66
  10.6 704.0 %all-reduce.56.cloned.1.call-start = ((), (), s32[]{:S(2)}) async-start(), calls=%async_computation.19 | async-start | bytes 131072 | tf_op jit(solution)/shard_map/psum | solution.py:90
  26.2 105.2 %copy-start.111 = (f32[1,256]{1,0:T(1,128)}, f32[1,256]{1,0:T(1,128)S(1)}, u32[]{:S(2)}) copy-start(f32[1,256]{1,0:T(1,128)S(1)} %get-tuple-element.222) | copy-start | bytes 3076
  26.2 105.2 %copy-start.117 = (f32[1,256]{1,0:T(1,128)}, f32[1,256]{1,0:T(1,128)S(1)}, u32[]{:S(2)}) copy-start(f32[1,256]{1,0:T(1,128)S(1)} %get-tuple-element.221) | copy-start | bytes 3076
  26.2 165.1 %copy-start.180 = (f32[1,256]{1,0:T(1,128)}, f32[1,256]{1,0:T(1,128)S(1)}, u32[]{:S(2)}) copy-start(f32[1,256]{1,0:T(1,128)S(1)} %get-tuple-element.219) | copy-start | bytes 3076
  26.2 223.5 %copy-start.94 = (f32[1,1024]{1,0:T(1,128)}, f32[1,1024]{1,0:T(1,128)S(1)}, u32[]{:S(2)}) copy-start(f32[1,1024]{1,0:T(1,128)S(1)} %get-tuple-element.218) | copy-start | bytes 12292
  42.1 100.7 %copy-start.123 = (f32[10]{0:T(128)}, f32[10]{0:T(128)S(1)}, u32[]{:S(2)}) copy-start(f32[10]{0:T(128)S(1)} %compare_convert_fusion.1) | copy-start | bytes 124
  42.1 95.9 %copy-start.119 = (f32[20]{0:T(128)}, f32[20]{0:T(128)S(1)}, u32[]{:S(2)}) copy-start(f32[20]{0:T(128)S(1)} %compare_convert_fusion) | copy-start | bytes 244
  59.0 14.8 copy-start.31
  74.4 52.4 %copy-start.12 = (f32[20,6,6,256]{3,0,2,1:T(8,128)}, f32[20,6,6,256]{3,0,2,1:T(8,128)S(1)}, u32[]{:S(2)}) copy-start(f32[20,6,6,256]{3,0,2,1:T(8,128)S(1)} %get-tuple-element.287) | copy-start | bytes 2211844
  78.7 52.7 %copy-start.1 = (f32[10,14,14,256]{3,2,1,0:T(8,128)}, f32[10,14,14,256]{3,2,1,0:T(8,128)S(1)}, u32[]{:S(2)}) copy-start(f32[10,14,14,256]{3,2,1,0:T(8,128)S(1)} %get-tuple-element.288) | copy-start | bytes 6021124
  194.4 49.8 %copy-start.5 = (f32[20,6,6,1024]{3,0,2,1:T(8,128)}, f32[20,6,6,1024]{3,0,2,1:T(8,128)S(1)}, u32[]{:S(2)}) copy-start(f32[20,6,6,1024]{3,0,2,1:T(8,128)S(1)} %get-tuple-element.291) | copy-start | bytes 8847364
  262.1 45.2 %copy-start.103 = (f32[1,512]{1,0:T(1,128)S(1)}, f32[1,512]{1,0:T(1,128)}, u32[]{:S(2)}) copy-start(f32[1,512]{1,0:T(1,128)} %get-tuple-element.178) | copy-start | bytes 6148
  262.1 45.8 %copy-start.116 = (f32[1,512]{1,0:T(1,128)S(1)}, f32[1,512]{1,0:T(1,128)}, u32[]{:S(2)}) copy-start(f32[1,512]{1,0:T(1,128)} %get-tuple-element.177) | copy-start | bytes 6148
  307.9 157.5 %copy-start.138 = (f32[512]{0:T(512)}, f32[512]{0:T(512)S(1)}, u32[]{:S(2)}) copy-start(f32[512]{0:T(512)S(1)} %get-tuple-element.230) | copy-start | bytes 6148
  533.9 50.3 %copy-start.90 = (f32[20,3,3,512]{3,0,2,1:T(8,128)}, f32[20,3,3,512]{3,0,2,1:T(8,128)S(1)}, u32[]{:S(2)}) copy-start(f32[20,3,3,512]{3,0,2,1:T(8,128)S(1)} %get-tuple-element.295) | copy-start | bytes 1105924
  533.9 50.2 %copy-start.171 = (f32[1,512]{1,0:T(1,128)S(1)}, f32[1,512]{1,0:T(1,128)}, u32[]{:S(2)}) copy-start(f32[1,512]{1,0:T(1,128)} %get-tuple-element.175) | copy-start | bytes 6148
  533.9 50.2 %copy-start.189 = (f32[1,512]{1,0:T(1,128)S(1)}, f32[1,512]{1,0:T(1,128)}, u32[]{:S(2)}) copy-start(f32[1,512]{1,0:T(1,128)} %get-tuple-element.176) | copy-start | bytes 6148
  584.0 243.1 %copy-start.146 = (f32[1,512]{1,0:T(1,128)}, f32[1,512]{1,0:T(1,128)S(1)}, u32[]{:S(2)}) copy-start(f32[1,512]{1,0:T(1,128)S(1)} %get-tuple-element.242) | copy-start | bytes 6148
  584.0 298.0 %copy-start.148 = (f32[1,512]{1,0:T(1,128)}, f32[1,512]{1,0:T(1,128)S(1)}, u32[]{:S(2)}) copy-start(f32[1,512]{1,0:T(1,128)S(1)} %get-tuple-element.241) | copy-start | bytes 6148
  584.1 243.1 %copy-start.164 = (f32[512]{0:T(512)}, f32[512]{0:T(512)S(1)}, u32[]{:S(2)}) copy-start(f32[512]{0:T(512)S(1)} %get-tuple-element.236) | copy-start | bytes 6148
  584.1 298.0 %copy-start.173 = (f32[512]{0:T(512)}, f32[512]{0:T(512)S(1)}, u32[]{:S(2)}) copy-start(f32[512]{0:T(512)S(1)} %get-tuple-element.267) | copy-start | bytes 6148
  588.3 129.5 %copy-start.92 = (f32[1,2048]{1,0:T(1,128)S(1)}, f32[1,2048]{1,0:T(1,128)}, u32[]{:S(2)}) copy-start(f32[1,2048]{1,0:T(1,128)} %get-tuple-element.173) | copy-start | bytes 24580
  588.3 129.5 %copy-start.85 = (bf16[20,3,3,2048]{3,0,2,1:T(8,128)(2,1)S(1)}, bf16[20,3,3,2048]{3,0,2,1:T(8,128)(2,1)}, u32[]{:S(2)}) copy-start(bf16[20,3,3,2048]{3,0,2,1:T(8,128)(2,1)} %param.27) | copy-start | bytes 2211844
  588.4 129.5 %copy-start.101 = (f32[1,2048]{1,0:T(1,128)S(1)}, f32[1,2048]{1,0:T(1,128)}, u32[]{:S(2)}) copy-start(f32[1,2048]{1,0:T(1,128)} %get-tuple-element.172) | copy-start | bytes 24580
  588.4 129.5 %copy-start.102 = (f32[1,2048]{1,0:T(1,128)S(1)}, f32[1,2048]{1,0:T(1,128)}, u32[]{:S(2)}) copy-start(f32[1,2048]{1,0:T(1,128)} %get-tuple-element.174) | copy-start | bytes 24580
  596.2 1004.4 %reduce-scatter.22.cloned.1.call-start = ((), (), s32[]{:S(2)}) async-start(), calls=%async_computation.18 | async-start | bytes 589824
  722.8 50.6 %copy-start.121 = (f32[20]{0:T(128)S(1)}, f32[20]{0:T(128)}, u32[]{:S(2)}) copy-start(f32[20]{0:T(128)} %copy-done.119) | copy-start | bytes 244
  843.9 12.9 copy-start.73
  1166.3 41.0 %slice-start.4 = ((s8[5242880]{0:T(1024)(128)(4,1)}), s8[1048576]{0:T(1024)(128)(4,1)S(1)}, s32[]{:S(2)}) async-start(s8[5242880]{0:T(1024)(128)(4,1)} %bitcast.399), calls=%async_computation.25 | async-start | bytes 2097152
  1200.5 22.5 %slice-start = ((s8[4587520]{0:T(1024)(128)(4,1)}), s8[4194304]{0:T(1024)(128)(4,1)S(1)}, s32[]{:S(2)}) async-start(s8[4587520]{0:T(1024)(128)(4,1)} %bitcast.395), calls=%async_computation.21 | async-start | bytes 8388608
  1207.3 15.7 slice-start.1
  1330.7 15.2 copy-start.152
  1330.7 15.2 copy-start.151
  1330.7 55.4 %copy-start.105 = (f32[1024]{0:T(1024)S(1)}, f32[1024]{0:T(1024)}, u32[]{:S(2)}) copy-start(f32[1024]{0:T(1024)} %copy-done.104) | copy-start | bytes 12292
  1330.7 55.4 %copy-start.127 = (f32[10]{0:T(128)S(1)}, f32[10]{0:T(128)}, u32[]{:S(2)}) copy-start(f32[10]{0:T(128)} %copy-done.123) | copy-start | bytes 124
  1330.8 55.4 %copy-start.150 = (f32[1024]{0:T(1024)S(1)}, f32[1024]{0:T(1024)}, u32[]{:S(2)}) copy-start(f32[1024]{0:T(1024)} %get-tuple-element.224) | copy-start | bytes 12292
  1386.1 13.4 copy-start.134
  1386.1 13.4 copy-start.135
  1386.1 13.3 copy-start.53
  1386.1 13.3 copy-start.162
  1386.1 13.3 copy-start.182
  1386.2 13.3 copy-start.185
  1386.2 13.3 copy-start.194
  1411.2 42.9 %copy-start.177 = (f32[256]{0:T(256)S(1)}, f32[256]{0:T(256)}, u32[]{:S(2)}) copy-start(f32[256]{0:T(256)} %get-tuple-element.259) | copy-start | bytes 3076
  1412.1 42.4 %copy-start.30 = (bf16[2304,256]{0,1:T(8,128)(2,1)S(1)}, bf16[2304,256]{0,1:T(8,128)(2,1)}, u32[]{:S(2)}) copy-start(bf16[2304,256]{0,1:T(8,128)(2,1)} %all-gather.7.cloned.1.call-done) | copy-start | bytes 3538948
  1413.2 189.3 %reduce-scatter.10.cloned.1.call-start = ((), (), s32[]{:S(2)}) async-start(), calls=%async_computation.12 | async-start | bytes 589824 | tf_op jit(solution)/shard_map/reduce_scatter | solution.py:74
  1470.4 12.1 copy-start.137
  1470.4 12.1 copy-start.136
  1491.2 44.4 %copy-start.183 = (f32[256]{0:T(256)S(1)}, f32[256]{0:T(256)}, u32[]{:S(2)}) copy-start(f32[256]{0:T(256)} %get-tuple-element.278) | copy-start | bytes 3076
  1544.1 64.8 %reduce-scatter.14.cloned.1.call-start = ((), (), s32[]{:S(2)}) async-start(), calls=%async_computation.14 | async-start | bytes 1179648 | tf_op jit(solution)/shard_map/reduce_scatter | solution.py:74
  1552.3 90.6 %reduce-scatter.12.cloned.1.call-start = ((), (), s32[]{:S(2)}) async-start(), calls=%async_computation.13 | async-start | bytes 1327104 | tf_op jit(solution)/shard_map/reduce_scatter | solution.py:74
  1565.5 114.2 %reduce-scatter.18.cloned.1.call-start = ((), (), s32[]{:S(2)}) async-start(), calls=%async_computation.16 | async-start | bytes 2359296 | tf_op jit(solution)/shard_map/reduce_scatter | solution.py:74
  1578.7 151.9 %reduce-scatter.20.cloned.1.call-start = ((), (), s32[]{:S(2)}) async-start(), calls=%async_computation.17 | async-start | bytes 4718592 | tf_op jit(solution)/shard_map/reduce_scatter | solution.py:74
  1588.7 197.9 %reduce-scatter.16.cloned.1.call-start = ((), (), s32[]{:S(2)}) async-start(), calls=%async_computation.15 | async-start | bytes 5308416 | tf_op jit(solution)/shard_map/reduce_scatter | solution.py:74
  1600.2 189.0 %copy-start.108 = (f32[2,2048]{1,0:T(2,128)S(1)}, f32[2,2048]{1,0:T(2,128)}, u32[]{:S(2)}) copy-start(f32[2,2048]{1,0:T(2,128)} %copy-done.107) | copy-start | bytes 49156
  1600.3 206.7 %copy-start.4 = (f32[20,6,6,1024]{3,0,2,1:T(8,128)S(1)}, f32[20,6,6,1024]{3,0,2,1:T(8,128)}, u32[]{:S(2)}) copy-start(f32[20,6,6,1024]{3,0,2,1:T(8,128)} %get-tuple-element.122) | copy-start | bytes 8847364
  1600.3 255.1 %all-reduce.58.cloned.1.call-start = ((), (), s32[]{:S(2)}) async-start(), calls=%async_computation.20 | async-start | bytes 3571712 | tf_op jit(solution)/shard_map/psum | solution.py:76
  (155 other events, 654.6 us)
Sparse Core Ops, SparseCore 0:
  9.7 25.3 all-gather.6
  36.7 24.7 all-gather.8
  63.1 48.1 all-gather.14
  112.7 49.8 all-gather.10
  164.1 29.9 all-gather.12
  596.4 118.1 all-reduce.55
  1413.3 31.4 reduce-scatter.21
  1544.2 31.3 reduce-scatter.9
  1578.4 30.4 reduce-scatter.13
  1611.6 31.2 reduce-scatter.11
  1645.8 33.8 reduce-scatter.17
  1681.8 48.7 reduce-scatter.19
  1733.4 53.1 reduce-scatter.15
  1791.0 64.3 all-reduce.57
where the time goes:
time: 1910 us; the launch traced here: 1870 us
  local copies, waits for them, and re-layouts  610 us (32%)
  blocking collectives  510 us (27%)
  waiting for transfers between devices  341 us (18%)
  other arithmetic  203 us (11%)
  matrix products  185 us (10%)
  between operations  23.6 us (1%)
    psum x6, blocking collectives, norm_back(): summed = lax.psum(tuple(members), ('rep', 'fsdp'))  244 us
    psum x5, blocking collectives, batch_norm(): summed = lax.psum(tuple(members), ('rep', 'fsdp'))  207 us
    unnamed x451, local copies, waits for them, and re-layouts  194 us
    reduce_scatter x6, waiting for transfers between devices, combine_grads(): lax.psum_scatter(for_sending(gradients), 'fsdp', scatter_dimension=1, til...  184 us
    slice x9, local copies, waits for them, and re-layouts, patches(): lax.slice(padded, (0, shift_row, shift_col, 0), (batch_views, shift_row +...  154 us
    dot_general x28, matrix products, project(): return jnp.dot(operand, weight, preferred_element_type=jnp.float32)  124 us
    pad x6, local copies, waits for them, and re-layouts, patches(): lax.slice(padded, (0, shift_row, shift_col, 0), (batch_views, shift_row +...  119 us
    psum x1, waiting for transfers between devices, batch_norm(): summed = lax.psum(tuple(members), ('rep', 'fsdp'))  118 us
  transfers between devices with their start and end apart: 14, of which 7 were waited for; matrix products, arithmetic and copies ran while one was open for 23% of the time, Pallas kernels for 0%

commit v1 on v0

v1 whole, which is shorter than its diff:
```python
import functools

import jax
import jax.numpy as jnp
from jax import lax
from jax.experimental import pallas as pl
from jax.experimental.pallas import tpu as pltpu
from jax.sharding import PartitionSpec as P

EPSILON = 1e-05
F32 = jnp.float32
BF16 = jnp.bfloat16
MESH = pl.DeviceIdType.MESH
CELLS = 16


def nt(left, right):
    return lax.dot_general(left, right, (((1,), (1,)), ((), ())), preferred_element_type=F32)


def nn(left, right):
    return lax.dot_general(left, right, (((1,), (0,)), ((), ())), preferred_element_type=F32)


def tn(left, right):
    return lax.dot_general(left, right, (((0,), (0,)), ((), ())), preferred_element_type=F32)


def sig(values):
    return 0.5 * jnp.tanh(0.5 * values) + 0.5


def silu(values):
    return values * sig(values)


def slope(values):
    gate = sig(values)
    held = values * gate
    return gate + held - held * gate


def lanes(tile, width):
    return jnp.concatenate([tile] * (width // tile.shape[1]), axis=1)


def fold(values):
    return jnp.sum(values.reshape(values.shape[0] // 8, 8, values.shape[1]), axis=0)


class Geometry:
    def __init__(self, views, side_global, side_local):
        self.slabs = views
        self.hg, self.hl = side_global, side_local
        assert side_global < CELLS and side_local < CELLS // 2
        self.rg, self.rl = side_global * CELLS, side_local * CELLS
        self.rows = self.rg + self.rl
        self.og, self.ol = (side_global - 1) // 2 + 1, (side_local - 1) // 2 + 1
        self.sg, self.sl = self.og * 8, self.ol * 8
        self.small = self.sg + self.sl
        self.total, self.small_total = self.slabs * self.rows, self.slabs * self.small
        self.halo = self.rows + 2 * CELLS
        self.halo_total = self.slabs * self.halo + CELLS
        self.chunk = 32
        assert self.rg % self.chunk == 0 and self.rl % self.chunk == 0 and self.small % 16 == 0

    def pieces(self, width):
        if width <= 256:
            return [(0, self.rg, 0), (self.rg, self.rl, 1)]
        step = self.chunk
        return [(start, step, 0) for start in range(0, self.rg, step)] + [
            (start, step, 1) for start in range(self.rg, self.rows, step)
        ]

    def mask(self, count, group, width):
        row = lax.broadcasted_iota(jnp.int32, (count, 128), 0)
        if group == 0:
            keep = (row & (CELLS - 1)) < self.hg
        else:
            keep = (row & (CELLS // 2 - 1)) < self.hl
        return lanes(keep.astype(F32), width)

    def small_mask(self, group, width):
        count = self.sl if group else self.sg
        row = lax.broadcasted_iota(jnp.int32, (count, 128), 0)
        keep = (row & 3) < self.ol if group else (row & 7) < self.og
        return lanes(keep.astype(F32), width)

    def small_pieces(self):
        return [(0, self.sg, 0), (self.sg, self.sl, 1)]


def alive(live, slab):
    return jnp.where(slab < 2 * live[0], 1.0, 0.0).astype(F32)


def cells(geo, count, group, width, small=False):
    images = lanes(count[8:9, 0:128], width)
    if small:
        return images * float(2 * geo.og * geo.og if group == 0 else 4 * geo.ol * geo.ol)
    return images * float(2 * geo.hg * geo.hg if group == 0 else 4 * geo.hl * geo.hl)


def member(sums, row, width):
    parts = width // sums.shape[1]
    return jnp.concatenate(
        [sums[row * parts + k : row * parts + k + 1, :] for k in range(parts)], axis=1
    )


def norm_terms(stats, norm, number, group):
    width = norm.shape[1]
    mean = member(stats, 2 * group, width) / number
    spread = member(stats, 2 * group + 1, width) / number - mean * mean
    inverse = lax.rsqrt(spread + EPSILON)
    scale = norm[0:1, :] * inverse
    return mean, inverse, scale, norm[1:2, :] - mean * scale


def back_terms(stats, norm, number, group, first, second_raw):
    mean, inverse, scale, unused = norm_terms(stats, norm, number, group)
    second = inverse * (second_raw - mean * first)
    by_value = -scale * inverse * (second / number)
    constant = -scale * (first / number) - by_value * mean
    return scale, by_value, constant, second


def forward_terms(geo, count, stats, norm, width, small=False):
    return [
        norm_terms(stats, norm, cells(geo, count, group, width, small), group)[2:]
        for group in range(2)
    ]


def backward_terms(geo, count, stats, norm, sums, out, width, small=False, rows=((0, 1), (2, 3))):
    terms = []
    seconds = []
    for group in range(2):
        number = cells(geo, count, group, width, small)
        first = member(sums, rows[group][0], width)
        raw = member(sums, rows[group][1], width)
        scale, by_value, constant, second = back_terms(stats, norm, number, group, first, raw)
        terms.append((scale, by_value, constant))
        seconds.append((second, first))
    out[...] = jnp.zeros(out.shape, F32)
    out[0:1, :] = seconds[0][0] + seconds[1][0]
    out[1:2, :] = seconds[0][1] + seconds[1][1]
    return terms


def finish(stats, acc, members, begin=0):
    part = stats.shape[1]
    parts = acc.shape[2] // part
    for row in range(members):
        total = jnp.sum(acc[begin + row], axis=0, keepdims=True)
        for k in range(parts):
            stats[row * parts + k : row * parts + k + 1, :] = total[:, k * part : (k + 1) * part]


def put(store, place, values):
    for k in range(store.shape[0]):
        store[k, place, :] = values[:, k * 128 : (k + 1) * 128]


def take(store, place):
    return jnp.concatenate([store[k, place, :] for k in range(store.shape[0])], axis=1)


def put_pieces(pieces, first, values, begin=0):
    cores, chips, reps, size = pieces.shape[:4]
    cols = slice(begin, begin + values.shape[1])
    for k in range(values.shape[0] // size):
        index = first // size + k
        shard, rep = index // reps, index % reps
        part = values[k * size : (k + 1) * size]
        pieces[shard % cores, shard // cores, rep, :, cols] = part.astype(BF16)


def loop(count, step):
    def one(index, carry):
        step(index)
        return carry

    lax.fori_loop(0, count, one, 0)


def at(index, size):
    return pl.ds(pl.multiple_of(index * size, size), size)


def stage_a(geo, net, live, xg, xl, packed, conv, acc, weight, own_g, own_l, arrive):
    loads = (
        pltpu.make_async_copy(xg, own_g, arrive.at[0]),
        pltpu.make_async_copy(xl, own_l, arrive.at[1]),
    )
    for load in loads:
        load.start()
    net.open()
    acc[...] = jnp.zeros(acc.shape, F32)
    blank = jnp.zeros((CELLS, packed.shape[1]), BF16)
    half = CELLS // 2
    for load in loads:
        load.wait()

    def pack(s):
        base = s * geo.rows
        keep = alive(live, s).astype(BF16)
        for i in range(geo.hg):
            start = pl.multiple_of(base + i * CELLS, CELLS)
            packed[pl.ds(start, CELLS), :] = blank
            packed[pl.ds(start, geo.hg), :] = own_g[s, i] * keep
        for i in range(geo.hl):
            start = pl.multiple_of(base + geo.rg + i * CELLS, CELLS)
            packed[pl.ds(start, CELLS), :] = blank
            for side in range(2):
                place = pl.multiple_of(start + side * half, half)
                packed[pl.ds(place, geo.hl), :] = own_l[2 * s + side, i] * keep

    third = geo.slabs // 3
    loop(third, pack)
    net.turn(1)
    loop(third, lambda s: pack(s + third))
    net.turn(2)
    loop(geo.slabs - 2 * third, lambda s: pack(s + 2 * third))
    net.turn(3)
    gathered = net.job_out(2)
    weight[...] = gathered[...].astype(F32).reshape(weight.shape).astype(BF16)

    def slab(s):
        result = nt(packed[at(s, geo.rows), :], weight[...])
        conv[at(s, geo.rows), :] = result.astype(BF16)
        for start, size, group in geo.pieces(256):
            piece = result[start : start + size]
            acc[2 * group] += fold(piece)
            acc[2 * group + 1] += fold(piece * piece)

    loop(geo.slabs, slab)
    finish(net.own, acc, 4)
    net.own[8:16, :] = jnp.full((8, net.own.shape[1]), live[0], jnp.int32).astype(F32)
    net.begin()
    net.turn(4)
    net.middle()
    net.turn(5)
    net.end()


def spread_taps(geo, store, s, values, reverse):
    width = values[0].shape[1]
    for group in range(2):
        rows = values[group]
        size = rows.shape[0]
        start = pl.multiple_of(s * geo.halo + CELLS + group * (geo.rg + CELLS), CELLS)
        before = pltpu.roll(rows, 1, 0)
        after = pltpu.roll(rows, size - 1, 0)
        order = (after, rows, before) if reverse else (before, rows, after)
        for tap in range(3):
            store[pl.ds(start, size), tap * width : (tap + 1) * width] = order[tap].astype(BF16)


def clear_halo(geo, store):
    blank = jnp.zeros((CELLS, store.shape[1]), BF16)

    def slab(s):
        store[pl.ds(pl.multiple_of(s * geo.halo, CELLS), CELLS), :] = blank
        store[pl.ds(pl.multiple_of(s * geo.halo + CELLS + geo.rg, CELLS), CELLS), :] = blank

    loop(geo.slabs, slab)
    store[geo.slabs * geo.halo : geo.slabs * geo.halo + CELLS, :] = blank


def activate(geo, live, conv, s, terms):
    values = []
    width = conv.shape[1]
    keep = alive(live, s)
    for group in range(2):
        start, size = (geo.rg, geo.rl) if group else (0, geo.rg)
        rows = conv[pl.ds(pl.multiple_of(s * geo.rows + start, CELLS), size), :].astype(F32)
        scale, shift = terms[group]
        values.append(silu(rows * scale + shift) * (geo.mask(size, group, width) * keep))
    return values


def stage_b(geo, net, live, count, za, stats_a, norm, weight, conv, taps, acc):
    net.open()
    acc[...] = jnp.zeros(acc.shape, F32)
    width = za.shape[1]
    terms = forward_terms(geo, count, stats_a, norm, width)
    clear_halo(geo, taps)
    loop(
        geo.slabs,
        lambda s: spread_taps(geo, taps, s, activate(geo, live, za, s, terms), False),
    )
    net.turn(1)
    span = geo.halo - CELLS

    def slab(s):
        result = None
        for dy in range(3):
            rows = taps[pl.ds(pl.multiple_of(s * geo.halo + dy * CELLS, CELLS), span), :]
            term = nt(rows, weight[:, dy * 3 * width : (dy + 1) * 3 * width])
            result = term if result is None else result + term
        keep = alive(live, s)
        for group, (begin, size) in enumerate(((0, geo.rg), (geo.rg + CELLS, geo.rl))):
            piece = result[begin : begin + size]
            start = pl.multiple_of(s * geo.rows + group * geo.rg, CELLS)
            conv[pl.ds(start, size), :] = piece.astype(BF16)
            piece = piece * (geo.mask(size, group, width) * keep)
            acc[2 * group] += fold(piece)
            acc[2 * group + 1] += fold(piece * piece)

    loop(geo.slabs, slab)
    finish(net.own, acc, 4)
    net.run()


def stage_c(geo, net, live, count, zb, stats_b, norm, weight, conv, act, acc):
    net.open()
    acc[...] = jnp.zeros(acc.shape, F32)
    terms = forward_terms(geo, count, stats_b, norm, zb.shape[1])
    step = 256

    def slab(s):
        values = activate(geo, live, zb, s, terms)
        act[0 : geo.rg, :] = values[0].astype(BF16)
        act[geo.rg : geo.rows, :] = values[1].astype(BF16)
        for c in range(0, weight.shape[0], step):
            result = nt(act[...], weight[c : c + step, :])
            conv[at(s, geo.rows), c : c + step] = result.astype(BF16)
            for start, size, group in geo.pieces(256):
                piece = result[start : start + size]
                acc[2 * group, :, c : c + step] += fold(piece)
                acc[2 * group + 1, :, c : c + step] += fold(piece * piece)

    loop(geo.slabs, slab)
    finish(net.own, acc, 4)
    net.run()


def even_rows(geo):
    return [2 * i * CELLS for i in range(geo.og)] + [
        geo.rg + 2 * i * CELLS for i in range(geo.ol)
    ]


def stage_d(
    geo, net, live, count, zc, stats_c, norm, packed, weight, short, hid, outg, outl, conv, conv_s,
    sub, stats_s, full, acc, acc_s,
):
    net.open()
    acc[...] = jnp.zeros(acc.shape, F32)
    acc_s[...] = jnp.zeros(acc_s.shape, F32)
    width = zc.shape[1]
    terms = forward_terms(geo, count, stats_c, norm, width)

    def slab(s):
        keep = alive(live, s)
        for start, size, group in geo.pieces(width):
            rows = pl.ds(pl.multiple_of(s * geo.rows + start, CELLS), size)
            scale, shift = terms[group]
            joined = zc[rows, :].astype(F32) * scale + shift + packed[rows, :].astype(F32)
            value = silu(joined) * (geo.mask(size, group, width) * keep)
            put(full, pl.ds(start, size), value)
            low = value.astype(BF16)
            hid[rows, :] = low
            for k in range(size // CELLS):
                i = (start - group * geo.rg) // CELLS + k
                if group == 0:
                    outg[s, i] = low[k * CELLS : k * CELLS + geo.hg]
                else:
                    for side in range(2):
                        begin = k * CELLS + side * CELLS // 2
                        outl[2 * s + side, i] = low[begin : begin + geo.hl]
        picked = [take(full, pl.ds(start, 8, stride=2)) for start in even_rows(geo)]
        sub[at(s, geo.small), :] = jnp.concatenate(picked, axis=0).astype(BF16)
        result = nt(hid[at(s, geo.rows), :], weight[...])
        conv[at(s, geo.rows), :] = result.astype(BF16)
        for start, size, group in geo.pieces(256):
            piece = result[start : start + size]
            acc[2 * group] += fold(piece)
            acc[2 * group + 1] += fold(piece * piece)

    loop(geo.slabs, slab)
    finish(net.own, acc, 4)
    net.begin()
    half = short.shape[0] // 2
    small_product(geo, sub, short, conv_s, acc_s, 0, half)
    net.middle()
    small_product(geo, sub, short, conv_s, acc_s, half, 2 * half)
    finish(stats_s, acc_s, 4)
    net.end()


def small_product(geo, left, weight, conv, acc, first, last):
    step = 256
    for c in range(first, last, step):
        result = nt(left[...], weight[c : c + step, :])
        conv[:, c : c + step] = result.astype(BF16)
        for s in range(geo.slabs):
            for start, size, group in geo.small_pieces():
                piece = result[s * geo.small + start : s * geo.small + start + size]
                acc[2 * group, :, c : c + step] += fold(piece)
                acc[2 * group + 1, :, c : c + step] += fold(piece * piece)


def gather_taps(geo, live, zd, terms, full, taps):
    width = zd.shape[1]
    blank = jnp.zeros((8, width), F32)
    full[:, 0:CELLS, :] = jnp.zeros((width // 128, CELLS, 128), F32)
    full[:, CELLS + geo.rg : 2 * CELLS + geo.rg, :] = jnp.zeros((width // 128, CELLS, 128), F32)

    def slab(s):
        keep = alive(live, s)
        for start, size, group in geo.pieces(width):
            rows = pl.ds(pl.multiple_of(s * geo.rows + start, CELLS), size)
            scale, shift = terms[group]
            value = silu(zd[rows, :].astype(F32) * scale + shift)
            begin = CELLS + start + group * CELLS
            put(full, pl.ds(begin, size), value * (geo.mask(size, group, width) * keep))
        for dy in range(3):
            for dx in range(3):
                picked = []
                for group in range(2):
                    for i in range(geo.ol if group else geo.og):
                        line = 2 * i + dy - 1
                        if line < 0:
                            picked.append(blank)
                            continue
                        begin = CELLS + group * (geo.rg + CELLS) + line * CELLS + dx - 1
                        picked.append(take(full, pl.ds(begin, 8, stride=2)))
                tap = dy * 3 + dx
                taps[at(s, geo.small), tap * width : (tap + 1) * width] = jnp.concatenate(
                    picked, axis=0
                ).astype(BF16)

    loop(geo.slabs, slab)


def stage_e(geo, net, live, count, zd, stats_d, norm, weight, conv, full, taps, acc):
    net.open()
    net.side.begin()
    acc[...] = jnp.zeros(acc.shape, F32)
    terms = forward_terms(geo, count, stats_d, norm, zd.shape[1])
    gather_taps(geo, live, zd, terms, full, taps)
    net.side.middle()
    step = 256
    for c in range(0, weight.shape[0], step):
        result = nt(taps[...], weight[c : c + step, :])
        conv[:, c : c + step] = result.astype(BF16)
        for s in range(geo.slabs):
            keep = alive(live, s)
            for start, size, group in geo.small_pieces():
                piece = result[s * geo.small + start : s * geo.small + start + size]
                piece = piece * (geo.small_mask(group, step) * keep)
                acc[2 * group, :, c : c + step] += fold(piece)
                acc[2 * group + 1, :, c : c + step] += fold(piece * piece)
    net.side.end()
    finish(net.own, acc, 4)
    net.run()


def stage_f(geo, net, live, count, ze, stats_e, norm, weight, act, conv, acc):
    acc[...] = jnp.zeros(acc.shape, F32)
    width = ze.shape[1]
    terms = forward_terms(geo, count, stats_e, norm, width, True)

    def slab(s):
        keep = alive(live, s)
        rows = ze[at(s, geo.small), :].astype(F32)
        parts = []
        for start, size, group in geo.small_pieces():
            scale, shift = terms[group]
            value = silu(rows[start : start + size] * scale + shift)
            parts.append(value * (geo.small_mask(group, width) * keep))
        act[at(s, geo.small), :] = jnp.concatenate(parts, axis=0).astype(BF16)

    loop(geo.slabs, slab)
    small_product(geo, act, weight, conv, acc, 0, weight.shape[0])
    finish(net.own, acc, 4)
    net.run()


def stage_out(
    geo, net, live, count, zf, zs, stats_f, stats_s, norm_f, norm_s, cotg, cotl, outg, outl, grad,
    pooled_sums, pool, cot, acc,
):
    acc[...] = jnp.zeros(acc.shape, F32)
    cot[...] = jnp.zeros(cot.shape, F32)
    pool[...] = jnp.zeros(pool.shape, F32)
    width = zf.shape[1]
    step = 512
    terms_f = forward_terms(geo, count, stats_f, norm_f, width, True)
    terms_s = forward_terms(geo, count, stats_s, norm_s, width, True)

    def slab(s):
        keep = alive(live, s)
        for c in range(0, width, step):
            cols = slice(c, c + step)
            for i in range(geo.og):
                cot[i * 8 : i * 8 + geo.og, :] = cotg[s, i, :, cols].astype(F32)
            for i in range(geo.ol):
                for side in range(2):
                    begin = geo.sg + i * 8 + side * 4
                    cot[begin : begin + geo.ol, :] = cotl[2 * s + side, i, :, cols].astype(F32)
            rows_f = zf[at(s, geo.small), cols].astype(F32)
            rows_s = zs[at(s, geo.small), cols].astype(F32)
            grads = []
            for start, size, group in geo.small_pieces():
                part = slice(start, start + size)
                vf, vs = rows_f[part], rows_s[part]
                scale_f, shift_f = (item[:, cols] for item in terms_f[group])
                scale_s, shift_s = (item[:, cols] for item in terms_s[group])
                joined = vf * scale_f + vs * scale_s + (shift_f + shift_s)
                mask = geo.small_mask(group, step) * keep
                gate = sig(joined)
                held = joined * gate
                value = held * mask
                low = value.astype(BF16)
                dy = cot[part, :] * ((gate + held - held * gate) * mask)
                grads.append(dy)
                acc[3 * group, :, cols] += fold(dy)
                acc[3 * group + 1, :, cols] += fold(dy * vf)
                acc[3 * group + 2, :, cols] += fold(dy * vs)
                summed = fold(value)
                if group == 0:
                    for i in range(geo.og):
                        outg[s, i, :, cols] = value[i * 8 : i * 8 + geo.og].astype(BF16)
                    pool[s, 0:1, cols] = jnp.sum(summed, axis=0, keepdims=True) * (
                        1.0 / (geo.og * geo.og)
                    )
                else:
                    row = lax.broadcasted_iota(jnp.int32, (8, step), 0)
                    for side in range(2):
                        own = jnp.where((row >= 4) == (side == 1), summed, 0.0)
                        pool[s, 1 + side : 2 + side, cols] = jnp.sum(
                            own, axis=0, keepdims=True
                        ) * (1.0 / (geo.ol * geo.ol))
                        for i in range(geo.ol):
                            begin = i * 8 + side * 4
                            outl[2 * s + side, i, :, cols] = value[begin : begin + geo.ol].astype(
                                BF16
                            )
            grad[at(s, geo.small), cols] = jnp.concatenate(grads, axis=0).astype(BF16)
        pooled = pool[s]
        square = jnp.mean(pooled * pooled, axis=1, keepdims=True)
        normed = pooled * lax.rsqrt(square + 1e-06)
        acc[6] += normed
        acc[7] += normed * normed

    loop(geo.slabs, slab)
    finish(net.own, acc, 6)
    net.begin()
    finish(pooled_sums, acc, 2, 6)
    net.middle()
    net.end()


def small_back(geo, live, s, grad, conv, terms, width, cols):
    keep = alive(live, s)
    rows_g = grad[at(s, geo.small), cols].astype(F32)
    rows_z = conv[at(s, geo.small), cols].astype(F32)
    parts = []
    for start, size, group in geo.small_pieces():
        scale, by_value, constant = (item[:, cols] for item in terms[group])
        part = slice(start, start + size)
        value = rows_g[part] * scale + rows_z[part] * by_value + constant
        parts.append(value * (geo.small_mask(group, width) * keep))
    return jnp.concatenate(parts, axis=0).astype(BF16)


def stage_f_back(
    geo, net, live, count, zf, zs, stats_f, stats_s, norm_f, norm_s, grad, sums, act, sub, weight,
    short, ze, stats_e, norm_e, wgrad_f, wgrad_s, back_sub, back_e, ngrad_f, ngrad_s, dzf, dzs, acc,
):
    acc[...] = jnp.zeros(acc.shape, F32)
    width = zf.shape[1]
    step = 512
    rows_f, rows_s = ((0, 1), (3, 4)), ((0, 2), (3, 5))
    terms_f = backward_terms(geo, count, stats_f, norm_f, sums, ngrad_f, width, True, rows_f)
    terms_s = backward_terms(geo, count, stats_s, norm_s, sums, ngrad_s, width, True, rows_s)

    def slab(s):
        for c in range(0, width, step):
            cols = slice(c, c + step)
            dzf[at(s, geo.small), cols] = small_back(geo, live, s, grad, zf, terms_f, step, cols)
            dzs[at(s, geo.small), cols] = small_back(geo, live, s, grad, zs, terms_s, step, cols)

    loop(geo.slabs, slab)
    net.open()
    net.side.begin()
    block = 256
    terms_e = forward_terms(geo, count, stats_e, norm_e, ze.shape[1], True)
    for c in range(0, act.shape[1], block):
        cols = slice(c, c + block)
        result = nn(dzf[...], weight[:, cols])
        for s in range(geo.slabs):
            keep = alive(live, s)
            rows = ze[s * geo.small : (s + 1) * geo.small, cols].astype(F32)
            parts = []
            for start, size, group in geo.small_pieces():
                scale, shift = (item[:, cols] for item in terms_e[group])
                value = rows[start : start + size]
                mask = geo.small_mask(group, block) * keep
                piece = result[s * geo.small + start : s * geo.small + start + size]
                piece = piece * (slope(value * scale + shift) * mask)
                parts.append(piece)
                acc[2 * group, :, cols] += fold(piece)
                acc[2 * group + 1, :, cols] += fold(piece * value)
            back_e[s * geo.small : (s + 1) * geo.small, cols] = jnp.concatenate(
                parts, axis=0
            ).astype(BF16)
    finish(net.own, acc, 4)
    net.begin()
    for c in range(0, width, block):
        cols = slice(c, c + block)
        put_pieces(wgrad_f, c, tn(dzf[:, cols], act[...]))
    net.side.middle()
    net.middle()
    for c in range(0, width, block):
        cols = slice(c, c + block)
        put_pieces(wgrad_s, c, tn(dzs[:, cols], sub[...]))
    for c in range(0, sub.shape[1], block):
        cols = slice(c, c + block)
        back_sub[:, cols] = nn(dzs[...], short[:, cols]).astype(BF16)
    net.side.end()
    net.end()


def stage_e_back(
    geo, net, live, count, ze, stats_e, norm_e, back_e, sums_e, zd, stats_d, norm_d, weight, wgrad,
    back_d, ngrad, full, taps, dze, moved, parity, acc,
):
    acc[...] = jnp.zeros(acc.shape, F32)
    width = ze.shape[1]
    terms_e = backward_terms(geo, count, stats_e, norm_e, sums_e, ngrad, width, True)
    terms_d = forward_terms(geo, count, stats_d, norm_d, width)
    gather_taps(geo, live, zd, terms_d, full, taps)
    net.open()

    def shift(s):
        value = small_back(geo, live, s, back_e, ze, terms_e, width, slice(0, width)).astype(F32)
        blank = jnp.zeros((8, width), F32)
        down = jnp.concatenate(
            [value[8 : geo.sg], blank, value[geo.sg + 8 :], blank], axis=0
        )
        size = geo.small
        dze[at(s, size), :] = value.astype(BF16)
        moved[0, at(s, size), :] = pltpu.roll(value, size - 1, 0).astype(BF16)
        moved[1, at(s, size), :] = down.astype(BF16)
        moved[2, at(s, size), :] = pltpu.roll(down, size - 1, 0).astype(BF16)

    loop(geo.slabs, shift)

    def tap(dy, dx):
        return weight[:, (dy * 3 + dx) * width : (dy * 3 + dx + 1) * width]

    def grads(first, last):
        for t in range(first, last):
            result = tn(dze[...], taps[:, t * width : (t + 1) * width])
            put_pieces(wgrad, 0, result, t * width)

    parity[0] = nn(dze[...], tap(1, 1))
    parity[1] = nn(dze[...], tap(1, 2)) + nn(moved[0], tap(1, 0))
    parity[2] = nn(dze[...], tap(2, 1)) + nn(moved[1], tap(0, 1))
    parity[3] = (
        nn(dze[...], tap(2, 2))
        + nn(moved[0], tap(2, 0))
        + nn(moved[1], tap(0, 2))
        + nn(moved[2], tap(0, 0))
    )

    def slab(s):
        keep = alive(live, s)
        for group in range(2):
            for i in range(geo.ol if group else geo.og):
                for a in range(2):
                    for b in range(2):
                        begin = group * geo.rg + (2 * i + a) * CELLS + b
                        source = s * geo.small + group * geo.sg + i * 8
                        part = parity[2 * a + b, pl.ds(pl.multiple_of(source, 8), 8), :]
                        put(full, pl.ds(begin, 8, stride=2), part)
        for start, size, group in geo.pieces(width):
            rows = pl.ds(pl.multiple_of(s * geo.rows + start, CELLS), size)
            scale, shift_d = terms_d[group]
            value = zd[rows, :].astype(F32)
            mask = geo.mask(size, group, width) * keep
            piece = take(full, pl.ds(start, size)) * (slope(value * scale + shift_d) * mask)
            back_d[rows, :] = piece.astype(BF16)
            acc[2 * group] += fold(piece)
            acc[2 * group + 1] += fold(piece * value)

    loop(geo.slabs, slab)
    finish(net.own, acc, 4)
    net.begin()
    grads(0, 4)
    net.middle()
    grads(4, 9)
    net.end()


def wide_back(geo, live, s, grad, conv, terms, low):
    width = conv.shape[1]
    keep = alive(live, s)
    for start, size, group in geo.pieces(width):
        rows = pl.ds(pl.multiple_of(s * geo.rows + start, CELLS), size)
        scale, by_value, constant = terms[group]
        value = grad[rows, :].astype(F32) * scale + conv[rows, :].astype(F32) * by_value + constant
        low[rows, :] = (value * (geo.mask(size, group, width) * keep)).astype(BF16)


def stage_d_back(
    geo, net, live, count, zd, stats_d, norm_d, back_d, sums_d, hid, packed, zc, stats_c, norm_c,
    back_sub, weight, wgrad, joined, ngrad, dzd, full, acc,
):
    acc[...] = jnp.zeros(acc.shape, F32)
    width = zc.shape[1]
    terms_d = backward_terms(geo, count, stats_d, norm_d, sums_d, ngrad, zd.shape[1])
    terms_c = forward_terms(geo, count, stats_c, norm_c, width)

    net.open()

    def slab(s):
        wide_back(geo, live, s, back_d, zd, terms_d, dzd)
        put(full, pl.ds(0, geo.rows), nn(dzd[at(s, geo.rows), :], weight[...]))
        extra = back_sub[at(s, geo.small), :].astype(F32)
        for k, start in enumerate(even_rows(geo)):
            place = pl.ds(start, 8, stride=2)
            put(full, place, take(full, place) + extra[k * 8 : k * 8 + 8])
        keep = alive(live, s)
        for start, size, group in geo.pieces(width):
            rows = pl.ds(pl.multiple_of(s * geo.rows + start, CELLS), size)
            scale, shift = terms_c[group]
            value = zc[rows, :].astype(F32)
            pre = value * scale + shift + packed[rows, :].astype(F32)
            mask = geo.mask(size, group, width) * keep
            piece = take(full, pl.ds(start, size)) * (slope(pre) * mask)
            joined[rows, :] = piece.astype(BF16)
            acc[2 * group] += fold(piece)
            acc[2 * group + 1] += fold(piece * value)

    loop(geo.slabs, slab)
    finish(net.own, acc, 4)
    block = 256
    net.begin()
    for c in range(0, dzd.shape[1], block):
        put_pieces(wgrad, c, tn(dzd[:, c : c + block], hid[...]))
        if c == 0:
            net.middle()
    net.end()


def stage_c_back(
    geo, net, live, count, zc, stats_c, norm_c, joined, sums_c, zb, stats_b, norm_b, weight, wgrad,
    back_b, ngrad, dzc, act, acc,
):
    acc[...] = jnp.zeros(acc.shape, F32)
    terms_c = backward_terms(geo, count, stats_c, norm_c, sums_c, ngrad, zc.shape[1])
    terms_b = forward_terms(geo, count, stats_b, norm_b, zb.shape[1])
    width = zb.shape[1]

    net.open()

    def slab(s):
        wide_back(geo, live, s, joined, zc, terms_c, dzc)
        result = nn(dzc[at(s, geo.rows), :], weight[...])
        keep = alive(live, s)
        for start, size, group in geo.pieces(width):
            rows = pl.ds(pl.multiple_of(s * geo.rows + start, CELLS), size)
            scale, shift = terms_b[group]
            value = zb[rows, :].astype(F32)
            pre = value * scale + shift
            mask = geo.mask(size, group, width) * keep
            gate = sig(pre)
            held = pre * gate
            act[rows, :] = (held * mask).astype(BF16)
            piece = result[start : start + size] * ((gate + held - held * gate) * mask)
            back_b[rows, :] = piece.astype(BF16)
            acc[2 * group] += fold(piece)
            acc[2 * group + 1] += fold(piece * value)

    loop(geo.slabs, slab)
    finish(net.own, acc, 4)
    net.begin()
    half = dzc.shape[1] // 2
    put_pieces(wgrad, 0, tn(dzc[:, 0:half], act[...]))
    net.middle()
    put_pieces(wgrad, half, tn(dzc[:, half:], act[...]))
    net.end()


def stage_b_back(
    geo, net, live, count, zb, stats_b, norm_b, back_b, sums_b, za, stats_a, norm_a, weight, wgrad,
    back_a, ngrad, taps, dtaps, stacked, total, acc,
):
    acc[...] = jnp.zeros(acc.shape, F32)
    width = za.shape[1]
    terms_b = backward_terms(geo, count, stats_b, norm_b, sums_b, ngrad, width)
    terms_a = forward_terms(geo, count, stats_a, norm_a, width)
    clear_halo(geo, taps)
    clear_halo(geo, dtaps)
    for t in range(9):
        stacked[t * width : (t + 1) * width, :] = weight[:, t * width : (t + 1) * width]

    def fill(s):
        spread_taps(geo, taps, s, activate(geo, live, za, s, terms_a), False)
        keep = alive(live, s)
        values = []
        for start, size, group in geo.pieces(width):
            rows = pl.ds(pl.multiple_of(s * geo.rows + start, CELLS), size)
            scale, by_value, constant = terms_b[group]
            value = back_b[rows, :].astype(F32) * scale + zb[rows, :].astype(F32) * by_value
            values.append((value + constant) * (geo.mask(size, group, width) * keep))
        spread_taps(geo, dtaps, s, values, True)

    loop(geo.slabs, fill)
    net.open()
    span = geo.halo - CELLS
    total[...] = jnp.zeros(total.shape, F32)

    def slab(s):
        result = None
        for dy in range(3):
            begin = pl.multiple_of(s * geo.halo + (2 - dy) * CELLS, CELLS)
            term = nn(
                dtaps[pl.ds(begin, span), :], stacked[dy * 3 * width : (dy + 1) * 3 * width, :]
            )
            result = term if result is None else result + term
        keep = alive(live, s)
        for group, (begin, size) in enumerate(((0, geo.rg), (geo.rg + CELLS, geo.rl))):
            rows = pl.ds(pl.multiple_of(s * geo.rows + group * geo.rg, CELLS), size)
            scale, shift = terms_a[group]
            value = za[rows, :].astype(F32)
            mask = geo.mask(size, group, width) * keep
            piece = result[begin : begin + size] * (slope(value * scale + shift) * mask)
            back_a[rows, :] = piece.astype(BF16)
            acc[2 * group] += fold(piece)
            acc[2 * group + 1] += fold(piece * value)

    def grads(s):
        own = dtaps[
            pl.ds(pl.multiple_of(s * geo.halo + CELLS, CELLS), span), width : 2 * width
        ]
        for dy in range(3):
            begin = pl.multiple_of(s * geo.halo + dy * CELLS, CELLS)
            total[:, dy * 3 * width : (dy + 1) * 3 * width] += tn(own, taps[pl.ds(begin, span), :])

    loop(geo.slabs, slab)
    finish(net.own, acc, 4)
    half = geo.slabs // 2
    net.begin()
    loop(half, grads)
    net.middle()
    loop(geo.slabs - half, lambda s: grads(s + half))
    put_pieces(wgrad, 0, total[...])
    net.end()


def stage_a_back(
    geo, net, live, count, za, stats_a, norm_a, back_a, sums_a, packed, joined, weight, wgrad, dxg, dxl,
    ngrad, dza,
):
    terms_a = backward_terms(geo, count, stats_a, norm_a, sums_a, ngrad, za.shape[1])

    net.open()

    def slab(s):
        wide_back(geo, live, s, back_a, za, terms_a, dza)
        result = nn(dza[at(s, geo.rows), :], weight[...])
        half = CELLS // 2
        for i in range(geo.hg):
            rows = pl.ds(pl.multiple_of(s * geo.rows + i * CELLS, CELLS), CELLS)
            value = result[i * CELLS : (i + 1) * CELLS] + joined[rows, :].astype(F32)
            dxg[s, i] = value[0 : geo.hg]
        for i in range(geo.hl):
            begin = geo.rg + i * CELLS
            rows = pl.ds(pl.multiple_of(s * geo.rows + begin, CELLS), CELLS)
            value = result[begin : begin + CELLS] + joined[rows, :].astype(F32)
            for side in range(2):
                dxl[2 * s + side, i] = value[side * half : side * half + geo.hl]

    loop(geo.slabs, slab)
    put_pieces(wgrad, 0, tn(dza[...], packed[...]))
    net.close()


class Sums:
    def __init__(self, reps, shards, own, out, first, second, sems):
        self.reps, self.shards = reps, shards
        self.own, self.out, self.first, self.second = own, out, first, second
        self.sems = sems
        self.rep, self.shard = lax.axis_index("rep"), lax.axis_index("fsdp")
        self.copies = []

    def begin(self):
        self.copies = []
        for hop in range(1, self.shards):
            copy = pltpu.make_async_remote_copy(
                self.own, self.first.at[self.shard], self.sems[0].at[hop], self.sems[1].at[hop],
                device_id={"fsdp": lax.rem(self.shard + hop, self.shards)}, device_id_type=MESH,
            )
            copy.start()
            self.copies.append(copy)
        self.first[self.shard] = self.own[...]

    def middle(self):
        for copy in self.copies:
            copy.wait()
        total = self.first[0]
        for k in range(1, self.shards):
            total = total + self.first[k]
        self.second[self.rep] = total
        self.copies = []
        for hop in range(1, self.reps):
            place = self.second.at[self.rep]
            copy = pltpu.make_async_remote_copy(
                place, place, self.sems[2].at[hop], self.sems[3].at[hop],
                device_id={"rep": lax.rem(self.rep + hop, self.reps)}, device_id_type=MESH,
            )
            copy.start()
            self.copies.append(copy)

    def end(self):
        for copy in self.copies:
            copy.wait()
        total = self.second[0]
        for k in range(1, self.reps):
            total = total + self.second[k]
        self.out[...] = total


class Net:
    def __init__(self, reps, shards, sums=None, side=None, jobs=(), plans=()):
        self.reps, self.shards = reps, shards
        self.sums, self.side, self.jobs, self.plans = sums, side, jobs, plans
        self.own = None if sums is None else sums.own
        self.opened = False
        self.started, self.finished = set(), set()

    def enter(self):
        rep, shard = lax.axis_index("rep"), lax.axis_index("fsdp")
        barrier = pltpu.get_barrier_semaphore()
        for hop in range(1, self.shards):
            other = {"fsdp": lax.rem(shard + hop, self.shards)}
            pl.semaphore_signal(barrier, inc=1, device_id=other, device_id_type=MESH)
        for hop in range(1, self.reps):
            other = {"rep": lax.rem(rep + hop, self.reps)}
            pl.semaphore_signal(barrier, inc=1, device_id=other, device_id_type=MESH)

    def open(self):
        if not self.opened:
            self.opened = True
            pl.semaphore_wait(pltpu.get_barrier_semaphore(), self.shards + self.reps - 2)
            self.turn(0)

    def turn(self, number):
        for k, (start, end) in enumerate(self.plans):
            if end == number:
                self.finish(k)
        for k, (start, end) in enumerate(self.plans):
            if start == number:
                self.started.add(k)
                self.jobs[k].start()

    def finish(self, k):
        assert k in self.started and k not in self.finished
        self.finished.add(k)
        self.jobs[k].finish()

    def job_out(self, k):
        return self.jobs[k].out

    def begin(self):
        self.open()
        self.sums.begin()

    def middle(self):
        self.sums.middle()

    def end(self):
        self.sums.end()
        self.close()

    def run(self):
        self.begin()
        self.middle()
        self.end()

    def close(self):
        for k in range(len(self.jobs)):
            if k not in self.finished:
                self.finish(k)


class Job:
    def __init__(self, kind, reps, shards, sources, out, held, send, recv):
        self.kind, self.source, self.out, self.held = kind, sources[0], out, held
        self.sources = sources
        self.send, self.recv = send, recv
        self.reps, self.chips = reps, shards // 2
        self.rep, shard = lax.axis_index("rep"), lax.axis_index("fsdp")
        self.chip, self.core = shard // 2, lax.rem(shard, 2)
        if kind in ("pair", "join"):
            self.members, self.me = 2, self.core
            self.address = lambda k: {"fsdp": self.chip * 2 + k}
        elif kind in ("line", "spread"):
            self.members, self.me = self.chips, self.chip
            self.address = lambda k: {"fsdp": k * 2 + self.core}
        elif kind == "all":
            self.members, self.me = shards, shard
            self.address = lambda k: {"fsdp": k}
        else:
            self.members, self.me = reps, self.rep
            self.address = lambda k: {"rep": k}

    def give(self, source, target, hop):
        other = lax.rem(self.me + hop, self.members)
        k = len(self.copies)
        if hop == 0:
            copy = pltpu.make_async_copy(source, target, self.send.at[k])
        else:
            copy = pltpu.make_async_remote_copy(
                source, target, self.send.at[k], self.recv.at[k],
                device_id=self.address(other), device_id_type=MESH,
            )
        copy.start()
        self.copies.append(copy)

    def start(self):
        self.copies = []
        kind, out = self.kind, self.out
        order = list(range(1, self.members)) + [0]
        if kind == "spread":
            for hop in order:
                self.give(self.source.at[self.rep], out.at[self.chip], hop)
        elif kind == "fan":
            for hop in order:
                for step in range(1, self.chips):
                    chip = lax.rem(self.chip + step, self.chips)
                    self.give(self.source.at[chip], out.at[chip, self.rep], hop)
            self.give(self.sources[1], out.at[self.chip], 0)
        elif kind == "join":
            for hop in order:
                for chip in range(self.chips):
                    self.give(self.source.at[chip], out.at[chip, self.core], hop)
        elif kind == "all":
            for hop in order:
                self.give(self.source, out.at[self.me], hop)
        else:
            for hop in order:
                other = lax.rem(self.me + hop, self.members)
                block = self.source if kind == "share" else self.source.at[other]
                self.give(block, self.held.at[self.me], hop)

    def finish(self):
        for copy in self.copies:
            copy.wait()
        held, out = self.held, self.out
        if held is None:
            return
        if self.kind == "share":
            for k in range(self.members):
                out[k] = held[k].astype(F32)
            return
        blocks = held.shape[1:-2]

        def one(index):
            place = (index // blocks[-1], lax.rem(index, blocks[-1])) if len(blocks) == 2 else (
                (index,) if blocks else ()
            )
            total = held[(0,) + place].astype(F32)
            for k in range(1, self.members):
                total = total + held[(k,) + place].astype(F32)
            out[place[::-1]] = total.astype(BF16)

        if blocks:
            loop(blocks[0] * (blocks[1] if len(blocks) == 2 else 1), one)
        else:
            total = held[0].astype(F32)
            for k in range(1, self.members):
                total = total + held[k].astype(F32)
            out[...] = total.astype(BF16)


def job_shapes(kind, reps, shards, shape):
    chips = shards // 2
    if kind == "spread":
        return None, (chips,) + shape[1:], chips
    if kind == "fan":
        return None, (chips, reps) + shape[1:], reps * (chips - 1) + 1
    if kind == "join":
        return None, (chips, 2) + shape[1:], 2 * chips
    if kind == "all":
        return None, (shards,) + shape, shards
    if kind == "pair":
        return shape, (shape[2], shape[1]) + shape[3:], 2
    if kind == "share":
        return (reps,) + shape, (reps,) + shape, reps
    return shape, shape[1:], shape[0]


VMEM_CAP = 60 << 20
FAR = ("spread", "fan")


def sums_scratch(reps, shards, shape, own):
    return [pltpu.VMEM(shape, F32)] * own + [
        pltpu.VMEM((shards,) + shape, F32),
        pltpu.VMEM((reps,) + shape, F32),
        pltpu.SemaphoreType.DMA((shards,)),
        pltpu.SemaphoreType.DMA((shards,)),
        pltpu.SemaphoreType.DMA((reps,)),
        pltpu.SemaphoreType.DMA((reps,)),
    ]


def run(name, kernel, geo, reps, shards, number, live, operands, results, scratch, sums, jobs, side, far=()):
    own_results = len(results)
    results = list(results)
    spaces = [pltpu.VMEM] * own_results
    extra = []
    arrays = []
    shapes = []
    for kind, sources, start, end in jobs:
        source = sources[0]
        if isinstance(source, int):
            shape, dtype = shapes[source]
        else:
            shape, dtype = source.shape, source.dtype
        arrays += [item for item in sources if not isinstance(item, int)]
        held, out, copies = job_shapes(kind, reps, shards, shape)
        shapes.append((out, F32 if kind == "share" else dtype))
        results.append(shapes[-1])
        spaces.append(pl.ANY if kind in FAR else pltpu.VMEM)
        extra += [] if held is None else [pltpu.VMEM(held, BF16)]
        extra += [pltpu.SemaphoreType.DMA((copies,))] * 2
    operands = tuple(operands)
    near = len(operands)
    if side is not None:
        operands += (side,)
        results.append((side.shape, F32))
        spaces.append(pltpu.VMEM)
        extra += sums_scratch(reps, shards, side.shape, 0)
    if sums is not None:
        results.append((sums, F32))
        spaces.append(pltpu.VMEM)
        extra += sums_scratch(reps, shards, sums, 1)
    inputs = 1 + len(operands)
    remote = bool(jobs) or sums is not None

    def whole(*refs):
        sources_in = list(refs[inputs : inputs + len(arrays)])
        first_out = inputs + len(arrays)
        outs = refs[first_out : first_out + len(results)]
        more = list(refs[first_out + len(results) :])
        made = []
        for k, (kind, sources, start, end) in enumerate(jobs):
            refs_of = [
                made[item].out if isinstance(item, int) else sources_in.pop(0) for item in sources
            ]
            held = more.pop(0) if job_shapes(kind, reps, shards, refs_of[0].shape)[0] else None
            made.append(
                Job(kind, reps, shards, refs_of, outs[own_results + k], held, more.pop(0), more.pop(0))
            )
        beside, main = None, None
        place = own_results + len(jobs)
        if side is not None:
            beside = Sums(reps, shards, refs[near + 1], outs[place], more[0], more[1], more[2:6])
            more = more[6:]
        if sums is not None:
            main = Sums(reps, shards, more[0], outs[-1], more[1], more[2], more[3:7])
            more = more[7:]
        net = None
        if remote:
            plans = [(start, end) for unused, unused_too, start, end in jobs]
            net = Net(reps, shards, main, beside, made, plans)
            net.enter()
        kernel(geo, net, *refs[: near + 1], *outs[:own_results], *more)

    params = {"collective_id": number, "has_side_effects": True} if remote else {}
    return pl.pallas_call(
        whole,
        out_shape=[jax.ShapeDtypeStruct(shape, dtype) for shape, dtype in results],
        in_specs=[pl.BlockSpec(memory_space=pltpu.SMEM)]
        + [pl.BlockSpec(memory_space=pl.ANY if k in far else pltpu.VMEM) for k in range(len(operands))]
        + [pl.BlockSpec(memory_space=pl.ANY)] * len(arrays),
        out_specs=[pl.BlockSpec(memory_space=space) for space in spaces],
        scratch_shapes=extra
        + [item if not isinstance(item, tuple) else pltpu.VMEM(*item) for item in scratch],
        compiler_params=pltpu.CompilerParams(vmem_limit_bytes=VMEM_CAP, **params),
        name=name,
    )(live, *operands, *arrays)


def tail_kernel(reps, shards, plan, *refs):
    count = len(plan)
    current = list(refs[:count])
    outs, more = refs[count : 2 * count], list(refs[2 * count :])
    net = Net(reps, shards)
    net.enter()
    net.open()
    for turn in range(max(len(kinds) for kinds in plan)):
        active = []
        for k, kinds in enumerate(plan):
            if turn >= len(kinds):
                continue
            held, send, recv = more[:3]
            more = more[3:]
            target = outs[k]
            if turn < len(kinds) - 1:
                target = more.pop(0)
            job = Job(kinds[turn], reps, shards, (current[k],), target, held, send, recv)
            job.start()
            active.append((k, job))
        for k, job in active:
            job.finish()
            current[k] = job.out


def run_tail(reps, shards, number, entries):
    shapes = [source.shape for unused, source in entries]
    plan = [kinds for kinds, unused in entries]
    scratch = []
    for turn in range(max(len(kinds) for kinds in plan)):
        for k, kinds in enumerate(plan):
            if turn >= len(kinds):
                continue
            held, out, copies = job_shapes(kinds[turn], reps, shards, shapes[k])
            scratch += [pltpu.VMEM(held, BF16)] + [pltpu.SemaphoreType.DMA((copies,))] * 2
            if turn < len(kinds) - 1:
                scratch.append(pltpu.VMEM(out, BF16))
            shapes[k] = out
    return pl.pallas_call(
        functools.partial(tail_kernel, reps, shards, plan),
        out_shape=[jax.ShapeDtypeStruct(shape, F32) for shape in shapes],
        in_specs=[pl.BlockSpec(memory_space=pl.ANY)] * len(entries),
        out_specs=[pl.BlockSpec(memory_space=pltpu.VMEM)] * len(entries),
        scratch_shapes=scratch,
        compiler_params=pltpu.CompilerParams(
            vmem_limit_bytes=VMEM_CAP, collective_id=number, has_side_effects=True
        ),
        name="tail",
    )(*[source for unused, source in entries])


def columns_of(rows):
    return rows.reshape(-1, rows.shape[-1]).T


def own_norms(first, second):
    flat = jnp.concatenate([first.reshape(-1), second.reshape(-1)]).astype(F32)
    size = -(-flat.shape[0] // 1024) * 1024
    return jnp.pad(flat, (0, size - flat.shape[0])).reshape(8, -1)


def all_norms(gathered, first, second):
    shards = gathered.shape[0]
    flat = gathered.reshape(shards, -1)
    split, last = first.size, first.size + second.size

    def whole(part):
        return part.reshape(shards, 2, -1).transpose(1, 0, 2).reshape(2, -1)

    return whole(flat[:, :split]), whole(flat[:, split:last])


def body(reps, shards, *arguments):
    (
        global_views, local_views, live, first_reduce, first_spatial, first_expand, first_norms,
        second_reduce, second_spatial, second_expand, second_short, second_norms, global_cotan,
        local_cotan,
    ) = arguments
    geo = Geometry(global_views.shape[0], global_views.shape[1], local_views.shape[1])
    assert local_views.shape[0] == 2 * geo.slabs
    channels = global_views.shape[3]
    ha, hb, hc, hd, he, hf, hs = (
        item.T.reshape(reps, -1, item.shape[0])
        for item in (
            first_reduce, first_spatial, first_expand, second_reduce, second_spatial,
            second_expand, second_short,
        )
    )
    mid_1, mid_2 = first_reduce.shape[1] * shards, second_reduce.shape[1] * shards
    wide = second_expand.shape[1] * shards

    def rows_of(gathered):
        return gathered.reshape(-1, gathered.shape[-1])

    big, small = geo.total, geo.small_total

    numbers = iter(range(100))

    def go(name, kernel, operands, results, scratch, width=None, members=4, jobs=(), side=None, far=()):
        parts = {4: 2, 6: 4, 8: 2}[members]
        sums = None if width is None else (members * parts, width // parts)
        return run(
            name, kernel, geo, reps, shards, next(numbers), live, operands, results, scratch, sums,
            jobs, side, far,
        )

    def pieces(weight):
        size = weight.shape[0] // (shards * reps)
        return ((2, shards // 2, reps, size, weight.shape[1]), BF16)

    def acc(width, members=4):
        return ((members, 8, width), F32)

    def stat(width):
        return ((8, width), F32)

    (
        packed, za, spread_a, fan_a, wa, spread_b, fan_b, wb, norms, spread_c, spread_d, spread_s, sa,
    ) = go(
        "stage_a", stage_a, (global_views, local_views),
        [((big, channels), BF16), ((big, mid_1), BF16)],
        [
            acc(mid_1), ((mid_1, channels), BF16), (global_views.shape, BF16),
            (local_views.shape, BF16), pltpu.SemaphoreType.DMA((2,)),
        ],
        mid_1, 8,
        jobs=(
            ("spread", (ha,), 0, 1), ("fan", (0, ha), 1, 2), ("join", (1,), 2, 3),
            ("spread", (hb,), 0, 2), ("fan", (3, hb), 2, 4), ("join", (4,), 4, 5),
            ("all", (own_norms(first_norms, second_norms),), 1, None),
            ("spread", (hc,), 2, None), ("spread", (hd,), 3, None), ("spread", (hs,), 3, None),
        ),
        far=(0, 1),
    )
    count = sa
    wa, wb = rows_of(wa), rows_of(wb)
    norms_1, norms_2 = all_norms(norms, first_norms, second_norms)
    na, nb, nc = norms_1[:, :mid_1], norms_1[:, mid_1 : 2 * mid_1], norms_1[:, 2 * mid_1 :]
    nd, ne = norms_2[:, :mid_2], norms_2[:, mid_2 : 2 * mid_2]
    nf, ns = norms_2[:, 2 * mid_2 : 2 * mid_2 + wide], norms_2[:, 2 * mid_2 + wide :]
    zb, fan_c, wc, fan_d, fan_s, spread_e, sb = go(
        "stage_b", stage_b, (count, za, sa, na, wb), [((big, mid_1), BF16)],
        [((geo.halo_total, 3 * mid_1), BF16), acc(mid_1)], mid_1,
        jobs=(
            ("fan", (spread_c, hc), 0, 1), ("join", (0,), 1, None), ("fan", (spread_d, hd), 0, None),
            ("fan", (spread_s, hs), 0, None), ("spread", (he,), 0, None),
        ),
    )
    wc = rows_of(wc)
    zc, wd, ws, spread_f, fan_e, sc = go(
        "stage_c", stage_c, (count, zb, sb, nb, wc), [((big, channels), BF16)],
        [((geo.rows, mid_1), BF16), acc(channels)], channels,
        jobs=(
            ("join", (fan_d,), 0, None), ("join", (fan_s,), 0, None), ("spread", (hf,), 0, None),
            ("fan", (spread_e, he), 0, None),
        ),
    )
    wd, ws = rows_of(wd), rows_of(ws)
    hid, first_g, first_l, zd, zs, sub, local_s, we, fan_f, sd = go(
        "stage_d", stage_d, (count, zc, sc, nc, packed, wd, ws),
        [
            ((big, channels), BF16), (global_views.shape, BF16), (local_views.shape, BF16),
            ((big, mid_2), BF16), ((small, wide), BF16), ((small, channels), BF16), stat(wide // 2),
        ],
        [((channels // 128, geo.rows, 128), F32), acc(mid_2), acc(wide)], mid_2,
        jobs=(("join", (fan_e,), 0, None), ("fan", (spread_f, hf), 0, None)),
    )
    we = rows_of(we)
    ze, wf, ss, se = go(
        "stage_e", stage_e, (count, zd, sd, nd, we), [((small, mid_2), BF16)],
        [((mid_2 // 128, geo.halo, 128), F32), ((small, 9 * mid_2), BF16), acc(mid_2)], mid_2,
        jobs=(("join", (fan_f,), 0, None),), side=local_s,
    )
    wf = rows_of(wf)
    act_e, zf, sf = go(
        "stage_f", stage_f, (count, ze, se, ne, wf),
        [((small, mid_2), BF16), ((small, wide), BF16)], [acc(wide)], wide,
    )
    second_g, second_l, grad, local_pool, so = go(
        "stage_out", stage_out,
        (count, zf, zs, sf, ss, nf, ns, global_cotan, local_cotan),
        [
            (global_cotan.shape, BF16), (local_cotan.shape, BF16), ((small, wide), BF16),
            stat(wide // 4),
        ],
        [((geo.slabs, 8, wide), F32), ((geo.small, 512), F32), acc(wide, 8)], wide, 6,
    )
    wgrad_f, wgrad_s, back_sub, back_e, ngrad_f, ngrad_s, pool, qe = go(
        "stage_f_back", stage_f_back,
        (count, zf, zs, sf, ss, nf, ns, grad, so, act_e, sub, wf, ws, ze, se, ne),
        [
            pieces(wf), pieces(ws), ((small, channels), BF16), ((small, mid_2), BF16),
            stat(wide), stat(wide),
        ],
        [((small, wide), BF16), ((small, wide), BF16), acc(mid_2)], mid_2, side=local_pool,
    )
    views = count[8, 0] * 6.0
    pool = pool.reshape(2, wide)
    center = pool[0] / views
    spread = pool[1] / views - center * center
    pooled_std = jnp.mean(jnp.sqrt(spread + 1e-06))
    wgrad_e, back_d, ngrad_e, pair_f, pair_s, qd = go(
        "stage_e_back", stage_e_back,
        (count, ze, se, ne, back_e, qe, zd, sd, nd, we),
        [pieces(we), ((big, mid_2), BF16), stat(mid_2)],
        [
            ((mid_2 // 128, geo.halo, 128), F32), ((small, 9 * mid_2), BF16),
            ((small, mid_2), BF16), ((3, small, mid_2), BF16), ((4, small, mid_2), F32),
            acc(mid_2),
        ],
        mid_2, jobs=(("pair", (wgrad_f,), 0, None), ("pair", (wgrad_s,), 0, None)),
    )
    wgrad_d, joined, ngrad_d, rep_f, rep_s, pair_e, qc = go(
        "stage_d_back", stage_d_back,
        (count, zd, sd, nd, back_d, qd, hid, packed, zc, sc, nc, back_sub, wd),
        [pieces(wd), ((big, channels), BF16), stat(mid_2)],
        [((big, mid_2), BF16), ((channels // 128, geo.rows, 128), F32), acc(channels)], channels,
        jobs=(("rep", (pair_f,), 0, None), ("rep", (pair_s,), 0, None), ("pair", (wgrad_e,), 0, None)),
    )
    wgrad_c, back_b, ngrad_c, line_f, line_s, rep_e, pair_d, qb = go(
        "stage_c_back", stage_c_back,
        (count, zc, sc, nc, joined, qc, zb, sb, nb, wc),
        [pieces(wc), ((big, mid_1), BF16), stat(channels)],
        [((big, channels), BF16), ((big, mid_1), BF16), acc(mid_1)], mid_1,
        jobs=(("line", (rep_f,), 0, None), ("line", (rep_s,), 0, None), ("rep", (pair_e,), 0, None), ("pair", (wgrad_d,), 0, None)),
    )
    wgrad_b, back_a, ngrad_b, out_f, out_s, line_e, rep_d, pair_c, qa = go(
        "stage_b_back", stage_b_back,
        (count, zb, sb, nb, back_b, qb, za, sa, na, wb),
        [pieces(wb), ((big, mid_1), BF16), stat(mid_1)],
        [
            ((geo.halo_total, 3 * mid_1), BF16), ((geo.halo_total, 3 * mid_1), BF16),
            ((9 * mid_1, mid_1), BF16), (wb.shape, F32), acc(mid_1),
        ],
        mid_1,
        jobs=(
            ("share", (line_f,), 0, None), ("share", (line_s,), 0, None), ("line", (rep_e,), 0, None), ("rep", (pair_d,), 0, None), ("pair", (wgrad_c,), 0, None),
        ),
    )
    wgrad_a, grad_g, grad_l, ngrad_a, out_e, line_d, rep_c, pair_b = go(
        "stage_a_back", stage_a_back,
        (count, za, sa, na, back_a, qa, packed, joined, wa),
        [pieces(wa), (global_views.shape, F32), (local_views.shape, F32), stat(mid_1)],
        [((big, mid_1), BF16)],
        jobs=(("share", (line_e,), 0, None), ("line", (rep_d,), 0, None), ("rep", (pair_c,), 0, None), ("pair", (wgrad_b,), 0, None)),
    )
    out_a, out_b, out_c, out_d = run_tail(
        reps, shards, next(numbers),
        (
            (("pair", "rep", "line", "share"), wgrad_a), (("rep", "line", "share"), pair_b),
            (("line", "share"), rep_c), (("share",), line_d),
        ),
    )
    shard = lax.axis_index("fsdp")

    def own_columns(parts, width):
        whole = jnp.concatenate([part[0:2] for part in parts], axis=1)
        return lax.dynamic_slice_in_dim(whole, shard * width, width, 1)

    return (
        first_g, first_l, second_g, second_l, grad_g, grad_l,
        columns_of(out_a), columns_of(out_b), columns_of(out_c),
        own_columns((ngrad_a, ngrad_b, ngrad_c), first_norms.shape[1]),
        columns_of(out_d), columns_of(out_e), columns_of(out_f), columns_of(out_s),
        own_columns((ngrad_d, ngrad_e, ngrad_f, ngrad_s), second_norms.shape[1]),
        pooled_std,
    )


def solution(mesh):
    views = P(("rep", "fsdp"), None, None, None)
    columns = P(None, "fsdp")
    return jax.shard_map(
        functools.partial(body, mesh.shape["rep"], mesh.shape["fsdp"]),
        mesh=mesh,
        in_specs=(views, views, P(("rep", "fsdp"))) + (columns,) * 9 + (views, views),
        out_specs=(views,) * 6 + (columns,) * 9 + (P(),),
        check_vma=False,
    )
```

time: 1910 us -> 538 us (0.28); the launches traced: 1870 us -> 529 us
  local copies, waits for them, and re-layouts: 610 us -> 48.2 us
  blocking collectives: 510 us -> 0 us
  Pallas kernels: 0 us -> 474 us
  waiting for transfers between devices: 341 us -> 0 us
  other arithmetic: 203 us -> 1.92 us
  matrix products: 185 us -> 0 us
  between operations: 23.6 us -> 4.47 us
    pallas_call x0 -> x14, Pallas kernels: none -> 474 us  [the longest x13 448 us: run(): pl.pallas_call(whole, out_shape=[jax.ShapeDtypeStruct(shape, dtype) for s...]
    psum x11 -> x0, blocking collectives: 450 us -> none  [the longest x6 244 us: norm_back(): summed = lax.psum(tuple(members), ('rep', 'fsdp'))]
    pad x11 -> x0, local copies, waits for them, and re-layouts: 199 us -> none  [the longest x6 119 us: patches(): lax.slice(padded, (0, shift_row, shift_col, 0), (batch_views, shift_row +...]
    dot_general x42 -> x0, matrix products: 185 us -> none  [the longest x28 124 us: project(): return jnp.dot(operand, weight, preferred_element_type=jnp.float32)]
    reduce_scatter x6 -> x0, waiting for transfers between devices: 184 us -> none  [combine_grads(): lax.psum_scatter(for_sending(gradients), 'fsdp', scatter_dimension=1, til...]
    slice x11 -> x14, local copies, waits for them, and re-layouts: 190 us -> 8.86 us  [the longest x7 5.28 us: own_columns(): whole = jnp.concatenate([part[0:2] for part in parts], axis=1)]
    unnamed x451 -> x44, local copies, waits for them, and re-layouts: 194 us -> 31.9 us
    psum x2 -> x0, waiting for transfers between devices: 154 us -> none  [the longest x1 118 us: batch_norm(): summed = lax.psum(tuple(members), ('rep', 'fsdp'))]
  transfers between devices with their start and end apart: 14 -> 0, of which waited for: 7 -> 0; matrix products, arithmetic and copies ran while one was open for 23% -> 0% of each run, Pallas kernels for 0% -> 0%
where the time goes in v1:
time: 538 us; the launch traced here: 529 us
  Pallas kernels  474 us (88%)
  local copies, waits for them, and re-layouts  48.2 us (9%)
    pallas_call x13, Pallas kernels, run(): pl.pallas_call(whole, out_shape=[jax.ShapeDtypeStruct(shape, dtype) for s...  448 us
    unnamed x44, local copies, waits for them, and re-layouts  31.9 us
    pallas_call x1, Pallas kernels, run_tail(): pl.pallas_call(functools.partial(tail_kernel, reps, shards, plan), out_sh...  26.5 us

profile of v1, /device:TPU:0, one launch (start us, length us, event | category | flops | bytes accessed | tf_op | source)
XLA Modules:
  0.0 528.9 jit_solution(2638866886883797678)
XLA Ops:
  0.6 0.0 copy-start.13
  1.4 3.6 copy.43.refs_2_
  5.0 0.0 copy-done.13
  5.0 0.0 copy-done.14
  5.0 0.1 reshape.130
  5.1 0.6 reshape.159.refs_7_
  5.7 0.7 copy.41
  6.4 0.0 copy-done.5
  6.4 1.0 copy.42
  7.5 43.1 %stage_a.1 = (bf16[3200,1024]{1,0:T(8,128)(2,1)}, bf16[3200,256]{1,0:T(8,128)(2,1)}, bf16[4,8,1024]{2,1,0:T(8,128)(2,1)}, bf16[4,4,8,1024]{3,2,1,0:T(8,128)(2,1)...) custom-call(s32[1]{0:T(128)S(6)} %copy.62.refs_0_, ...), custom_call_target="tpu_custom_call" | custom-call | tf_op jit(solution)/shard_map/stage_a/pallas_call | solution.py:1179
  50.5 0.9 copy.53
  51.4 0.1 reshape.138
  51.5 0.1 reshape.139
  51.6 0.6 fusion.12
  52.2 50.4 %stage_b.1 = (bf16[3200,256]{1,0:T(8,128)(2,1)}, bf16[4,4,32,256]{3,2,1,0:T(8,128)(2,1)}, bf16[4,2,4,32,256]{4,3,2,1,0:T(8,128)(2,1)}, bf16[4,4,16,1024]{3,2,1,0...) custom-call(s32[1]{0:T(128)S(6)} %copy.62.refs_0_, ...), custom_call_target="tpu_custom_call" | custom-call | tf_op jit(solution)/shard_map/stage_b/pallas_call | solution.py:1179
  102.6 0.8 copy.45
  103.5 42.7 %stage_c.1 = (bf16[3200,1024]{1,0:T(8,128)(2,1)}, bf16[4,2,4,16,1024]{4,3,2,1,0:T(8,128)(2,1)}, bf16[4,2,4,64,1024]{4,3,2,1,0:T(8,128)(2,1)}, bf16[4,64,512]{2,1...) custom-call(s32[1]{0:T(128)S(6)} %copy.62.refs_0_, ...), custom_call_target="tpu_custom_call" | custom-call | tf_op jit(solution)/shard_map/stage_c/pallas_call | solution.py:1179
  146.2 0.6 slice.81.refs_4_.refs_11_
  146.8 35.1 %stage_d.1 = (bf16[3200,1024]{1,0:T(8,128)(2,1)}, bf16[10,14,14,1024]{3,2,1,0:T(8,128)(2,1)}, bf16[20,6,6,1024]{3,2,1,0:T(8,128)(2,1)}, bf16[3200,512]{1,0:T(8,1...) custom-call(s32[1]{0:T(128)S(6)} %copy.62.refs_0_, ...), custom_call_target="tpu_custom_call" | custom-call | tf_op jit(solution)/shard_map/stage_d/pallas_call | solution.py:1179
  181.9 3.6 copy.50
  185.5 0.6 fusion.11
  186.1 26.4 %stage_e.1 = (bf16[800,512]{1,0:T(8,128)(2,1)}, bf16[4,2,4,64,512]{4,3,2,1,0:T(8,128)(2,1)}, f32[8,1024]{1,0:T(8,128)}, f32[8,256]{1,0:T(8,128)}) custom-call(s32[1]{0:T(128)S(6)} %copy.62.refs_0_, f32[16,128]{1,0:T(8,128)} %get-tuple-element.109.refs_1_.refs_3_.refs_8_, bf16[3200,512]{1,0:T(8,128)(2,1)} %get-tuple-element.131.refs_2_.refs_7_, ...), custom_call_target="tpu_custom_call" | custom-call | tf_op jit(solution)/shard_map/stage_e/pallas_call | solution.py:1179
  212.6 0.0 copy-start.4
  212.6 15.7 %stage_f.1 = (bf16[800,512]{1,0:T(8,128)(2,1)}, bf16[800,2048]{1,0:T(8,128)(2,1)}, f32[8,1024]{1,0:T(8,128)}) custom-call(s32[1]{0:T(128)S(6)} %copy.62.refs_0_, f32[16,128]{1,0:T(8,128)} %get-tuple-element.109.refs_1_.refs_3_.refs_8_, bf16[800,512]{1,0:T(8,128)(2,1)} %get-tuple-element.136.refs_2_.refs_14_, f32[8,256]{1,0:T(8,128)} %get-tuple-element.137.refs_3_.refs_15_, ...), custom_call_target="tpu_custom_call" | custom-call | tf_op jit(solution)/shard_map/stage_f/pallas_call | solution.py:1179
  228.3 0.6 fusion.10
  228.9 1.6 copy.46.refs_9_
  230.5 27.0 %stage_out.1 = (bf16[10,7,7,2048]{3,2,1,0:T(8,128)(2,1)}, bf16[20,3,3,2048]{3,2,1,0:T(4,128)(2,1)}, bf16[800,2048]{1,0:T(8,128)(2,1)}, f32[8,512]{1,0:T(8,128)}, f32[24,512]{1,0:T(8,128)}) custom-call(s32[1]{0:T(128)S(6)} %copy.62.refs_0_, f32[16,128]{1,0:T(8,128)} %get-tuple-element.109.refs_1_.refs_3_.refs_8_, ...), custom_call_target="tpu_custom_call" | custom-call | tf_op jit(solution)/shard_map/stage_out/pallas_call | solution.py:1179
  257.6 2.7 copy.51
  260.2 32.3 %stage_f_back.1 = (bf16[2,4,4,64,512]{4,3,2,1,0:T(8,128)(2,1)}, bf16[2,4,4,64,1024]{4,3,2,1,0:T(8,128)(2,1)}, bf16[800,1024]{1,0:T(8,128)(2,1)}, bf16[800,512]{1...) custom-call(s32[1]{0:T(128)S(6)} %copy.62.refs_0_, ...), custom_call_target="tpu_custom_call" | custom-call | tf_op jit(solution)/shard_map/stage_f_back/pallas_call | solution.py:1179
  292.5 27.4 %stage_e_back.1 = (bf16[2,4,4,16,4608]{4,3,2,1,0:T(8,128)(2,1)}, bf16[3200,512]{1,0:T(8,128)(2,1)}, f32[8,512]{1,0:T(8,128)}, bf16[4,4,64,512]{3,2,1,0:T(8,128)(...) custom-call(s32[1]{0:T(128)S(6)} %copy.62.refs_0_, f32[16,128]{1,0:T(8,128)} %get-tuple-element.109.refs_1_.refs_3_.refs_8_, ...), custom_call_target="tpu_custom_call" | custom-call | tf_op jit(solution)/shard_map/stage_e_back/pallas_call | solution.py:1179
  319.9 55.0 %stage_d_back.1 = (bf16[2,4,4,16,1024]{4,3,2,1,0:T(8,128)(2,1)}, bf16[3200,1024]{1,0:T(8,128)(2,1)}, f32[8,512]{1,0:T(8,128)}, bf16[4,64,512]{2,1,0:T(8,128)(2,1...) custom-call(s32[1]{0:T(128)S(6)} %copy.62.refs_0_, ...), custom_call_target="tpu_custom_call" | custom-call | tf_op jit(solution)/shard_map/stage_d_back/pallas_call | solution.py:1179
  374.9 37.5 %stage_c_back.1 = (bf16[2,4,4,32,256]{4,3,2,1,0:T(8,128)(2,1)}, bf16[3200,256]{1,0:T(8,128)(2,1)}, f32[8,1024]{1,0:T(8,128)}, bf16[64,512]{1,0:T(8,128)(2,1)}, b...) custom-call(s32[1]{0:T(128)S(6)} %copy.62.refs_0_, ...), custom_call_target="tpu_custom_call" | custom-call | tf_op jit(solution)/shard_map/stage_c_back/pallas_call | solution.py:1179
  412.4 30.0 %stage_b_back.1 = (bf16[2,4,4,8,2304]{4,3,2,1,0:T(8,128)(2,1)}, bf16[3200,256]{1,0:T(8,128)(2,1)}, f32[8,256]{1,0:T(8,128)}, f32[4,64,512]{2,1,0:T(8,128)}, f32[...) custom-call(s32[1]{0:T(128)S(6)} %copy.62.refs_0_, ...), custom_call_target="tpu_custom_call" | custom-call | tf_op jit(solution)/shard_map/stage_b_back/pallas_call | solution.py:1179
  442.4 25.1 %stage_a_back.1 = (bf16[2,4,4,8,1024]{4,3,2,1,0:T(8,128)(2,1)}, f32[10,14,14,1024]{3,2,1,0:T(8,128)}, f32[20,6,6,1024]{3,2,1,0:T(8,128)}, f32[8,256]{1,0:T(8,128...) custom-call(s32[1]{0:T(128)S(6)} %copy.62.refs_0_, ...), custom_call_target="tpu_custom_call" | custom-call | tf_op jit(solution)/shard_map/stage_a_back/pallas_call | solution.py:1179
  467.5 0.0 copy-start.6
  467.5 5.8 %copy.52 = f32[20,6,6,1024]{3,0,2,1:T(8,128)} copy(f32[20,6,6,1024]{3,2,1,0:T(8,128)} %get-tuple-element.223) | data formatting | bytes 5898240
  473.3 26.5 %tail.1 = (f32[4,8,1024]{2,1,0:T(8,128)}, f32[4,8,2304]{2,1,0:T(8,128)}, f32[4,32,256]{2,1,0:T(8,128)}, f32[4,16,1024]{2,1,0:T(8,128)}) custom-call(bf16[2,4,4,8,1024]{4,3,2,1,0:T(8,128)(2,1)} %get-tuple-element.183.refs_0_, bf16[4,4,8,2304]{3,2,1,0:T(8,128)(2,1)} %get-tuple-element.184.refs_1_, bf16[4,32,256]{2,1,0:T(8,128)(2,1)} %get-tuple-element.185.refs_2_, ...), custom_call_target="tpu_custom_call" | custom-call | tf_op jit(solution)/shard_map/tail/pallas_call | solution.py:1231
  499.8 1.7 copy.47
  501.4 0.8 slice.70
  502.2 0.7 slice.69
  502.9 0.7 slice.68
  503.6 0.7 fusion.9
  504.3 0.0 copy-done.6
  504.3 1.0 copy.48
  505.3 1.3 copy.49
  506.6 0.8 slice.74
  507.4 0.8 slice.73
  508.3 0.7 slice.72
  509.0 0.7 slice.71
  509.7 0.6 fusion.5
  510.3 1.2 slice.76
  512.2 0.6 sqrt_reduce_fusion
  513.4 5.6 %copy.63 = bf16[10,14,14,1024]{3,2,1,0:T(8,128)(2,1)} copy(bf16[10,14,14,1024]{3,2,1,0:T(8,128)(2,1)} %get-tuple-element.256) | data formatting | bytes 8028160
  519.1 1.4 copy.64
  520.5 0.0 copy-done
  520.5 0.0 copy-start.2
  520.5 3.7 copy.65
  524.2 0.0 copy-done.10
  524.2 0.7 copy.66
  524.8 0.0 copy-done.7
  524.8 0.7 copy.67
  525.6 0.0 copy-done.9
  525.6 0.7 copy.68
  526.3 1.0 copy.69
  (24 shorter events, 0.1 us)
Async XLA Ops:
  0.6 4.3 copy-start.13
  0.7 4.3 copy-start.14
  0.7 5.0 copy-start.11
  0.7 5.8 %copy-start.5 = (bf16[1024,256]{1,0:T(8,128)(2,1)S(1)}, bf16[1024,256]{1,0:T(8,128)(2,1)}, u32[]{:S(2)}) copy-start(bf16[1024,256]{1,0:T(8,128)(2,1)} %param.24) | copy-start | bytes 1572868
  52.2 50.5 %copy-start.8 = (bf16[512,256]{1,0:T(8,128)(2,1)S(1)}, bf16[512,256]{1,0:T(8,128)(2,1)}, u32[]{:S(2)}) copy-start(bf16[512,256]{1,0:T(8,128)(2,1)} %param.23) | copy-start | bytes 786436
  212.6 16.4 %copy-start.4 = (bf16[20,3,3,2048]{3,0,2,1:T(8,128)(2,1)S(1)}, bf16[20,3,3,2048]{3,0,2,1:T(8,128)(2,1)}, u32[]{:S(2)}) copy-start(bf16[20,3,3,2048]{3,0,2,1:T(8,128)(2,1)} %param.27) | copy-start | bytes 2211844
  467.5 36.8 %copy-start.6 = (f32[4,64,512]{2,1,0:T(8,128)S(1)}, f32[4,64,512]{2,1,0:T(8,128)}, u32[]{:S(2)}) copy-start(f32[4,64,512]{2,1,0:T(8,128)} %get-tuple-element.195) | copy-start | bytes 1572868
  473.2 32.0 %copy-start.3 = (f32[4,64,1024]{2,1,0:T(8,128)S(1)}, f32[4,64,1024]{2,1,0:T(8,128)}, u32[]{:S(2)}) copy-start(f32[4,64,1024]{2,1,0:T(8,128)} %get-tuple-element.196) | copy-start | bytes 3145732
  473.3 38.9 %copy-start.12 = (f32[8,512]{1,0:T(8,128)S(1)}, f32[8,512]{1,0:T(8,128)}, u32[]{:S(2)}) copy-start(f32[8,512]{1,0:T(8,128)} %get-tuple-element.201) | copy-start | bytes 49156
  505.3 13.8 %copy-start.1 = (bf16[10,7,7,2048]{3,2,1,0:T(8,128)(2,1)S(1)}, bf16[10,7,7,2048]{3,2,1,0:T(8,128)(2,1)}, u32[]{:S(2)}) copy-start(bf16[10,7,7,2048]{3,2,1,0:T(8,128)(2,1)} %get-tuple-element.258) | copy-start | bytes 6021124
  513.4 7.0 %copy-start = (f32[10,14,14,1024]{3,2,1,0:T(8,128)S(1)}, f32[10,14,14,1024]{3,2,1,0:T(8,128)}, u32[]{:S(2)}) copy-start(f32[10,14,14,1024]{3,2,1,0:T(8,128)} %get-tuple-element.260) | copy-start | bytes 24084484
  520.5 3.7 copy-start.10
  520.5 4.4 copy-start.7
  520.5 5.1 copy-start.9
  520.5 5.8 %copy-start.2 = (f32[4,16,4608]{2,1,0:T(8,128)S(1)}, f32[4,16,4608]{2,1,0:T(8,128)}, u32[]{:S(2)}) copy-start(f32[4,16,4608]{2,1,0:T(8,128)} %get-tuple-element.194) | copy-start | bytes 3538948

commit v2 on v1

--- a/solution.py
+++ b/solution.py
@@ -142,7 +142,6 @@
         scale, by_value, constant, second = back_terms(stats, norm, number, group, first, raw)
         terms.append((scale, by_value, constant))
         seconds.append((second, first))
-    out[...] = jnp.zeros(out.shape, F32)
     out[0:1, :] = seconds[0][0] + seconds[1][0]
     out[1:2, :] = seconds[0][1] + seconds[1][1]
     return terms
@@ -343,12 +342,10 @@
 
 
 def stage_d(
-    geo, net, live, count, zc, stats_c, norm, packed, weight, short, hid, outg, outl, conv, conv_s,
-    sub, stats_s, full, acc, acc_s,
+    geo, net, live, count, zc, stats_c, norm, packed, weight, hid, outg, outl, conv, sub, full, acc,
 ):
     net.open()
     acc[...] = jnp.zeros(acc.shape, F32)
-    acc_s[...] = jnp.zeros(acc_s.shape, F32)
     width = zc.shape[1]
     terms = forward_terms(geo, count, stats_c, norm, width)
 
@@ -360,16 +357,7 @@
             joined = zc[rows, :].astype(F32) * scale + shift + packed[rows, :].astype(F32)
             value = silu(joined) * (geo.mask(size, group, width) * keep)
             put(full, pl.ds(start, size), value)
-            low = value.astype(BF16)
-            hid[rows, :] = low
-            for k in range(size // CELLS):
-                i = (start - group * geo.rg) // CELLS + k
-                if group == 0:
-                    outg[s, i] = low[k * CELLS : k * CELLS + geo.hg]
-                else:
-                    for side in range(2):
-                        begin = k * CELLS + side * CELLS // 2
-                        outl[2 * s + side, i] = low[begin : begin + geo.hl]
+            hid[rows, :] = value.astype(BF16)
         picked = [take(full, pl.ds(start, 8, stride=2)) for start in even_rows(geo)]
         sub[at(s, geo.small), :] = jnp.concatenate(picked, axis=0).astype(BF16)
         result = nt(hid[at(s, geo.rows), :], weight[...])
@@ -379,14 +367,27 @@
             acc[2 * group] += fold(piece)
             acc[2 * group + 1] += fold(piece * piece)
 
-    loop(geo.slabs, slab)
+    def emit(s):
+        for i in range(geo.hg):
+            start = pl.multiple_of(s * geo.rows + i * CELLS, CELLS)
+            outg[s, i] = hid[pl.ds(start, CELLS), :][0 : geo.hg]
+        for i in range(geo.hl):
+            start = pl.multiple_of(s * geo.rows + geo.rg + i * CELLS, CELLS)
+            rows = hid[pl.ds(start, CELLS), :]
+            for side in range(2):
+                begin = side * CELLS // 2
+                outl[2 * s + side, i] = rows[begin : begin + geo.hl]
+
+    half = geo.slabs // 2
+    loop(half, slab)
+    net.turn(1)
+    loop(geo.slabs - half, lambda s: slab(s + half))
+    net.turn(2)
     finish(net.own, acc, 4)
     net.begin()
-    half = short.shape[0] // 2
-    small_product(geo, sub, short, conv_s, acc_s, 0, half)
+    loop(half, emit)
     net.middle()
-    small_product(geo, sub, short, conv_s, acc_s, half, 2 * half)
-    finish(stats_s, acc_s, 4)
+    loop(geo.slabs - half, lambda s: emit(s + half))
     net.end()
 
 
@@ -435,13 +436,16 @@
     loop(geo.slabs, slab)
 
 
-def stage_e(geo, net, live, count, zd, stats_d, norm, weight, conv, full, taps, acc):
+def stage_e(
+    geo, net, live, count, zd, stats_d, norm, weight, sub, short, conv, conv_s, stats_s, full, taps,
+    acc, acc_s,
+):
     net.open()
-    net.side.begin()
     acc[...] = jnp.zeros(acc.shape, F32)
+    acc_s[...] = jnp.zeros(acc_s.shape, F32)
     terms = forward_terms(geo, count, stats_d, norm, zd.shape[1])
     gather_taps(geo, live, zd, terms, full, taps)
-    net.side.middle()
+    net.turn(1)
     step = 256
     for c in range(0, weight.shape[0], step):
         result = nt(taps[...], weight[c : c + step, :])
@@ -453,12 +457,20 @@
                 piece = piece * (geo.small_mask(group, step) * keep)
                 acc[2 * group, :, c : c + step] += fold(piece)
                 acc[2 * group + 1, :, c : c + step] += fold(piece * piece)
-    net.side.end()
+    net.turn(2)
     finish(net.own, acc, 4)
-    net.run()
+    net.begin()
+    half = short.shape[0] // 2
+    small_product(geo, sub, short, conv_s, acc_s, 0, half)
+    net.middle()
+    small_product(geo, sub, short, conv_s, acc_s, half, 2 * half)
+    finish(stats_s, acc_s, 4)
+    net.end()
 
 
 def stage_f(geo, net, live, count, ze, stats_e, norm, weight, act, conv, acc):
+    net.open()
+    net.side.begin()
     acc[...] = jnp.zeros(acc.shape, F32)
     width = ze.shape[1]
     terms = forward_terms(geo, count, stats_e, norm, width, True)
@@ -474,7 +486,11 @@
         act[at(s, geo.small), :] = jnp.concatenate(parts, axis=0).astype(BF16)
 
     loop(geo.slabs, slab)
-    small_product(geo, act, weight, conv, acc, 0, weight.shape[0])
+    half = weight.shape[0] // 2
+    small_product(geo, act, weight, conv, acc, 0, half)
+    net.side.middle()
+    small_product(geo, act, weight, conv, acc, half, 2 * half)
+    net.side.end()
     finish(net.own, acc, 4)
     net.run()
 
@@ -613,11 +629,13 @@
     for c in range(0, width, block):
         cols = slice(c, c + block)
         put_pieces(wgrad_f, c, tn(dzf[:, cols], act[...]))
+    net.turn(1)
     net.side.middle()
     net.middle()
     for c in range(0, width, block):
         cols = slice(c, c + block)
         put_pieces(wgrad_s, c, tn(dzs[:, cols], sub[...]))
+    net.turn(2)
     for c in range(0, sub.shape[1], block):
         cols = slice(c, c + block)
         back_sub[:, cols] = nn(dzs[...], short[:, cols]).astype(BF16)
@@ -629,12 +647,12 @@
     geo, net, live, count, ze, stats_e, norm_e, back_e, sums_e, zd, stats_d, norm_d, weight, wgrad,
     back_d, ngrad, full, taps, dze, moved, parity, acc,
 ):
+    net.open()
     acc[...] = jnp.zeros(acc.shape, F32)
     width = ze.shape[1]
     terms_e = backward_terms(geo, count, stats_e, norm_e, sums_e, ngrad, width, True)
     terms_d = forward_terms(geo, count, stats_d, norm_d, width)
     gather_taps(geo, live, zd, terms_d, full, taps)
-    net.open()
 
     def shift(s):
         value = small_back(geo, live, s, back_e, ze, terms_e, width, slice(0, width)).astype(F32)
@@ -689,6 +707,7 @@
             acc[2 * group + 1] += fold(piece * value)
 
     loop(geo.slabs, slab)
+    net.turn(1)
     finish(net.own, acc, 4)
     net.begin()
     grads(0, 4)
@@ -737,7 +756,11 @@
             acc[2 * group] += fold(piece)
             acc[2 * group + 1] += fold(piece * value)
 
-    loop(geo.slabs, slab)
+    third = geo.slabs // 3
+    loop(third, slab)
+    net.turn(1)
+    loop(geo.slabs - third, lambda s: slab(s + third))
+    net.turn(2)
     finish(net.own, acc, 4)
     block = 256
     net.begin()
@@ -777,7 +800,11 @@
             acc[2 * group] += fold(piece)
             acc[2 * group + 1] += fold(piece * value)
 
-    loop(geo.slabs, slab)
+    half = geo.slabs // 2
+    loop(half, slab)
+    net.turn(1)
+    loop(geo.slabs - half, lambda s: slab(s + half))
+    net.turn(2)
     finish(net.own, acc, 4)
     net.begin()
     half = dzc.shape[1] // 2
@@ -811,8 +838,9 @@
             values.append((value + constant) * (geo.mask(size, group, width) * keep))
         spread_taps(geo, dtaps, s, values, True)
 
+    net.open()
     loop(geo.slabs, fill)
-    net.open()
+    net.turn(1)
     span = geo.halo - CELLS
     total[...] = jnp.zeros(total.shape, F32)
 
@@ -844,6 +872,7 @@
             total[:, dy * 3 * width : (dy + 1) * 3 * width] += tn(own, taps[pl.ds(begin, span), :])
 
     loop(geo.slabs, slab)
+    net.turn(2)
     finish(net.own, acc, 4)
     half = geo.slabs // 2
     net.begin()
@@ -855,31 +884,65 @@
 
 
 def stage_a_back(
-    geo, net, live, count, za, stats_a, norm_a, back_a, sums_a, packed, joined, weight, wgrad, dxg, dxl,
-    ngrad, dza,
+    geo, net, live, count, za, stats_a, norm_a, back_a, sums_a, packed, wgrad, dza, ngrad,
 ):
+    net.open()
     terms_a = backward_terms(geo, count, stats_a, norm_a, sums_a, ngrad, za.shape[1])
-
-    net.open()
-
-    def slab(s):
-        wide_back(geo, live, s, back_a, za, terms_a, dza)
-        result = nn(dza[at(s, geo.rows), :], weight[...])
-        half = CELLS // 2
-        for i in range(geo.hg):
-            rows = pl.ds(pl.multiple_of(s * geo.rows + i * CELLS, CELLS), CELLS)
-            value = result[i * CELLS : (i + 1) * CELLS] + joined[rows, :].astype(F32)
-            dxg[s, i] = value[0 : geo.hg]
-        for i in range(geo.hl):
-            begin = geo.rg + i * CELLS
-            rows = pl.ds(pl.multiple_of(s * geo.rows + begin, CELLS), CELLS)
-            value = result[begin : begin + CELLS] + joined[rows, :].astype(F32)
-            for side in range(2):
-                dxl[2 * s + side, i] = value[side * half : side * half + geo.hl]
-
-    loop(geo.slabs, slab)
+    loop(geo.slabs, lambda s: wide_back(geo, live, s, back_a, za, terms_a, dza))
     put_pieces(wgrad, 0, tn(dza[...], packed[...]))
+    for number in range(1, 8):
+        net.turn(number)
     net.close()
+
+
+def last_kernel(geo, joined, dza, weight, *refs):
+    count = (len(refs) - 2) // 2
+    rows_in, dxg, dxl, columns = refs[:count], refs[count], refs[count + 1], refs[count + 2 :]
+    result = nn(dza[...], weight[...]) + joined[...].astype(F32)
+    half = CELLS // 2
+    for i in range(geo.hg):
+        dxg[0, i] = result[i * CELLS : i * CELLS + geo.hg]
+    for i in range(geo.hl):
+        for side in range(2):
+            begin = geo.rg + i * CELLS + side * half
+            dxl[side, i] = result[begin : begin + geo.hl]
+
+    def turn_over(k):
+        @pl.when(pl.program_id(0) == k % geo.slabs)
+        def write():
+            source, target = rows_in[k], columns[k]
+            size = target.shape[1]
+            whole = source[...].astype(F32).reshape(size, target.shape[0])
+            target[...] = whole.T
+
+    for k in range(count):
+        turn_over(k)
+
+
+def run_last(geo, joined, dza, weight, parts, global_shape, local_shape):
+    def whole(shape):
+        return pl.BlockSpec(shape, lambda s: (0,) * len(shape))
+
+    shapes = [(part.shape[-1], part.shape[0] * part.shape[1]) for part in parts]
+    return pl.pallas_call(
+        functools.partial(last_kernel, geo),
+        grid=(geo.slabs,),
+        out_shape=[jax.ShapeDtypeStruct(global_shape, F32), jax.ShapeDtypeStruct(local_shape, F32)]
+        + [jax.ShapeDtypeStruct(shape, F32) for shape in shapes],
+        in_specs=[
+            pl.BlockSpec((geo.rows, joined.shape[1]), lambda s: (s, 0)),
+            pl.BlockSpec((geo.rows, dza.shape[1]), lambda s: (s, 0)),
+            whole(weight.shape),
+        ]
+        + [whole(part.shape) for part in parts],
+        out_specs=[
+            pl.BlockSpec((1,) + global_shape[1:], lambda s: (s, 0, 0, 0)),
+            pl.BlockSpec((2,) + local_shape[1:], lambda s: (s, 0, 0, 0)),
+        ]
+        + [whole(shape) for shape in shapes],
+        compiler_params=pltpu.CompilerParams(vmem_limit_bytes=VMEM_CAP),
+        name="last",
+    )(joined, dza, weight, *parts)
 
 
 class Sums:
@@ -952,16 +1015,20 @@
             self.turn(0)
 
     def turn(self, number):
-        for k, (start, end) in enumerate(self.plans):
+        for k, (start, middle, end) in enumerate(self.plans):
             if end == number:
                 self.finish(k)
-        for k, (start, end) in enumerate(self.plans):
+        for k, (start, middle, end) in enumerate(self.plans):
+            if middle == number:
+                self.jobs[k].middle()
+        for k, (start, middle, end) in enumerate(self.plans):
             if start == number:
                 self.started.add(k)
                 self.jobs[k].start()
 
     def finish(self, k):
         assert k in self.started and k not in self.finished
+        self.jobs[k].middle()
         self.finished.add(k)
         self.jobs[k].finish()
 
@@ -996,6 +1063,7 @@
         self.sources = sources
         self.send, self.recv = send, recv
         self.reps, self.chips = reps, shards // 2
+        self.halving = kind == "rep" and reps == 4
         self.rep, shard = lax.axis_index("rep"), lax.axis_index("fsdp")
         self.chip, self.core = shard // 2, lax.rem(shard, 2)
         if kind in ("pair", "join"):
@@ -1041,14 +1109,59 @@
             for hop in order:
                 for chip in range(self.chips):
                     self.give(self.source.at[chip], out.at[chip, self.core], hop)
-        elif kind == "all":
+        elif kind in ("all", "share"):
             for hop in order:
                 self.give(self.source, out.at[self.me], hop)
+        elif self.halving:
+            low, high = lax.rem(self.rep, 2), self.rep // 2
+            first = self.core == 0
+            mine = jnp.where(first, low, high)
+            self.rest = jnp.where(first, high, low)
+            unit, step = jnp.where(first, 1, 2), jnp.where(first, 2, 1)
+            self.partners = (
+                jnp.where(first, high * 2 + 1 - low, (1 - high) * 2 + low),
+                jnp.where(first, (1 - high) * 2 + low, high * 2 + 1 - low),
+            )
+            for k in range(2):
+                self.send_to(
+                    self.partners[0], self.source.at[(1 - mine) * unit + k * step],
+                    self.held.at[2 + k],
+                )
+            for k in range(2):
+                self.give(self.source.at[mine * unit + k * step], self.held.at[k], 0)
         else:
             for hop in order:
                 other = lax.rem(self.me + hop, self.members)
-                block = self.source if kind == "share" else self.source.at[other]
-                self.give(block, self.held.at[self.me], hop)
+                self.give(self.source.at[other], self.held.at[self.me], hop)
+        self.halfway = False
+
+    def send_to(self, rep, source, target):
+        k = len(self.copies)
+        copy = pltpu.make_async_remote_copy(
+            source, target, self.send.at[k], self.recv.at[k], device_id={"rep": rep},
+            device_id_type=MESH,
+        )
+        copy.start()
+        self.copies.append(copy)
+
+    def middle(self):
+        if not self.halving or self.halfway:
+            return
+        self.halfway = True
+        held = self.held
+        for copy in self.copies:
+            copy.wait()
+        blocks = held.shape[1]
+
+        def one(index):
+            k, place = index // blocks, lax.rem(index, blocks)
+            total = held[k, place].astype(F32) + held[2 + k, place].astype(F32)
+            held[k, place] = total.astype(BF16)
+
+        loop(2 * blocks, one)
+        done = len(self.copies)
+        self.send_to(self.partners[1], held.at[1 - self.rest], held.at[4])
+        self.copies = self.copies[done:]
 
     def finish(self):
         for copy in self.copies:
@@ -1056,9 +1169,13 @@
         held, out = self.held, self.out
         if held is None:
             return
-        if self.kind == "share":
-            for k in range(self.members):
-                out[k] = held[k].astype(F32)
+        if self.halving:
+
+            def add(place):
+                total = held[self.rest, place].astype(F32) + held[4, place].astype(F32)
+                out[place] = total.astype(BF16)
+
+            loop(held.shape[1], add)
             return
         blocks = held.shape[1:-2]
 
@@ -1093,7 +1210,9 @@
     if kind == "pair":
         return shape, (shape[2], shape[1]) + shape[3:], 2
     if kind == "share":
-        return (reps,) + shape, (reps,) + shape, reps
+        return None, (reps,) + shape, reps
+    if kind == "rep" and reps == 4:
+        return (5,) + shape[1:], shape[1:], 5
     return shape, shape[1:], shape[0]
 
 
@@ -1119,17 +1238,19 @@
     extra = []
     arrays = []
     shapes = []
-    for kind, sources, start, end in jobs:
+    for kind, sources, start, middle, end in jobs:
         source = sources[0]
         if isinstance(source, int):
             shape, dtype = shapes[source]
+        elif isinstance(source, str):
+            shape, dtype = results[int(source)]
         else:
             shape, dtype = source.shape, source.dtype
-        arrays += [item for item in sources if not isinstance(item, int)]
+        arrays += [item for item in sources if not isinstance(item, (int, str))]
         held, out, copies = job_shapes(kind, reps, shards, shape)
-        shapes.append((out, F32 if kind == "share" else dtype))
+        shapes.append((out, dtype))
         results.append(shapes[-1])
-        spaces.append(pl.ANY if kind in FAR else pltpu.VMEM)
+        spaces.append(pltpu.HBM if kind in FAR else pltpu.VMEM)
         extra += [] if held is None else [pltpu.VMEM(held, BF16)]
         extra += [pltpu.SemaphoreType.DMA((copies,))] * 2
     operands = tuple(operands)
@@ -1152,10 +1273,15 @@
         outs = refs[first_out : first_out + len(results)]
         more = list(refs[first_out + len(results) :])
         made = []
-        for k, (kind, sources, start, end) in enumerate(jobs):
-            refs_of = [
-                made[item].out if isinstance(item, int) else sources_in.pop(0) for item in sources
-            ]
+        for k, (kind, sources, start, middle, end) in enumerate(jobs):
+            refs_of = []
+            for item in sources:
+                if isinstance(item, int):
+                    refs_of.append(made[item].out)
+                elif isinstance(item, str):
+                    refs_of.append(outs[int(item)])
+                else:
+                    refs_of.append(sources_in.pop(0))
             held = more.pop(0) if job_shapes(kind, reps, shards, refs_of[0].shape)[0] else None
             made.append(
                 Job(kind, reps, shards, refs_of, outs[own_results + k], held, more.pop(0), more.pop(0))
@@ -1170,7 +1296,7 @@
             more = more[7:]
         net = None
         if remote:
-            plans = [(start, end) for unused, unused_too, start, end in jobs]
+            plans = [job[2:] for job in jobs]
             net = Net(reps, shards, main, beside, made, plans)
             net.enter()
         kernel(geo, net, *refs[: near + 1], *outs[:own_results], *more)
@@ -1180,7 +1306,7 @@
         whole,
         out_shape=[jax.ShapeDtypeStruct(shape, dtype) for shape, dtype in results],
         in_specs=[pl.BlockSpec(memory_space=pltpu.SMEM)]
-        + [pl.BlockSpec(memory_space=pl.ANY if k in far else pltpu.VMEM) for k in range(len(operands))]
+        + [pl.BlockSpec(memory_space=pltpu.HBM if k in far else pltpu.VMEM) for k in range(len(operands))]
         + [pl.BlockSpec(memory_space=pl.ANY)] * len(arrays),
         out_specs=[pl.BlockSpec(memory_space=space) for space in spaces],
         scratch_shapes=extra
@@ -1188,61 +1314,6 @@
         compiler_params=pltpu.CompilerParams(vmem_limit_bytes=VMEM_CAP, **params),
         name=name,
     )(live, *operands, *arrays)
-
-
-def tail_kernel(reps, shards, plan, *refs):
-    count = len(plan)
-    current = list(refs[:count])
-    outs, more = refs[count : 2 * count], list(refs[2 * count :])
-    net = Net(reps, shards)
-    net.enter()
-    net.open()
-    for turn in range(max(len(kinds) for kinds in plan)):
-        active = []
-        for k, kinds in enumerate(plan):
-            if turn >= len(kinds):
-                continue
-            held, send, recv = more[:3]
-            more = more[3:]
-            target = outs[k]
-            if turn < len(kinds) - 1:
-                target = more.pop(0)
-            job = Job(kinds[turn], reps, shards, (current[k],), target, held, send, recv)
-            job.start()
-            active.append((k, job))
-        for k, job in active:
-            job.finish()
-            current[k] = job.out
-
-
-def run_tail(reps, shards, number, entries):
-    shapes = [source.shape for unused, source in entries]
-    plan = [kinds for kinds, unused in entries]
-    scratch = []
-    for turn in range(max(len(kinds) for kinds in plan)):
-        for k, kinds in enumerate(plan):
-            if turn >= len(kinds):
-                continue
-            held, out, copies = job_shapes(kinds[turn], reps, shards, shapes[k])
-            scratch += [pltpu.VMEM(held, BF16)] + [pltpu.SemaphoreType.DMA((copies,))] * 2
-            if turn < len(kinds) - 1:
-                scratch.append(pltpu.VMEM(out, BF16))
-            shapes[k] = out
-    return pl.pallas_call(
-        functools.partial(tail_kernel, reps, shards, plan),
-        out_shape=[jax.ShapeDtypeStruct(shape, F32) for shape in shapes],
-        in_specs=[pl.BlockSpec(memory_space=pl.ANY)] * len(entries),
-        out_specs=[pl.BlockSpec(memory_space=pltpu.VMEM)] * len(entries),
-        scratch_shapes=scratch,
-        compiler_params=pltpu.CompilerParams(
-            vmem_limit_bytes=VMEM_CAP, collective_id=number, has_side_effects=True
-        ),
-        name="tail",
-    )(*[source for unused, source in entries])
-
-
-def columns_of(rows):
-    return rows.reshape(-1, rows.shape[-1]).T
 
 
 def own_norms(first, second):
@@ -1306,8 +1377,11 @@
     def stat(width):
         return ((8, width), F32)
 
+    def both(width):
+        return ((2, width), F32)
+
     (
-        packed, za, spread_a, fan_a, wa, spread_b, fan_b, wb, norms, spread_c, spread_d, spread_s, sa,
+        packed, za, spread_a, fan_a, wa, spread_b, fan_b, wb, norms, spread_c, spread_d, sa,
     ) = go(
         "stage_a", stage_a, (global_views, local_views),
         [((big, channels), BF16), ((big, mid_1), BF16)],
@@ -1317,10 +1391,10 @@
         ],
         mid_1, 8,
         jobs=(
-            ("spread", (ha,), 0, 1), ("fan", (0, ha), 1, 2), ("join", (1,), 2, 3),
-            ("spread", (hb,), 0, 2), ("fan", (3, hb), 2, 4), ("join", (4,), 4, 5),
-            ("all", (own_norms(first_norms, second_norms),), 1, None),
-            ("spread", (hc,), 2, None), ("spread", (hd,), 3, None), ("spread", (hs,), 3, None),
+            ("spread", (ha,), 0, None, 1), ("fan", (0, ha), 1, None, 2), ("join", (1,), 2, None, 3),
+            ("spread", (hb,), 0, None, 2), ("fan", (3, hb), 2, None, 4), ("join", (4,), 4, None, 5),
+            ("all", (own_norms(first_norms, second_norms),), 1, None, None),
+            ("spread", (hc,), 2, None, None), ("spread", (hd,), 3, None, None),
         ),
         far=(0, 1),
     )
@@ -1330,43 +1404,50 @@
     na, nb, nc = norms_1[:, :mid_1], norms_1[:, mid_1 : 2 * mid_1], norms_1[:, 2 * mid_1 :]
     nd, ne = norms_2[:, :mid_2], norms_2[:, mid_2 : 2 * mid_2]
     nf, ns = norms_2[:, 2 * mid_2 : 2 * mid_2 + wide], norms_2[:, 2 * mid_2 + wide :]
-    zb, fan_c, wc, fan_d, fan_s, spread_e, sb = go(
+    zb, fan_c, wc, fan_d, spread_e, sb = go(
         "stage_b", stage_b, (count, za, sa, na, wb), [((big, mid_1), BF16)],
         [((geo.halo_total, 3 * mid_1), BF16), acc(mid_1)], mid_1,
         jobs=(
-            ("fan", (spread_c, hc), 0, 1), ("join", (0,), 1, None), ("fan", (spread_d, hd), 0, None),
-            ("fan", (spread_s, hs), 0, None), ("spread", (he,), 0, None),
+            ("fan", (spread_c, hc), 0, None, 1), ("join", (0,), 1, None, None),
+            ("fan", (spread_d, hd), 0, None, None), ("spread", (he,), 0, None, None),
         ),
     )
     wc = rows_of(wc)
-    zc, wd, ws, spread_f, fan_e, sc = go(
+    zc, wd, fan_e, spread_s, spread_f, sc = go(
         "stage_c", stage_c, (count, zb, sb, nb, wc), [((big, channels), BF16)],
         [((geo.rows, mid_1), BF16), acc(channels)], channels,
         jobs=(
-            ("join", (fan_d,), 0, None), ("join", (fan_s,), 0, None), ("spread", (hf,), 0, None),
-            ("fan", (spread_e, he), 0, None),
+            ("join", (fan_d,), 0, None, None), ("fan", (spread_e, he), 0, None, None),
+            ("spread", (hs,), 0, None, None), ("spread", (hf,), 0, None, None),
         ),
     )
-    wd, ws = rows_of(wd), rows_of(ws)
-    hid, first_g, first_l, zd, zs, sub, local_s, we, fan_f, sd = go(
-        "stage_d", stage_d, (count, zc, sc, nc, packed, wd, ws),
+    wd = rows_of(wd)
+    hid, first_g, first_l, zd, sub, we, fan_s, ws, sd = go(
+        "stage_d", stage_d, (count, zc, sc, nc, packed, wd),
         [
             ((big, channels), BF16), (global_views.shape, BF16), (local_views.shape, BF16),
-            ((big, mid_2), BF16), ((small, wide), BF16), ((small, channels), BF16), stat(wide // 2),
+            ((big, mid_2), BF16), ((small, channels), BF16),
         ],
-        [((channels // 128, geo.rows, 128), F32), acc(mid_2), acc(wide)], mid_2,
-        jobs=(("join", (fan_e,), 0, None), ("fan", (spread_f, hf), 0, None)),
-    )
-    we = rows_of(we)
-    ze, wf, ss, se = go(
-        "stage_e", stage_e, (count, zd, sd, nd, we), [((small, mid_2), BF16)],
-        [((mid_2 // 128, geo.halo, 128), F32), ((small, 9 * mid_2), BF16), acc(mid_2)], mid_2,
-        jobs=(("join", (fan_f,), 0, None),), side=local_s,
+        [((channels // 128, geo.rows, 128), F32), acc(mid_2)], mid_2,
+        jobs=(
+            ("join", (fan_e,), 0, None, None), ("fan", (spread_s, hs), 0, None, 2),
+            ("join", (1,), 2, None, None),
+        ),
+    )
+    we, ws = rows_of(we), rows_of(ws)
+    ze, zs, local_s, fan_f, wf, se = go(
+        "stage_e", stage_e, (count, zd, sd, nd, we, sub, ws),
+        [((small, mid_2), BF16), ((small, wide), BF16), stat(wide // 2)],
+        [
+            ((mid_2 // 128, geo.halo, 128), F32), ((small, 9 * mid_2), BF16), acc(mid_2), acc(wide),
+        ],
+        mid_2,
+        jobs=(("fan", (spread_f, hf), 0, None, 2), ("join", (0,), 2, None, None)),
     )
     wf = rows_of(wf)
-    act_e, zf, sf = go(
+    act_e, zf, ss, sf = go(
         "stage_f", stage_f, (count, ze, se, ne, wf),
-        [((small, mid_2), BF16), ((small, wide), BF16)], [acc(wide)], wide,
+        [((small, mid_2), BF16), ((small, wide), BF16)], [acc(wide)], wide, side=local_s,
     )
     second_g, second_l, grad, local_pool, so = go(
         "stage_out", stage_out,
@@ -1377,83 +1458,95 @@
         ],
         [((geo.slabs, 8, wide), F32), ((geo.small, 512), F32), acc(wide, 8)], wide, 6,
     )
-    wgrad_f, wgrad_s, back_sub, back_e, ngrad_f, ngrad_s, pool, qe = go(
+    unused, unused, back_sub, back_e, ngrad_f, ngrad_s, pair_f, pair_s, pool, qe = go(
         "stage_f_back", stage_f_back,
         (count, zf, zs, sf, ss, nf, ns, grad, so, act_e, sub, wf, ws, ze, se, ne),
         [
             pieces(wf), pieces(ws), ((small, channels), BF16), ((small, mid_2), BF16),
-            stat(wide), stat(wide),
+            both(wide), both(wide),
         ],
-        [((small, wide), BF16), ((small, wide), BF16), acc(mid_2)], mid_2, side=local_pool,
+        [((small, wide), BF16), ((small, wide), BF16), acc(mid_2)], mid_2,
+        jobs=(("pair", ("0",), 1, None, None), ("pair", ("1",), 2, None, None)), side=local_pool,
     )
     views = count[8, 0] * 6.0
     pool = pool.reshape(2, wide)
     center = pool[0] / views
     spread = pool[1] / views - center * center
     pooled_std = jnp.mean(jnp.sqrt(spread + 1e-06))
-    wgrad_e, back_d, ngrad_e, pair_f, pair_s, qd = go(
+    wgrad_e, back_d, ngrad_e, rep_f, rep_s, qd = go(
         "stage_e_back", stage_e_back,
         (count, ze, se, ne, back_e, qe, zd, sd, nd, we),
-        [pieces(we), ((big, mid_2), BF16), stat(mid_2)],
+        [pieces(we), ((big, mid_2), BF16), both(mid_2)],
         [
             ((mid_2 // 128, geo.halo, 128), F32), ((small, 9 * mid_2), BF16),
             ((small, mid_2), BF16), ((3, small, mid_2), BF16), ((4, small, mid_2), F32),
             acc(mid_2),
         ],
-        mid_2, jobs=(("pair", (wgrad_f,), 0, None), ("pair", (wgrad_s,), 0, None)),
-    )
-    wgrad_d, joined, ngrad_d, rep_f, rep_s, pair_e, qc = go(
+        mid_2, jobs=(("rep", (pair_f,), 0, 1, None), ("rep", (pair_s,), 0, 1, None)),
+    )
+    wgrad_d, joined, ngrad_d, unused, rep_e, line_f, line_s, qc = go(
         "stage_d_back", stage_d_back,
         (count, zd, sd, nd, back_d, qd, hid, packed, zc, sc, nc, back_sub, wd),
-        [pieces(wd), ((big, channels), BF16), stat(mid_2)],
+        [pieces(wd), ((big, channels), BF16), both(mid_2)],
         [((big, mid_2), BF16), ((channels // 128, geo.rows, 128), F32), acc(channels)], channels,
-        jobs=(("rep", (pair_f,), 0, None), ("rep", (pair_s,), 0, None), ("pair", (wgrad_e,), 0, None)),
-    )
-    wgrad_c, back_b, ngrad_c, line_f, line_s, rep_e, pair_d, qb = go(
+        jobs=(
+            ("pair", (wgrad_e,), 0, None, 1), ("rep", (0,), 1, 2, None),
+            ("line", (rep_f,), 0, None, None), ("line", (rep_s,), 0, None, None),
+        ),
+    )
+    wgrad_c, back_b, ngrad_c, unused, rep_d, line_e, out_f, out_s, qb = go(
         "stage_c_back", stage_c_back,
         (count, zc, sc, nc, joined, qc, zb, sb, nb, wc),
-        [pieces(wc), ((big, mid_1), BF16), stat(channels)],
+        [pieces(wc), ((big, mid_1), BF16), both(channels)],
         [((big, channels), BF16), ((big, mid_1), BF16), acc(mid_1)], mid_1,
-        jobs=(("line", (rep_f,), 0, None), ("line", (rep_s,), 0, None), ("rep", (pair_e,), 0, None), ("pair", (wgrad_d,), 0, None)),
-    )
-    wgrad_b, back_a, ngrad_b, out_f, out_s, line_e, rep_d, pair_c, qa = go(
+        jobs=(
+            ("pair", (wgrad_d,), 0, None, 1), ("rep", (0,), 1, 2, None),
+            ("line", (rep_e,), 0, None, None), ("share", (line_f,), 0, None, None),
+            ("share", (line_s,), 0, None, None),
+        ),
+    )
+    wgrad_b, back_a, ngrad_b, unused, rep_c, line_d, out_e, qa = go(
         "stage_b_back", stage_b_back,
         (count, zb, sb, nb, back_b, qb, za, sa, na, wb),
-        [pieces(wb), ((big, mid_1), BF16), stat(mid_1)],
+        [pieces(wb), ((big, mid_1), BF16), both(mid_1)],
         [
             ((geo.halo_total, 3 * mid_1), BF16), ((geo.halo_total, 3 * mid_1), BF16),
             ((9 * mid_1, mid_1), BF16), (wb.shape, F32), acc(mid_1),
         ],
         mid_1,
         jobs=(
-            ("share", (line_f,), 0, None), ("share", (line_s,), 0, None), ("line", (rep_e,), 0, None), ("rep", (pair_d,), 0, None), ("pair", (wgrad_c,), 0, None),
+            ("pair", (wgrad_c,), 0, None, 1), ("rep", (0,), 1, 2, None),
+            ("line", (rep_d,), 0, None, None), ("share", (line_e,), 0, None, None),
         ),
     )
-    wgrad_a, grad_g, grad_l, ngrad_a, out_e, line_d, rep_c, pair_b = go(
-        "stage_a_back", stage_a_back,
-        (count, za, sa, na, back_a, qa, packed, joined, wa),
-        [pieces(wa), (global_views.shape, F32), (local_views.shape, F32), stat(mid_1)],
-        [((big, mid_1), BF16)],
-        jobs=(("share", (line_e,), 0, None), ("line", (rep_d,), 0, None), ("rep", (pair_c,), 0, None), ("pair", (wgrad_b,), 0, None)),
-    )
-    out_a, out_b, out_c, out_d = run_tail(
-        reps, shards, next(numbers),
-        (
-            (("pair", "rep", "line", "share"), wgrad_a), (("rep", "line", "share"), pair_b),
-            (("line", "share"), rep_c), (("share",), line_d),
+    more = go(
+        "stage_a_back", stage_a_back, (count, za, sa, na, back_a, qa, packed),
+        [pieces(wa), ((big, mid_1), BF16), both(mid_1)], [],
+        jobs=(
+            ("pair", (wgrad_b,), 0, None, 1), ("rep", (0,), 1, 2, 3), ("line", (1,), 3, None, 4),
+            ("share", (2,), 4, None, None),
+            ("pair", ("0",), 1, None, 2), ("rep", (4,), 2, 3, 4), ("line", (5,), 4, None, 5),
+            ("share", (6,), 5, None, None),
+            ("line", (rep_c,), 0, None, 1), ("share", (8,), 1, None, None),
+            ("share", (line_d,), 0, None, None),
         ),
     )
+    dza, ngrad_a, out_b, out_a, out_c, out_d = (more[k] for k in (1, 2, 6, 10, 12, 13))
+    grad_g, grad_l, *columns = run_last(
+        geo, joined, dza, wa, (out_a, out_b, out_c, out_d, out_e, out_f, out_s),
+        global_views.shape, local_views.shape,
+    )
     shard = lax.axis_index("fsdp")
 
     def own_columns(parts, width):
-        whole = jnp.concatenate([part[0:2] for part in parts], axis=1)
+        whole = jnp.concatenate(parts, axis=1)
         return lax.dynamic_slice_in_dim(whole, shard * width, width, 1)
 
     return (
         first_g, first_l, second_g, second_l, grad_g, grad_l,
-        columns_of(out_a), columns_of(out_b), columns_of(out_c),
+        *columns[0:3],
         own_columns((ngrad_a, ngrad_b, ngrad_c), first_norms.shape[1]),
-        columns_of(out_d), columns_of(out_e), columns_of(out_f), columns_of(out_s),
+        *columns[3:7],
         own_columns((ngrad_d, ngrad_e, ngrad_f, ngrad_s), second_norms.shape[1]),
         pooled_std,
     )

time: 538 us -> 523 us (0.972)
  local copies, waits for them, and re-layouts: 48.2 us -> 38.9 us
    pallas_call x1, Pallas kernels: 26.5 us -> 15.1 us  [run_last(): pl.pallas_call(functools.partial(last_kernel, geo), grid=(geo.slabs,), ou...]
    pallas_call x13, Pallas kernels: 448 us -> 455 us  [run(): pl.pallas_call(whole, out_shape=[jax.ShapeDtypeStruct(shape, dtype) for s...]
    unnamed x44 -> x47, local copies, waits for them, and re-layouts: 31.9 us -> 31.9 us
where the time goes in v2:
time: 523 us; the launch traced here: 515 us
  Pallas kernels  470 us (90%)
  local copies, waits for them, and re-layouts  38.9 us (7%)
    pallas_call x13, Pallas kernels, run(): pl.pallas_call(whole, out_shape=[jax.ShapeDtypeStruct(shape, dtype) for s...  455 us
    unnamed x47, local copies, waits for them, and re-layouts  31.9 us
    pallas_call x1, Pallas kernels, run_last(): pl.pallas_call(functools.partial(last_kernel, geo), grid=(geo.slabs,), ou...  15.1 us

profile of v2, /device:TPU:0, one launch (start us, length us, event | category | flops | bytes accessed | tf_op | source)
XLA Modules:
  0.0 515.2 jit_solution(5351666376746032896)
XLA Ops:
  0.6 0.0 copy-start.13
  0.7 0.0 copy-start.16
  0.7 0.0 copy-start.6
  1.4 3.6 copy.43.refs_2_
  4.9 0.0 copy-done.13
  5.0 0.0 copy-done.16
  5.0 0.1 reshape.109
  5.1 0.6 reshape.131.refs_7_
  5.7 0.0 copy-done.6
  5.7 0.7 copy.42
  6.4 32.7 %stage_a.1 = (bf16[3200,1024]{1,0:T(8,128)(2,1)}, bf16[3200,256]{1,0:T(8,128)(2,1)}, bf16[4,8,1024]{2,1,0:T(8,128)(2,1)}, bf16[4,4,8,1024]{3,2,1,0:T(8,128)(2,1)...) custom-call(s32[1]{0:T(128)S(6)} %copy.59.refs_0_, ...), custom_call_target="tpu_custom_call" | custom-call | tf_op jit(solution)/shard_map/stage_a/pallas_call | solution.py:1305
  39.1 0.0 copy-start.4
  39.1 0.9 copy.55
  40.0 0.1 reshape.116
  40.1 0.1 reshape.117
  40.2 0.6 fusion.12
  40.8 24.9 %stage_b.1 = (bf16[3200,256]{1,0:T(8,128)(2,1)}, bf16[4,4,32,256]{3,2,1,0:T(8,128)(2,1)}, bf16[4,2,4,32,256]{4,3,2,1,0:T(8,128)(2,1)}, bf16[4,4,16,1024]{3,2,1,0...) custom-call(s32[1]{0:T(128)S(6)} %copy.59.refs_0_, f32[16,128]{1,0:T(8,128)} %get-tuple-element.108.refs_1_.refs_3_.refs_8_, ...), custom_call_target="tpu_custom_call" | custom-call | tf_op jit(solution)/shard_map/stage_b/pallas_call | solution.py:1305
  65.7 0.0 copy-done.4
  65.7 1.0 copy.45
  66.7 0.0 copy-done.5
  66.7 0.8 copy.46
  67.6 45.9 %stage_c.1 = (bf16[3200,1024]{1,0:T(8,128)(2,1)}, bf16[4,2,4,16,1024]{4,3,2,1,0:T(8,128)(2,1)}, bf16[4,4,16,4608]{3,2,1,0:T(8,128)(2,1)}, bf16[4,64,1024]{2,1,0:...) custom-call(s32[1]{0:T(128)S(6)} %copy.59.refs_0_, f32[16,128]{1,0:T(8,128)} %get-tuple-element.108.refs_1_.refs_3_.refs_8_, ...), custom_call_target="tpu_custom_call" | custom-call | tf_op jit(solution)/shard_map/stage_c/pallas_call | solution.py:1305
  113.5 0.6 slice.53.refs_4_.refs_11_
  114.1 52.5 %stage_d.1 = (bf16[3200,1024]{1,0:T(8,128)(2,1)}, bf16[10,14,14,1024]{3,2,1,0:T(8,128)(2,1)}, bf16[20,6,6,1024]{3,2,1,0:T(8,128)(2,1)}, bf16[3200,512]{1,0:T(8,1...) custom-call(s32[1]{0:T(128)S(6)} %copy.59.refs_0_, ...), custom_call_target="tpu_custom_call" | custom-call | tf_op jit(solution)/shard_map/stage_d/pallas_call | solution.py:1305
  166.6 3.6 copy.48
  170.3 0.6 fusion.11
  170.9 31.9 %stage_e.1 = (bf16[800,512]{1,0:T(8,128)(2,1)}, bf16[800,2048]{1,0:T(8,128)(2,1)}, f32[8,1024]{1,0:T(8,128)}, bf16[4,4,64,512]{3,2,1,0:T(8,128)(2,1)}, bf16[4,2,...) custom-call(s32[1]{0:T(128)S(6)} %copy.59.refs_0_, f32[16,128]{1,0:T(8,128)} %get-tuple-element.108.refs_1_.refs_3_.refs_8_, ...), custom_call_target="tpu_custom_call" | custom-call | tf_op jit(solution)/shard_map/stage_e/pallas_call | solution.py:1305
  202.8 0.0 copy-start.3
  202.8 26.3 %stage_f.1 = (bf16[800,512]{1,0:T(8,128)(2,1)}, bf16[800,2048]{1,0:T(8,128)(2,1)}, f32[8,1024]{1,0:T(8,128)}, f32[8,1024]{1,0:T(8,128)}) custom-call(s32[1]{0:T(128)S(6)} %copy.59.refs_0_, f32[16,128]{1,0:T(8,128)} %get-tuple-element.108.refs_1_.refs_3_.refs_8_, bf16[800,512]{1,0:T(8,128)(2,1)} %get-tuple-element.133.refs_2_.refs_14_, ...), custom_call_target="tpu_custom_call" | custom-call | tf_op jit(solution)/shard_map/stage_f/pallas_call | solution.py:1305
  229.1 0.6 fusion.10
  229.7 0.0 copy-done.3
  229.7 1.6 copy.47.refs_9_
  231.3 29.0 %stage_out.1 = (bf16[10,7,7,2048]{3,2,1,0:T(8,128)(2,1)}, bf16[20,3,3,2048]{3,2,1,0:T(4,128)(2,1)}, bf16[800,2048]{1,0:T(8,128)(2,1)}, f32[8,512]{1,0:T(8,128)}, f32[24,512]{1,0:T(8,128)}) custom-call(s32[1]{0:T(128)S(6)} %copy.59.refs_0_, f32[16,128]{1,0:T(8,128)} %get-tuple-element.108.refs_1_.refs_3_.refs_8_, ...), custom_call_target="tpu_custom_call" | custom-call | tf_op jit(solution)/shard_map/stage_out/pallas_call | solution.py:1305
  260.3 2.7 copy.49
  263.0 32.4 %stage_f_back.1 = (bf16[2,4,4,64,512]{4,3,2,1,0:T(8,128)(2,1)}, bf16[2,4,4,64,1024]{4,3,2,1,0:T(8,128)(2,1)}, bf16[800,1024]{1,0:T(8,128)(2,1)}, bf16[800,512]{1...) custom-call(s32[1]{0:T(128)S(6)} %copy.59.refs_0_, ...), custom_call_target="tpu_custom_call" | custom-call | tf_op jit(solution)/shard_map/stage_f_back/pallas_call | solution.py:1305
  295.3 41.4 %stage_e_back.1 = (bf16[2,4,4,16,4608]{4,3,2,1,0:T(8,128)(2,1)}, bf16[3200,512]{1,0:T(8,128)(2,1)}, f32[2,512]{1,0:T(2,128)}, bf16[4,64,512]{2,1,0:T(8,128)(2,1)...) custom-call(s32[1]{0:T(128)S(6)} %copy.59.refs_0_, f32[16,128]{1,0:T(8,128)} %get-tuple-element.108.refs_1_.refs_3_.refs_8_, ...), custom_call_target="tpu_custom_call" | custom-call | tf_op jit(solution)/shard_map/stage_e_back/pallas_call | solution.py:1305
  336.8 46.4 %stage_d_back.1 = (bf16[2,4,4,16,1024]{4,3,2,1,0:T(8,128)(2,1)}, bf16[3200,1024]{1,0:T(8,128)(2,1)}, f32[2,512]{1,0:T(2,128)}, bf16[4,4,16,4608]{3,2,1,0:T(8,128...) custom-call(s32[1]{0:T(128)S(6)} %copy.59.refs_0_, ...), custom_call_target="tpu_custom_call" | custom-call | tf_op jit(solution)/shard_map/stage_d_back/pallas_call | solution.py:1305
  383.2 30.5 %stage_c_back.1 = (bf16[2,4,4,32,256]{4,3,2,1,0:T(8,128)(2,1)}, bf16[3200,256]{1,0:T(8,128)(2,1)}, f32[2,1024]{1,0:T(2,128)}, bf16[4,4,16,1024]{3,2,1,0:T(8,128)...) custom-call(s32[1]{0:T(128)S(6)} %copy.59.refs_0_, ...), custom_call_target="tpu_custom_call" | custom-call | tf_op jit(solution)/shard_map/stage_c_back/pallas_call | solution.py:1305
  413.7 25.9 %stage_b_back.1 = (bf16[2,4,4,8,2304]{4,3,2,1,0:T(8,128)(2,1)}, bf16[3200,256]{1,0:T(8,128)(2,1)}, f32[2,256]{1,0:T(2,128)}, bf16[4,4,32,256]{3,2,1,0:T(8,128)(2...) custom-call(s32[1]{0:T(128)S(6)} %copy.59.refs_0_, ...), custom_call_target="tpu_custom_call" | custom-call | tf_op jit(solution)/shard_map/stage_b_back/pallas_call | solution.py:1305
  439.6 35.2 %stage_a_back.1 = (bf16[2,4,4,8,1024]{4,3,2,1,0:T(8,128)(2,1)}, bf16[3200,256]{1,0:T(8,128)(2,1)}, f32[2,256]{1,0:T(2,128)}, bf16[4,4,8,2304]{3,2,1,0:T(8,128)(2...) custom-call(s32[1]{0:T(128)S(6)} %copy.59.refs_0_, ...), custom_call_target="tpu_custom_call" | custom-call | tf_op jit(solution)/shard_map/stage_a_back/pallas_call | solution.py:1305
  474.8 15.1 %last.1 = (f32[10,14,14,1024]{3,2,1,0:T(8,128)}, f32[20,6,6,1024]{3,2,1,0:T(8,128)}, f32[1024,32]{1,0:T(8,128)}, f32[2304,32]{1,0:T(8,128)}, f32[256,128]{1,0:T(...) custom-call(bf16[3200,1024]{1,0:T(8,128)(2,1)} %get-tuple-element.158.refs_5_.joined, ...), custom_call_target="tpu_custom_call" | custom-call | tf_op jit(solution)/shard_map/last/pallas_call | solution.py:927
  489.9 0.0 copy-start.2
  489.9 0.0 copy-start.10
  489.9 0.0 copy-start.14
  489.9 0.0 copy-start.15
  489.9 5.8 %copy.50 = f32[20,6,6,1024]{3,0,2,1:T(8,128)} copy(f32[20,6,6,1024]{3,2,1,0:T(8,128)} %get-tuple-element.221) | data formatting | bytes 5898240
  495.7 2.0 copy.51
  497.8 0.0 copy-done.2
  497.8 1.1 copy.52
  498.8 0.0 copy-start.9
  498.8 0.0 copy-done.10
  498.8 0.0 copy-done.14
  498.9 0.0 copy-done.15
  498.9 0.7 fusion.9
  499.5 1.9 copy.53
  501.5 0.0 copy-done
  501.5 1.7 copy.54
  503.2 0.0 copy-done.7
  503.2 0.0 copy-done.12
  503.2 0.6 fusion.5
  503.8 1.2 slice.48
  505.7 0.6 sqrt_reduce_fusion
  507.0 5.5 %copy.60 = bf16[10,14,14,1024]{3,2,1,0:T(8,128)(2,1)} copy(bf16[10,14,14,1024]{3,2,1,0:T(8,128)(2,1)} %get-tuple-element.254) | data formatting | bytes 8028160
  512.5 1.4 copy.61
  (17 shorter events, 0.1 us)
Async XLA Ops:
  0.6 4.3 copy-start.13
  0.7 4.3 copy-start.16
  0.7 5.0 copy-start.6
  39.1 26.6 %copy-start.4 = (bf16[1024,256]{1,0:T(8,128)(2,1)S(1)}, bf16[1024,256]{1,0:T(8,128)(2,1)}, u32[]{:S(2)}) copy-start(bf16[1024,256]{1,0:T(8,128)(2,1)} %param.24) | copy-start | bytes 1572868
  40.8 25.9 %copy-start.5 = (bf16[512,256]{1,0:T(8,128)(2,1)S(1)}, bf16[512,256]{1,0:T(8,128)(2,1)}, u32[]{:S(2)}) copy-start(bf16[512,256]{1,0:T(8,128)(2,1)} %param.23) | copy-start | bytes 786436
  202.8 26.9 %copy-start.3 = (bf16[20,3,3,2048]{3,0,2,1:T(8,128)(2,1)S(1)}, bf16[20,3,3,2048]{3,0,2,1:T(8,128)(2,1)}, u32[]{:S(2)}) copy-start(bf16[20,3,3,2048]{3,0,2,1:T(8,128)(2,1)} %param.27) | copy-start | bytes 2211844
  489.9 7.9 %copy-start.2 = (f32[2304,32]{1,0:T(8,128)S(1)}, f32[2304,32]{1,0:T(8,128)}, u32[]{:S(2)}) copy-start(f32[2304,32]{1,0:T(8,128)} %get-tuple-element.223) | copy-start | bytes 884740
  489.9 8.9 %copy-start.10 = (f32[2,1024]{1,0:T(2,128)S(1)}, f32[2,1024]{1,0:T(2,128)}, u32[]{:S(2)}) copy-start(f32[2,1024]{1,0:T(2,128)} %get-tuple-element.190) | copy-start | bytes 24580
  489.9 8.9 %copy-start.14 = (f32[2,256]{1,0:T(2,128)S(1)}, f32[2,256]{1,0:T(2,128)}, u32[]{:S(2)}) copy-start(f32[2,256]{1,0:T(2,128)} %get-tuple-element.189) | copy-start | bytes 6148
  489.9 8.9 %copy-start.15 = (f32[2,256]{1,0:T(2,128)S(1)}, f32[2,256]{1,0:T(2,128)}, u32[]{:S(2)}) copy-start(f32[2,256]{1,0:T(2,128)} %get-tuple-element.188) | copy-start | bytes 6148
  495.7 5.7 %copy-start = (f32[4608,64]{1,0:T(8,128)S(1)}, f32[4608,64]{1,0:T(8,128)}, u32[]{:S(2)}) copy-start(f32[4608,64]{1,0:T(8,128)} %get-tuple-element.227) | copy-start | bytes 3538948
  498.8 4.4 copy-start.7
  498.8 4.4 copy-start.8
  498.8 4.4 copy-start.11
  498.8 4.4 copy-start.12
  498.8 6.8 %copy-start.9 = (f32[8,512]{1,0:T(8,128)S(1)}, f32[8,512]{1,0:T(8,128)}, u32[]{:S(2)}) copy-start(f32[8,512]{1,0:T(8,128)} %get-tuple-element.199) | copy-start | bytes 49156
  507.0 5.5 %copy-start.1 = (bf16[10,7,7,2048]{3,2,1,0:T(8,128)(2,1)S(1)}, bf16[10,7,7,2048]{3,2,1,0:T(8,128)(2,1)}, u32[]{:S(2)}) copy-start(bf16[10,7,7,2048]{3,2,1,0:T(8,128)(2,1)} %get-tuple-element.256) | copy-start | bytes 6021124

commit v3 on v2

--- a/solution.py
+++ b/solution.py
@@ -236,11 +236,8 @@
     loop(geo.slabs, slab)
     finish(net.own, acc, 4)
     net.own[8:16, :] = jnp.full((8, net.own.shape[1]), live[0], jnp.int32).astype(F32)
-    net.begin()
     net.turn(4)
-    net.middle()
-    net.turn(5)
-    net.end()
+    net.run()
 
 
 def spread_taps(geo, store, s, values, reverse):
@@ -308,6 +305,7 @@
             acc[2 * group + 1] += fold(piece * piece)
 
     loop(geo.slabs, slab)
+    net.turn(2)
     finish(net.own, acc, 4)
     net.run()
 
@@ -331,6 +329,7 @@
                 acc[2 * group + 1, :, c : c + step] += fold(piece * piece)
 
     loop(geo.slabs, slab)
+    net.turn(2)
     finish(net.own, acc, 4)
     net.run()
 
@@ -342,7 +341,7 @@
 
 
 def stage_d(
-    geo, net, live, count, zc, stats_c, norm, packed, weight, hid, outg, outl, conv, sub, full, acc,
+    geo, net, live, count, zc, stats_c, norm, packed, weight, hid, conv, sub, full, acc,
 ):
     net.open()
     acc[...] = jnp.zeros(acc.shape, F32)
@@ -367,34 +366,15 @@
             acc[2 * group] += fold(piece)
             acc[2 * group + 1] += fold(piece * piece)
 
-    def emit(s):
-        for i in range(geo.hg):
-            start = pl.multiple_of(s * geo.rows + i * CELLS, CELLS)
-            outg[s, i] = hid[pl.ds(start, CELLS), :][0 : geo.hg]
-        for i in range(geo.hl):
-            start = pl.multiple_of(s * geo.rows + geo.rg + i * CELLS, CELLS)
-            rows = hid[pl.ds(start, CELLS), :]
-            for side in range(2):
-                begin = side * CELLS // 2
-                outl[2 * s + side, i] = rows[begin : begin + geo.hl]
-
-    half = geo.slabs // 2
-    loop(half, slab)
-    net.turn(1)
-    loop(geo.slabs - half, lambda s: slab(s + half))
+    loop(geo.slabs, slab)
     net.turn(2)
     finish(net.own, acc, 4)
-    net.begin()
-    loop(half, emit)
-    net.middle()
-    loop(geo.slabs - half, lambda s: emit(s + half))
-    net.end()
-
-
-def small_product(geo, left, weight, conv, acc, first, last):
-    step = 256
+    net.run()
+
+
+def small_product(geo, left, pick, step, conv, acc, first, last):
     for c in range(first, last, step):
-        result = nt(left[...], weight[c : c + step, :])
+        result = nt(left[...], pick(c))
         conv[:, c : c + step] = result.astype(BF16)
         for s in range(geo.slabs):
             for start, size, group in geo.small_pieces():
@@ -437,8 +417,8 @@
 
 
 def stage_e(
-    geo, net, live, count, zd, stats_d, norm, weight, sub, short, conv, conv_s, stats_s, full, taps,
-    acc, acc_s,
+    geo, net, live, count, zd, stats_d, norm, weight_0, weight_1, weight_2, sub, conv, conv_s,
+    stats_s, full, taps, acc, acc_s,
 ):
     net.open()
     acc[...] = jnp.zeros(acc.shape, F32)
@@ -447,8 +427,11 @@
     gather_taps(geo, live, zd, terms, full, taps)
     net.turn(1)
     step = 256
-    for c in range(0, weight.shape[0], step):
-        result = nt(taps[...], weight[c : c + step, :])
+    third = weight_0.shape[1]
+    for c in range(0, weight_0.shape[0], step):
+        result = nt(taps[:, 0:third], weight_0[c : c + step, :])
+        result = result + nt(taps[:, third : 2 * third], weight_1[c : c + step, :])
+        result = result + nt(taps[:, 2 * third :], weight_2[c : c + step, :])
         conv[:, c : c + step] = result.astype(BF16)
         for s in range(geo.slabs):
             keep = alive(live, s)
@@ -460,10 +443,17 @@
     net.turn(2)
     finish(net.own, acc, 4)
     net.begin()
-    half = short.shape[0] // 2
-    small_product(geo, sub, short, conv_s, acc_s, 0, half)
+    short = net.job_out(0)
+    step = short.shape[2] * short.shape[3]
+
+    def pick(c):
+        part = c // step
+        return short[part // 2, part % 2].reshape(step, short.shape[4])
+
+    half = conv_s.shape[1] // 2
+    small_product(geo, sub, pick, step, conv_s, acc_s, 0, half)
     net.middle()
-    small_product(geo, sub, short, conv_s, acc_s, half, 2 * half)
+    small_product(geo, sub, pick, step, conv_s, acc_s, half, 2 * half)
     finish(stats_s, acc_s, 4)
     net.end()
 
@@ -486,10 +476,14 @@
         act[at(s, geo.small), :] = jnp.concatenate(parts, axis=0).astype(BF16)
 
     loop(geo.slabs, slab)
-    half = weight.shape[0] // 2
-    small_product(geo, act, weight, conv, acc, 0, half)
+    half, step = weight.shape[0] // 2, 256
+
+    def pick(c):
+        return weight[c : c + step, :]
+
+    small_product(geo, act, pick, step, conv, acc, 0, half)
     net.side.middle()
-    small_product(geo, act, weight, conv, acc, half, 2 * half)
+    small_product(geo, act, pick, step, conv, acc, half, 2 * half)
     net.side.end()
     finish(net.own, acc, 4)
     net.run()
@@ -628,13 +622,13 @@
     net.begin()
     for c in range(0, width, block):
         cols = slice(c, c + block)
-        put_pieces(wgrad_f, c, tn(dzf[:, cols], act[...]))
-    net.turn(1)
+        put_pieces(wgrad_s, c, tn(dzs[:, cols], sub[...]))
     net.side.middle()
     net.middle()
+    net.turn(1)
     for c in range(0, width, block):
         cols = slice(c, c + block)
-        put_pieces(wgrad_s, c, tn(dzs[:, cols], sub[...]))
+        put_pieces(wgrad_f, c, tn(dzf[:, cols], act[...]))
     net.turn(2)
     for c in range(0, sub.shape[1], block):
         cols = slice(c, c + block)
@@ -644,8 +638,8 @@
 
 
 def stage_e_back(
-    geo, net, live, count, ze, stats_e, norm_e, back_e, sums_e, zd, stats_d, norm_d, weight, wgrad,
-    back_d, ngrad, full, taps, dze, moved, parity, acc,
+    geo, net, live, count, ze, stats_e, norm_e, back_e, sums_e, zd, stats_d, norm_d, weight_0, weight_1,
+    weight_2, wgrad, back_d, ngrad, full, taps, dze, moved, parity, acc,
 ):
     net.open()
     acc[...] = jnp.zeros(acc.shape, F32)
@@ -669,7 +663,7 @@
     loop(geo.slabs, shift)
 
     def tap(dy, dx):
-        return weight[:, (dy * 3 + dx) * width : (dy * 3 + dx + 1) * width]
+        return (weight_0, weight_1, weight_2)[dy][:, dx * width : (dx + 1) * width]
 
     def grads(first, last):
         for t in range(first, last):
@@ -707,7 +701,6 @@
             acc[2 * group + 1] += fold(piece * value)
 
     loop(geo.slabs, slab)
-    net.turn(1)
     finish(net.own, acc, 4)
     net.begin()
     grads(0, 4)
@@ -895,54 +888,68 @@
     net.close()
 
 
-def last_kernel(geo, joined, dza, weight, *refs):
-    count = (len(refs) - 2) // 2
-    rows_in, dxg, dxl, columns = refs[:count], refs[count], refs[count + 1], refs[count + 2 :]
+def last_kernel(geo, upright, joined, dza, hid, weight, *refs):
+    count = len(upright)
+    rows_in, refs = refs[:count], refs[count:]
+    dxg, dxl, outg, outl = refs[:4]
+    targets = refs[4:]
     result = nn(dza[...], weight[...]) + joined[...].astype(F32)
     half = CELLS // 2
     for i in range(geo.hg):
         dxg[0, i] = result[i * CELLS : i * CELLS + geo.hg]
+        outg[0, i] = hid[i * CELLS : (i + 1) * CELLS, :][0 : geo.hg]
     for i in range(geo.hl):
+        begin = geo.rg + i * CELLS
+        low = hid[begin : begin + CELLS, :]
         for side in range(2):
-            begin = geo.rg + i * CELLS + side * half
-            dxl[side, i] = result[begin : begin + geo.hl]
-
-    def turn_over(k):
+            part = begin + side * half
+            dxl[side, i] = result[part : part + geo.hl]
+            outl[side, i] = low[side * half : side * half + geo.hl]
+
+    def write(k):
         @pl.when(pl.program_id(0) == k % geo.slabs)
-        def write():
-            source, target = rows_in[k], columns[k]
-            size = target.shape[1]
-            whole = source[...].astype(F32).reshape(size, target.shape[0])
-            target[...] = whole.T
+        def one():
+            source, target = rows_in[k], targets[k]
+            rows = source.shape[0] * source.shape[1]
+            whole = source[...].astype(F32).reshape(rows, source.shape[2])
+            target[...] = whole.T if upright[k] else whole
 
     for k in range(count):
-        turn_over(k)
-
-
-def run_last(geo, joined, dza, weight, parts, global_shape, local_shape):
+        write(k)
+
+
+def run_last(geo, joined, dza, hid, weight, parts, global_shape, local_shape):
     def whole(shape):
         return pl.BlockSpec(shape, lambda s: (0,) * len(shape))
 
-    shapes = [(part.shape[-1], part.shape[0] * part.shape[1]) for part in parts]
-    return pl.pallas_call(
-        functools.partial(last_kernel, geo),
+    upright = [part.shape[0] * part.shape[1] >= 128 for part in parts]
+    shapes = []
+    for turn, part in zip(upright, parts):
+        rows = part.shape[0] * part.shape[1]
+        shapes.append((part.shape[2], rows) if turn else (rows, part.shape[2]))
+    views = [
+        pl.BlockSpec((1,) + global_shape[1:], lambda s: (s, 0, 0, 0)),
+        pl.BlockSpec((2,) + local_shape[1:], lambda s: (s, 0, 0, 0)),
+    ]
+    outs = pl.pallas_call(
+        functools.partial(last_kernel, geo, upright),
         grid=(geo.slabs,),
-        out_shape=[jax.ShapeDtypeStruct(global_shape, F32), jax.ShapeDtypeStruct(local_shape, F32)]
+        out_shape=[
+            jax.ShapeDtypeStruct(shape, dtype)
+            for dtype in (F32, BF16)
+            for shape in (global_shape, local_shape)
+        ]
         + [jax.ShapeDtypeStruct(shape, F32) for shape in shapes],
         in_specs=[
-            pl.BlockSpec((geo.rows, joined.shape[1]), lambda s: (s, 0)),
-            pl.BlockSpec((geo.rows, dza.shape[1]), lambda s: (s, 0)),
-            whole(weight.shape),
+            pl.BlockSpec((geo.rows, item.shape[1]), lambda s: (s, 0)) for item in (joined, dza, hid)
         ]
+        + [whole(weight.shape)]
         + [whole(part.shape) for part in parts],
-        out_specs=[
-            pl.BlockSpec((1,) + global_shape[1:], lambda s: (s, 0, 0, 0)),
-            pl.BlockSpec((2,) + local_shape[1:], lambda s: (s, 0, 0, 0)),
-        ]
-        + [whole(shape) for shape in shapes],
+        out_specs=views + views + [whole(shape) for shape in shapes],
         compiler_params=pltpu.CompilerParams(vmem_limit_bytes=VMEM_CAP),
         name="last",
-    )(joined, dza, weight, *parts)
+    )(joined, dza, hid, weight, *parts)
+    return outs[:4], [item if turn else item.T for turn, item in zip(upright, outs[4:])]
 
 
 class Sums:
@@ -1015,20 +1022,16 @@
             self.turn(0)
 
     def turn(self, number):
-        for k, (start, middle, end) in enumerate(self.plans):
+        for k, (start, end) in enumerate(self.plans):
             if end == number:
                 self.finish(k)
-        for k, (start, middle, end) in enumerate(self.plans):
-            if middle == number:
-                self.jobs[k].middle()
-        for k, (start, middle, end) in enumerate(self.plans):
+        for k, (start, end) in enumerate(self.plans):
             if start == number:
                 self.started.add(k)
                 self.jobs[k].start()
 
     def finish(self, k):
         assert k in self.started and k not in self.finished
-        self.jobs[k].middle()
         self.finished.add(k)
         self.jobs[k].finish()
 
@@ -1063,7 +1066,6 @@
         self.sources = sources
         self.send, self.recv = send, recv
         self.reps, self.chips = reps, shards // 2
-        self.halving = kind == "rep" and reps == 4
         self.rep, shard = lax.axis_index("rep"), lax.axis_index("fsdp")
         self.chip, self.core = shard // 2, lax.rem(shard, 2)
         if kind in ("pair", "join"):
@@ -1075,6 +1077,20 @@
         elif kind == "all":
             self.members, self.me = shards, shard
             self.address = lambda k: {"fsdp": k}
+        elif kind == "half":
+            wide = reps // 2
+            even = lax.rem(self.rep, 2) == 0
+            self.members, self.me = 2, 0
+            aside = jnp.where(even, self.rep + 1, self.rep - 1)
+            across = lax.rem(self.rep + wide, reps)
+            self.address = lambda k: {"rep": jnp.where(self.core == 0, aside, across)}
+        elif kind == "rest":
+            wide = reps // 2
+            low, high = lax.rem(self.rep, 2), self.rep // wide
+            first = self.core == 0
+            self.members = wide
+            self.me = jnp.where(first, self.rep // 2, lax.rem(self.rep, wide))
+            self.address = lambda k: {"rep": jnp.where(first, k * 2 + low, high * wide + k)}
         else:
             self.members, self.me = reps, self.rep
             self.address = lambda k: {"rep": k}
@@ -1112,70 +1128,27 @@
         elif kind in ("all", "share"):
             for hop in order:
                 self.give(self.source, out.at[self.me], hop)
-        elif self.halving:
-            low, high = lax.rem(self.rep, 2), self.rep // 2
+        elif kind == "half":
+            wide = self.reps // 2
             first = self.core == 0
-            mine = jnp.where(first, low, high)
-            self.rest = jnp.where(first, high, low)
-            unit, step = jnp.where(first, 1, 2), jnp.where(first, 2, 1)
-            self.partners = (
-                jnp.where(first, high * 2 + 1 - low, (1 - high) * 2 + low),
-                jnp.where(first, (1 - high) * 2 + low, high * 2 + 1 - low),
-            )
-            for k in range(2):
-                self.send_to(
-                    self.partners[0], self.source.at[(1 - mine) * unit + k * step],
-                    self.held.at[2 + k],
-                )
-            for k in range(2):
-                self.give(self.source.at[mine * unit + k * step], self.held.at[k], 0)
+            low, high = lax.rem(self.rep, 2), self.rep // wide
+            mine = jnp.where(first, low, high * wide)
+            theirs = jnp.where(first, 1 - low, (1 - high) * wide)
+            step = jnp.where(first, 2, 1)
+            for k in range(wide):
+                self.give(self.source.at[theirs + k * step], self.held.at[1, k], 1)
+            for k in range(wide):
+                self.give(self.source.at[mine + k * step], self.held.at[0, k], 0)
         else:
             for hop in order:
                 other = lax.rem(self.me + hop, self.members)
                 self.give(self.source.at[other], self.held.at[self.me], hop)
-        self.halfway = False
-
-    def send_to(self, rep, source, target):
-        k = len(self.copies)
-        copy = pltpu.make_async_remote_copy(
-            source, target, self.send.at[k], self.recv.at[k], device_id={"rep": rep},
-            device_id_type=MESH,
-        )
-        copy.start()
-        self.copies.append(copy)
-
-    def middle(self):
-        if not self.halving or self.halfway:
-            return
-        self.halfway = True
-        held = self.held
-        for copy in self.copies:
-            copy.wait()
-        blocks = held.shape[1]
-
-        def one(index):
-            k, place = index // blocks, lax.rem(index, blocks)
-            total = held[k, place].astype(F32) + held[2 + k, place].astype(F32)
-            held[k, place] = total.astype(BF16)
-
-        loop(2 * blocks, one)
-        done = len(self.copies)
-        self.send_to(self.partners[1], held.at[1 - self.rest], held.at[4])
-        self.copies = self.copies[done:]
 
     def finish(self):
         for copy in self.copies:
             copy.wait()
         held, out = self.held, self.out
         if held is None:
-            return
-        if self.halving:
-
-            def add(place):
-                total = held[self.rest, place].astype(F32) + held[4, place].astype(F32)
-                out[place] = total.astype(BF16)
-
-            loop(held.shape[1], add)
             return
         blocks = held.shape[1:-2]
 
@@ -1186,7 +1159,7 @@
             total = held[(0,) + place].astype(F32)
             for k in range(1, self.members):
                 total = total + held[(k,) + place].astype(F32)
-            out[place[::-1]] = total.astype(BF16)
+            out[place[::-1] if self.kind == "pair" else place] = total.astype(BF16)
 
         if blocks:
             loop(blocks[0] * (blocks[1] if len(blocks) == 2 else 1), one)
@@ -1211,8 +1184,8 @@
         return shape, (shape[2], shape[1]) + shape[3:], 2
     if kind == "share":
         return None, (reps,) + shape, reps
-    if kind == "rep" and reps == 4:
-        return (5,) + shape[1:], shape[1:], 5
+    if kind == "half":
+        return (2, reps // 2) + shape[1:], (reps // 2,) + shape[1:], reps
     return shape, shape[1:], shape[0]
 
 
@@ -1238,7 +1211,7 @@
     extra = []
     arrays = []
     shapes = []
-    for kind, sources, start, middle, end in jobs:
+    for kind, sources, start, end in jobs:
         source = sources[0]
         if isinstance(source, int):
             shape, dtype = shapes[source]
@@ -1273,7 +1246,7 @@
         outs = refs[first_out : first_out + len(results)]
         more = list(refs[first_out + len(results) :])
         made = []
-        for k, (kind, sources, start, middle, end) in enumerate(jobs):
+        for k, (kind, sources, start, end) in enumerate(jobs):
             refs_of = []
             for item in sources:
                 if isinstance(item, int):
@@ -1349,6 +1322,7 @@
             second_expand, second_short,
         )
     )
+    he_0, he_1, he_2 = (he[:, :, k * he.shape[2] // 3 : (k + 1) * he.shape[2] // 3] for k in range(3))
     mid_1, mid_2 = first_reduce.shape[1] * shards, second_reduce.shape[1] * shards
     wide = second_expand.shape[1] * shards
 
@@ -1367,9 +1341,8 @@
             jobs, side, far,
         )
 
-    def pieces(weight):
-        size = weight.shape[0] // (shards * reps)
-        return ((2, shards // 2, reps, size, weight.shape[1]), BF16)
+    def pieces(rows, columns):
+        return ((2, shards // 2, reps, rows // (shards * reps), columns), BF16)
 
     def acc(width, members=4):
         return ((members, 8, width), F32)
@@ -1381,7 +1354,8 @@
         return ((2, width), F32)
 
     (
-        packed, za, spread_a, fan_a, wa, spread_b, fan_b, wb, norms, spread_c, spread_d, sa,
+        packed, za, spread_a, fan_a, wa, spread_b, fan_b, wb, norms, unused, unused, wc,
+        unused, fan_d, spread_e0, spread_e1, sa,
     ) = go(
         "stage_a", stage_a, (global_views, local_views),
         [((big, channels), BF16), ((big, mid_1), BF16)],
@@ -1391,60 +1365,57 @@
         ],
         mid_1, 8,
         jobs=(
-            ("spread", (ha,), 0, None, 1), ("fan", (0, ha), 1, None, 2), ("join", (1,), 2, None, 3),
-            ("spread", (hb,), 0, None, 2), ("fan", (3, hb), 2, None, 4), ("join", (4,), 4, None, 5),
-            ("all", (own_norms(first_norms, second_norms),), 1, None, None),
-            ("spread", (hc,), 2, None, None), ("spread", (hd,), 3, None, None),
+            ("spread", (ha,), 0, 1), ("fan", (0, ha), 1, 2), ("join", (1,), 2, 3),
+            ("spread", (hb,), 0, 2), ("fan", (3, hb), 2, 4), ("join", (4,), 4, None),
+            ("all", (own_norms(first_norms, second_norms),), 1, 4),
+            ("spread", (hc,), 0, 3), ("fan", (7, hc), 3, 4), ("join", (8,), 4, None),
+            ("spread", (hd,), 0, 3), ("fan", (10, hd), 3, 4),
+            ("spread", (he_0,), 3, 4), ("spread", (he_1,), 3, 4),
         ),
         far=(0, 1),
     )
     count = sa
-    wa, wb = rows_of(wa), rows_of(wb)
+    wa, wb, wc = rows_of(wa), rows_of(wb), rows_of(wc)
     norms_1, norms_2 = all_norms(norms, first_norms, second_norms)
     na, nb, nc = norms_1[:, :mid_1], norms_1[:, mid_1 : 2 * mid_1], norms_1[:, 2 * mid_1 :]
     nd, ne = norms_2[:, :mid_2], norms_2[:, mid_2 : 2 * mid_2]
     nf, ns = norms_2[:, 2 * mid_2 : 2 * mid_2 + wide], norms_2[:, 2 * mid_2 + wide :]
-    zb, fan_c, wc, fan_d, spread_e, sb = go(
+    zb, wd, fan_e0, fan_e1, spread_e2, spread_s, sb = go(
         "stage_b", stage_b, (count, za, sa, na, wb), [((big, mid_1), BF16)],
         [((geo.halo_total, 3 * mid_1), BF16), acc(mid_1)], mid_1,
         jobs=(
-            ("fan", (spread_c, hc), 0, None, 1), ("join", (0,), 1, None, None),
-            ("fan", (spread_d, hd), 0, None, None), ("spread", (he,), 0, None, None),
+            ("join", (fan_d,), 0, 2), ("fan", (spread_e0, he_0), 0, 2),
+            ("fan", (spread_e1, he_1), 0, 2), ("spread", (he_2,), 0, 2), ("spread", (hs,), 0, 2),
         ),
     )
-    wc = rows_of(wc)
-    zc, wd, fan_e, spread_s, spread_f, sc = go(
+    zc, we_0, we_1, fan_e2, spread_f, sc = go(
         "stage_c", stage_c, (count, zb, sb, nb, wc), [((big, channels), BF16)],
         [((geo.rows, mid_1), BF16), acc(channels)], channels,
         jobs=(
-            ("join", (fan_d,), 0, None, None), ("fan", (spread_e, he), 0, None, None),
-            ("spread", (hs,), 0, None, None), ("spread", (hf,), 0, None, None),
+            ("join", (fan_e0,), 0, 2), ("join", (fan_e1,), 0, 2),
+            ("fan", (spread_e2, he_2), 0, 2), ("spread", (hf,), 0, 2),
         ),
     )
     wd = rows_of(wd)
-    hid, first_g, first_l, zd, sub, we, fan_s, ws, sd = go(
+    hid, zd, sub, we_2, fan_s, sd = go(
         "stage_d", stage_d, (count, zc, sc, nc, packed, wd),
-        [
-            ((big, channels), BF16), (global_views.shape, BF16), (local_views.shape, BF16),
-            ((big, mid_2), BF16), ((small, channels), BF16),
-        ],
+        [((big, channels), BF16), ((big, mid_2), BF16), ((small, channels), BF16)],
         [((channels // 128, geo.rows, 128), F32), acc(mid_2)], mid_2,
-        jobs=(
-            ("join", (fan_e,), 0, None, None), ("fan", (spread_s, hs), 0, None, 2),
-            ("join", (1,), 2, None, None),
-        ),
-    )
-    we, ws = rows_of(we), rows_of(ws)
-    ze, zs, local_s, fan_f, wf, se = go(
-        "stage_e", stage_e, (count, zd, sd, nd, we, sub, ws),
+        jobs=(("join", (fan_e2,), 0, 2), ("fan", (spread_s, hs), 0, 2)),
+    )
+    we = tuple(rows_of(item) for item in (we_0, we_1, we_2))
+    ze, zs, local_s, ws, fan_f, wf, se = go(
+        "stage_e", stage_e, (count, zd, sd, nd, *we, sub),
         [((small, mid_2), BF16), ((small, wide), BF16), stat(wide // 2)],
         [
             ((mid_2 // 128, geo.halo, 128), F32), ((small, 9 * mid_2), BF16), acc(mid_2), acc(wide),
         ],
         mid_2,
-        jobs=(("fan", (spread_f, hf), 0, None, 2), ("join", (0,), 2, None, None)),
-    )
-    wf = rows_of(wf)
+        jobs=(
+            ("join", (fan_s,), 0, 2), ("fan", (spread_f, hf), 0, 2), ("join", (1,), 2, None),
+        ),
+    )
+    wf, ws = rows_of(wf), rows_of(ws)
     act_e, zf, ss, sf = go(
         "stage_f", stage_f, (count, ze, se, ne, wf),
         [((small, mid_2), BF16), ((small, wide), BF16)], [acc(wide)], wide, side=local_s,
@@ -1462,78 +1433,80 @@
         "stage_f_back", stage_f_back,
         (count, zf, zs, sf, ss, nf, ns, grad, so, act_e, sub, wf, ws, ze, se, ne),
         [
-            pieces(wf), pieces(ws), ((small, channels), BF16), ((small, mid_2), BF16),
+            pieces(wide, mid_2), pieces(wide, channels), ((small, channels), BF16), ((small, mid_2), BF16),
             both(wide), both(wide),
         ],
         [((small, wide), BF16), ((small, wide), BF16), acc(mid_2)], mid_2,
-        jobs=(("pair", ("0",), 1, None, None), ("pair", ("1",), 2, None, None)), side=local_pool,
+        jobs=(("pair", ("0",), 2, None), ("pair", ("1",), 1, None)), side=local_pool,
     )
     views = count[8, 0] * 6.0
     pool = pool.reshape(2, wide)
     center = pool[0] / views
     spread = pool[1] / views - center * center
     pooled_std = jnp.mean(jnp.sqrt(spread + 1e-06))
-    wgrad_e, back_d, ngrad_e, rep_f, rep_s, qd = go(
+    wgrad_e, back_d, ngrad_e, half_f, half_s, qd = go(
         "stage_e_back", stage_e_back,
-        (count, ze, se, ne, back_e, qe, zd, sd, nd, we),
-        [pieces(we), ((big, mid_2), BF16), both(mid_2)],
+        (count, ze, se, ne, back_e, qe, zd, sd, nd, *we),
+        [pieces(mid_2, 9 * mid_2), ((big, mid_2), BF16), both(mid_2)],
         [
             ((mid_2 // 128, geo.halo, 128), F32), ((small, 9 * mid_2), BF16),
             ((small, mid_2), BF16), ((3, small, mid_2), BF16), ((4, small, mid_2), F32),
             acc(mid_2),
         ],
-        mid_2, jobs=(("rep", (pair_f,), 0, 1, None), ("rep", (pair_s,), 0, 1, None)),
-    )
-    wgrad_d, joined, ngrad_d, unused, rep_e, line_f, line_s, qc = go(
+        mid_2, jobs=(("half", (pair_f,), 0, None), ("half", (pair_s,), 0, None)),
+    )
+    wgrad_d, joined, ngrad_d, unused, half_e, rest_f, rest_s, qc = go(
         "stage_d_back", stage_d_back,
         (count, zd, sd, nd, back_d, qd, hid, packed, zc, sc, nc, back_sub, wd),
-        [pieces(wd), ((big, channels), BF16), both(mid_2)],
+        [pieces(mid_2, channels), ((big, channels), BF16), both(mid_2)],
         [((big, mid_2), BF16), ((channels // 128, geo.rows, 128), F32), acc(channels)], channels,
         jobs=(
-            ("pair", (wgrad_e,), 0, None, 1), ("rep", (0,), 1, 2, None),
-            ("line", (rep_f,), 0, None, None), ("line", (rep_s,), 0, None, None),
+            ("pair", (wgrad_e,), 0, 1), ("half", (0,), 1, None),
+            ("rest", (half_f,), 0, 1), ("rest", (half_s,), 0, 1),
         ),
     )
-    wgrad_c, back_b, ngrad_c, unused, rep_d, line_e, out_f, out_s, qb = go(
+    wgrad_c, back_b, ngrad_c, pair_d, rest_e, line_f, line_s, qb = go(
         "stage_c_back", stage_c_back,
         (count, zc, sc, nc, joined, qc, zb, sb, nb, wc),
-        [pieces(wc), ((big, mid_1), BF16), both(channels)],
+        [pieces(channels, mid_1), ((big, mid_1), BF16), both(channels)],
         [((big, channels), BF16), ((big, mid_1), BF16), acc(mid_1)], mid_1,
         jobs=(
-            ("pair", (wgrad_d,), 0, None, 1), ("rep", (0,), 1, 2, None),
-            ("line", (rep_e,), 0, None, None), ("share", (line_f,), 0, None, None),
-            ("share", (line_s,), 0, None, None),
+            ("pair", (wgrad_d,), 0, 2), ("rest", (half_e,), 0, 2), ("line", (rest_f,), 0, 2),
+            ("line", (rest_s,), 0, 2),
         ),
     )
-    wgrad_b, back_a, ngrad_b, unused, rep_c, line_d, out_e, qa = go(
+    wgrad_b, back_a, ngrad_b, unused, rest_d, unused, half_c, line_e, out_f, out_s, qa = go(
         "stage_b_back", stage_b_back,
         (count, zb, sb, nb, back_b, qb, za, sa, na, wb),
-        [pieces(wb), ((big, mid_1), BF16), both(mid_1)],
+        [pieces(mid_1, 9 * mid_1), ((big, mid_1), BF16), both(mid_1)],
         [
             ((geo.halo_total, 3 * mid_1), BF16), ((geo.halo_total, 3 * mid_1), BF16),
             ((9 * mid_1, mid_1), BF16), (wb.shape, F32), acc(mid_1),
         ],
         mid_1,
         jobs=(
-            ("pair", (wgrad_c,), 0, None, 1), ("rep", (0,), 1, 2, None),
-            ("line", (rep_d,), 0, None, None), ("share", (line_e,), 0, None, None),
+            ("half", (pair_d,), 0, 1), ("rest", (0,), 1, 2), ("pair", (wgrad_c,), 0, 1),
+            ("half", (2,), 1, 2), ("line", (rest_e,), 0, 2), ("share", (line_f,), 0, 2),
+            ("share", (line_s,), 0, 2),
         ),
     )
     more = go(
         "stage_a_back", stage_a_back, (count, za, sa, na, back_a, qa, packed),
-        [pieces(wa), ((big, mid_1), BF16), both(mid_1)], [],
+        [pieces(mid_1, channels), ((big, mid_1), BF16), both(mid_1)], [],
         jobs=(
-            ("pair", (wgrad_b,), 0, None, 1), ("rep", (0,), 1, 2, 3), ("line", (1,), 3, None, 4),
-            ("share", (2,), 4, None, None),
-            ("pair", ("0",), 1, None, 2), ("rep", (4,), 2, 3, 4), ("line", (5,), 4, None, 5),
-            ("share", (6,), 5, None, None),
-            ("line", (rep_c,), 0, None, 1), ("share", (8,), 1, None, None),
-            ("share", (line_d,), 0, None, None),
+            ("pair", (wgrad_b,), 0, 1), ("half", (0,), 1, 2), ("rest", (1,), 2, 3),
+            ("line", (2,), 3, 4), ("share", (3,), 4, None),
+            ("pair", ("0",), 1, 2), ("half", (5,), 2, 3), ("rest", (6,), 3, 4),
+            ("line", (7,), 4, 5), ("share", (8,), 5, None),
+            ("rest", (half_c,), 0, 1), ("line", (10,), 1, 2), ("share", (11,), 2, None),
+            ("line", (rest_d,), 0, 1), ("share", (13,), 1, None),
+            ("share", (line_e,), 0, None),
         ),
     )
-    dza, ngrad_a, out_b, out_a, out_c, out_d = (more[k] for k in (1, 2, 6, 10, 12, 13))
-    grad_g, grad_l, *columns = run_last(
-        geo, joined, dza, wa, (out_a, out_b, out_c, out_d, out_e, out_f, out_s),
+    dza, ngrad_a = more[1], more[2]
+    out_b, out_a, out_c, out_d, out_e = (more[3 + k] for k in (4, 9, 12, 14, 15))
+    (grad_g, grad_l, first_g, first_l), columns = run_last(
+        geo, joined, dza, hid, wa, (out_a, out_b, out_c, out_d, out_e, out_f, out_s),
         global_views.shape, local_views.shape,
     )
     shard = lax.axis_index("fsdp")

time: 523 us -> 529 us (1.011)
  Pallas kernels: 470 us -> 489 us
  local copies, waits for them, and re-layouts: 38.9 us -> 25.9 us
    pallas_call x13, Pallas kernels: 455 us -> 470 us  [run(): pl.pallas_call(whole, out_shape=[jax.ShapeDtypeStruct(shape, dtype) for s...]
    unnamed x47 -> x38, local copies, waits for them, and re-layouts: 31.9 us -> 16.9 us
where the time goes in v3:
time: 529 us; the launch traced here: 522 us
  Pallas kernels  489 us (92%)
  local copies, waits for them, and re-layouts  25.9 us (5%)
    pallas_call x13, Pallas kernels, run(): pl.pallas_call(whole, out_shape=[jax.ShapeDtypeStruct(shape, dtype) for s...  470 us
    pallas_call x1, Pallas kernels, run_last(): pl.pallas_call(functools.partial(last_kernel, geo, upright), grid=(geo.sl...  18.3 us
    unnamed x38, local copies, waits for them, and re-layouts  16.9 us

profile of v3, /device:TPU:0, one launch (start us, length us, event | category | flops | bytes accessed | tf_op | source)
XLA Modules:
  0.0 522.0 jit_solution(4507372825824130263)
XLA Ops:
  1.3 1.9 fusion.10
  3.2 0.0 copy-start.6
  3.2 0.0 copy-start.12
  3.2 0.0 copy-start.14
  3.2 3.6 copy.39.refs_2_
  6.8 0.0 copy-done.6
  6.8 0.7 copy.38
  7.6 0.0 copy-done.12
  7.6 0.0 copy-done.14
  7.6 0.1 reshape.115
  7.7 0.6 reshape.139.refs_7_
  8.3 0.0 copy-start.4
  8.3 50.6 %stage_a.1 = (bf16[3200,1024]{1,0:T(8,128)(2,1)}, bf16[3200,256]{1,0:T(8,128)(2,1)}, bf16[4,8,1024]{2,1,0:T(8,128)(2,1)}, bf16[4,4,8,1024]{3,2,1,0:T(8,128)(2,1)...) custom-call(s32[1]{0:T(128)S(6)} %copy.50.refs_0_, ...), custom_call_target="tpu_custom_call" | custom-call | tf_op jit(solution)/shard_map/stage_a/pallas_call | solution.py:1278
  59.0 0.9 copy.47
  59.8 0.1 reshape.123
  59.9 0.1 reshape.124
  60.0 0.6 fusion.13
  60.6 0.0 copy-done.4
  60.6 1.0 copy.41
  61.6 0.0 copy-start.5
  61.6 40.0 %stage_b.1 = (bf16[3200,256]{1,0:T(8,128)(2,1)}, bf16[4,2,4,16,1024]{4,3,2,1,0:T(8,128)(2,1)}, bf16[4,4,16,1536]{3,2,1,0:T(8,128)(2,1)}, bf16[4,4,16,1536]{3,2,1...) custom-call(s32[1]{0:T(128)S(6)} %copy.50.refs_0_, ...), custom_call_target="tpu_custom_call" | custom-call | tf_op jit(solution)/shard_map/stage_b/pallas_call | solution.py:1278
  101.6 0.0 copy-done.5
  101.6 0.8 copy.42
  102.4 28.9 %stage_c.1 = (bf16[3200,1024]{1,0:T(8,128)(2,1)}, bf16[4,2,4,16,1536]{4,3,2,1,0:T(8,128)(2,1)}, bf16[4,2,4,16,1536]{4,3,2,1,0:T(8,128)(2,1)}, bf16[4,4,16,1536]{...) custom-call(s32[1]{0:T(128)S(6)} %copy.50.refs_0_, ...), custom_call_target="tpu_custom_call" | custom-call | tf_op jit(solution)/shard_map/stage_c/pallas_call | solution.py:1278
  131.4 0.6 slice.68.refs_4_.refs_11_
  132.0 48.6 %stage_d.1 = (bf16[3200,1024]{1,0:T(8,128)(2,1)}, bf16[3200,512]{1,0:T(8,128)(2,1)}, bf16[800,1024]{1,0:T(8,128)(2,1)}, bf16[4,2,4,16,1536]{4,3,2,1,0:T(8,128)(2...) custom-call(s32[1]{0:T(128)S(6)} %copy.50.refs_0_, f32[16,128]{1,0:T(8,128)} %get-tuple-element.116.refs_1_.refs_3_.refs_8_, ...), custom_call_target="tpu_custom_call" | custom-call | tf_op jit(solution)/shard_map/stage_d/pallas_call | solution.py:1278
  180.7 0.6 fusion.12
  181.3 32.6 %stage_e.1 = (bf16[800,512]{1,0:T(8,128)(2,1)}, bf16[800,2048]{1,0:T(8,128)(2,1)}, f32[8,1024]{1,0:T(8,128)}, bf16[4,2,4,64,1024]{4,3,2,1,0:T(8,128)(2,1)}, bf16...) custom-call(s32[1]{0:T(128)S(6)} %copy.50.refs_0_, ...), custom_call_target="tpu_custom_call" | custom-call | tf_op jit(solution)/shard_map/stage_e/pallas_call | solution.py:1278
  213.9 0.0 copy-start.3
  213.9 26.2 %stage_f.1 = (bf16[800,512]{1,0:T(8,128)(2,1)}, bf16[800,2048]{1,0:T(8,128)(2,1)}, f32[8,1024]{1,0:T(8,128)}, f32[8,1024]{1,0:T(8,128)}) custom-call(s32[1]{0:T(128)S(6)} %copy.50.refs_0_, f32[16,128]{1,0:T(8,128)} %get-tuple-element.116.refs_1_.refs_3_.refs_8_, bf16[800,512]{1,0:T(8,128)(2,1)} %get-tuple-element.143.refs_2_.refs_14_, ...), custom_call_target="tpu_custom_call" | custom-call | tf_op jit(solution)/shard_map/stage_f/pallas_call | solution.py:1278
  240.0 0.6 fusion.11
  240.6 0.0 copy-done.3
  240.6 1.6 copy.43.refs_9_
  242.2 29.2 %stage_out.1 = (bf16[10,7,7,2048]{3,2,1,0:T(8,128)(2,1)}, bf16[20,3,3,2048]{3,2,1,0:T(4,128)(2,1)}, bf16[800,2048]{1,0:T(8,128)(2,1)}, f32[8,512]{1,0:T(8,128)}, f32[24,512]{1,0:T(8,128)}) custom-call(s32[1]{0:T(128)S(6)} %copy.50.refs_0_, f32[16,128]{1,0:T(8,128)} %get-tuple-element.116.refs_1_.refs_3_.refs_8_, ...), custom_call_target="tpu_custom_call" | custom-call | tf_op jit(solution)/shard_map/stage_out/pallas_call | solution.py:1278
  271.5 30.3 %stage_f_back.1 = (bf16[2,4,4,64,512]{4,3,2,1,0:T(8,128)(2,1)}, bf16[2,4,4,64,1024]{4,3,2,1,0:T(8,128)(2,1)}, bf16[800,1024]{1,0:T(8,128)(2,1)}, bf16[800,512]{1...) custom-call(s32[1]{0:T(128)S(6)} %copy.50.refs_0_, ...), custom_call_target="tpu_custom_call" | custom-call | tf_op jit(solution)/shard_map/stage_f_back/pallas_call | solution.py:1278
  301.8 31.9 %stage_e_back.1 = (bf16[2,4,4,16,4608]{4,3,2,1,0:T(8,128)(2,1)}, bf16[3200,512]{1,0:T(8,128)(2,1)}, f32[2,512]{1,0:T(2,128)}, bf16[2,4,64,512]{3,2,1,0:T(8,128)(...) custom-call(s32[1]{0:T(128)S(6)} %copy.50.refs_0_, f32[16,128]{1,0:T(8,128)} %get-tuple-element.116.refs_1_.refs_3_.refs_8_, ...), custom_call_target="tpu_custom_call" | custom-call | tf_op jit(solution)/shard_map/stage_e_back/pallas_call | solution.py:1278
  333.7 0.0 copy-start.7
  333.8 0.0 copy-start.8
  333.8 0.0 copy-start.11
  333.8 43.7 %stage_d_back.1 = (bf16[2,4,4,16,1024]{4,3,2,1,0:T(8,128)(2,1)}, bf16[3200,1024]{1,0:T(8,128)(2,1)}, f32[2,512]{1,0:T(2,128)}, bf16[4,4,16,4608]{3,2,1,0:T(8,128...) custom-call(s32[1]{0:T(128)S(6)} %copy.50.refs_0_, ...), custom_call_target="tpu_custom_call" | custom-call | tf_op jit(solution)/shard_map/stage_d_back/pallas_call | solution.py:1278
  377.5 0.0 copy-done.7
  377.5 0.0 copy-done.8
  377.5 0.0 copy-done.11
  377.5 1.3 fusion.5
  378.8 35.2 %stage_c_back.1 = (bf16[2,4,4,32,256]{4,3,2,1,0:T(8,128)(2,1)}, bf16[3200,256]{1,0:T(8,128)(2,1)}, f32[2,1024]{1,0:T(2,128)}, bf16[4,4,16,1024]{3,2,1,0:T(8,128)...) custom-call(s32[1]{0:T(128)S(6)} %copy.50.refs_0_, ...), custom_call_target="tpu_custom_call" | custom-call | tf_op jit(solution)/shard_map/stage_c_back/pallas_call | solution.py:1278
  414.0 31.8 %stage_b_back.1 = (bf16[2,4,4,8,2304]{4,3,2,1,0:T(8,128)(2,1)}, bf16[3200,256]{1,0:T(8,128)(2,1)}, f32[2,256]{1,0:T(2,128)}, bf16[2,4,16,1024]{3,2,1,0:T(8,128)(...) custom-call(s32[1]{0:T(128)S(6)} %copy.50.refs_0_, ...), custom_call_target="tpu_custom_call" | custom-call | tf_op jit(solution)/shard_map/stage_b_back/pallas_call | solution.py:1278
  445.8 0.0 copy-start.10
  445.8 0.0 copy-start.13
  445.8 41.4 %stage_a_back.1 = (bf16[2,4,4,8,1024]{4,3,2,1,0:T(8,128)(2,1)}, bf16[3200,256]{1,0:T(8,128)(2,1)}, f32[2,256]{1,0:T(2,128)}, bf16[4,4,8,2304]{3,2,1,0:T(8,128)(2...) custom-call(s32[1]{0:T(128)S(6)} %copy.50.refs_0_, ...), custom_call_target="tpu_custom_call" | custom-call | tf_op jit(solution)/shard_map/stage_a_back/pallas_call | solution.py:1278
  487.2 0.0 copy-done.10
  487.2 0.0 copy-done.13
  487.2 1.3 fusion.9
  488.5 18.3 %last.1 = (f32[10,14,14,1024]{3,2,1,0:T(8,128)}, f32[20,6,6,1024]{3,2,1,0:T(8,128)}, bf16[10,14,14,1024]{3,2,1,0:T(8,128)(2,1)}, bf16[20,6,6,1024]{3,2,1,0:T(8,1...) custom-call(bf16[3200,1024]{1,0:T(8,128)(2,1)} %get-tuple-element.16, ...), custom_call_target="tpu_custom_call" | custom-call | tf_op jit(solution)/shard_map/last/pallas_call | solution.py:934
  506.8 0.0 copy-start.1
  506.8 5.8 %copy.46 = f32[20,6,6,1024]{3,0,2,1:T(8,128)} copy(f32[20,6,6,1024]{3,2,1,0:T(8,128)} %get-tuple-element.237) | data formatting | bytes 5898240
  512.7 0.0 copy-done.1
  512.7 2.1 copy.44
  514.8 1.2 slice.60
  516.6 0.0 copy-done.9
  516.6 0.6 sqrt_reduce_fusion
  517.9 0.0 copy-done.2
  517.9 1.5 copy.45
  519.3 0.0 copy-done
  519.3 1.4 copy.51
  (9 shorter events, 0.1 us)
Async XLA Ops:
  3.2 3.6 copy-start.6
  3.2 4.4 copy-start.12
  3.2 4.4 copy-start.14
  8.3 52.3 %copy-start.4 = (bf16[1024,256]{1,0:T(8,128)(2,1)S(1)}, bf16[1024,256]{1,0:T(8,128)(2,1)}, u32[]{:S(2)}) copy-start(bf16[1024,256]{1,0:T(8,128)(2,1)} %param.24) | copy-start | bytes 1572868
  61.6 40.0 %copy-start.5 = (bf16[512,256]{1,0:T(8,128)(2,1)S(1)}, bf16[512,256]{1,0:T(8,128)(2,1)}, u32[]{:S(2)}) copy-start(bf16[512,256]{1,0:T(8,128)(2,1)} %param.23) | copy-start | bytes 786436
  213.9 26.8 %copy-start.3 = (bf16[20,3,3,2048]{3,0,2,1:T(8,128)(2,1)S(1)}, bf16[20,3,3,2048]{3,0,2,1:T(8,128)(2,1)}, u32[]{:S(2)}) copy-start(bf16[20,3,3,2048]{3,0,2,1:T(8,128)(2,1)} %param.27) | copy-start | bytes 2211844
  333.7 43.7 %copy-start.7 = (f32[2,2048]{1,0:T(2,128)S(1)}, f32[2,2048]{1,0:T(2,128)}, u32[]{:S(2)}) copy-start(f32[2,2048]{1,0:T(2,128)} %get-tuple-element.213) | copy-start | bytes 49156
  333.8 43.7 %copy-start.8 = (f32[2,2048]{1,0:T(2,128)S(1)}, f32[2,2048]{1,0:T(2,128)}, u32[]{:S(2)}) copy-start(f32[2,2048]{1,0:T(2,128)} %get-tuple-element.214) | copy-start | bytes 49156
  333.8 43.7 %copy-start.11 = (f32[2,512]{1,0:T(2,128)S(1)}, f32[2,512]{1,0:T(2,128)}, u32[]{:S(2)}) copy-start(f32[2,512]{1,0:T(2,128)} %get-tuple-element.212) | copy-start | bytes 12292
  445.8 41.4 %copy-start.10 = (f32[2,1024]{1,0:T(2,128)S(1)}, f32[2,1024]{1,0:T(2,128)}, u32[]{:S(2)}) copy-start(f32[2,1024]{1,0:T(2,128)} %get-tuple-element.206) | copy-start | bytes 24580
  445.8 41.4 %copy-start.13 = (f32[2,256]{1,0:T(2,128)S(1)}, f32[2,256]{1,0:T(2,128)}, u32[]{:S(2)}) copy-start(f32[2,256]{1,0:T(2,128)} %get-tuple-element.205) | copy-start | bytes 6148
  506.8 5.9 %copy-start.1 = (bf16[20,6,6,1024]{3,2,1,0:T(8,128)(2,1)S(1)}, bf16[20,6,6,1024]{3,2,1,0:T(8,128)(2,1)}, u32[]{:S(2)}) copy-start(bf16[20,6,6,1024]{3,2,1,0:T(8,128)(2,1)} %get-tuple-element.233) | copy-start | bytes 4423684
  512.7 3.9 copy-start.9
  512.7 5.2 copy-start.2
  512.7 6.7 %copy-start = (bf16[10,7,7,2048]{3,2,1,0:T(8,128)(2,1)S(1)}, bf16[10,7,7,2048]{3,2,1,0:T(8,128)(2,1)}, u32[]{:S(2)}) copy-start(bf16[10,7,7,2048]{3,2,1,0:T(8,128)(2,1)} %get-tuple-element.275) | copy-start | bytes 6021124

commit v4 on v3

--- a/solution.py
+++ b/solution.py
@@ -215,14 +215,13 @@
                 place = pl.multiple_of(start + side * half, half)
                 packed[pl.ds(place, geo.hl), :] = own_l[2 * s + side, i] * keep
 
-    third = geo.slabs // 3
-    loop(third, pack)
-    net.turn(1)
-    loop(third, lambda s: pack(s + third))
-    net.turn(2)
-    loop(geo.slabs - 2 * third, lambda s: pack(s + 2 * third))
-    net.turn(3)
-    gathered = net.job_out(2)
+    part = geo.slabs // 4
+    for number in range(4):
+        begin = number * part
+        size = part if number < 3 else geo.slabs - begin
+        loop(size, lambda s: pack(s + begin))
+        net.turn(number + 1)
+    gathered = net.job_out(3)
     weight[...] = gathered[...].astype(F32).reshape(weight.shape).astype(BF16)
 
     def slab(s):
@@ -236,7 +235,7 @@
     loop(geo.slabs, slab)
     finish(net.own, acc, 4)
     net.own[8:16, :] = jnp.full((8, net.own.shape[1]), live[0], jnp.int32).astype(F32)
-    net.turn(4)
+    net.turn(5)
     net.run()
 
 
@@ -277,16 +276,17 @@
 
 
 def stage_b(geo, net, live, count, za, stats_a, norm, weight, conv, taps, acc):
-    net.open()
     acc[...] = jnp.zeros(acc.shape, F32)
     width = za.shape[1]
     terms = forward_terms(geo, count, stats_a, norm, width)
     clear_halo(geo, taps)
-    loop(
-        geo.slabs,
-        lambda s: spread_taps(geo, taps, s, activate(geo, live, za, s, terms), False),
-    )
-    net.turn(1)
+
+    def fill(s):
+        spread_taps(geo, taps, s, activate(geo, live, za, s, terms), False)
+
+    loop(2, fill)
+    net.open()
+    loop(geo.slabs - 2, lambda s: fill(s + 2))
     span = geo.halo - CELLS
 
     def slab(s):
@@ -304,14 +304,15 @@
             acc[2 * group] += fold(piece)
             acc[2 * group + 1] += fold(piece * piece)
 
-    loop(geo.slabs, slab)
+    loop(2, slab)
+    net.turn(1)
+    loop(geo.slabs - 2, lambda s: slab(s + 2))
     net.turn(2)
     finish(net.own, acc, 4)
     net.run()
 
 
 def stage_c(geo, net, live, count, zb, stats_b, norm, weight, conv, act, acc):
-    net.open()
     acc[...] = jnp.zeros(acc.shape, F32)
     terms = forward_terms(geo, count, stats_b, norm, zb.shape[1])
     step = 256
@@ -328,7 +329,11 @@
                 acc[2 * group, :, c : c + step] += fold(piece)
                 acc[2 * group + 1, :, c : c + step] += fold(piece * piece)
 
-    loop(geo.slabs, slab)
+    loop(2, slab)
+    net.open()
+    loop(4, lambda s: slab(s + 2))
+    net.turn(1)
+    loop(geo.slabs - 6, lambda s: slab(s + 6))
     net.turn(2)
     finish(net.own, acc, 4)
     net.run()
@@ -343,7 +348,6 @@
 def stage_d(
     geo, net, live, count, zc, stats_c, norm, packed, weight, hid, conv, sub, full, acc,
 ):
-    net.open()
     acc[...] = jnp.zeros(acc.shape, F32)
     width = zc.shape[1]
     terms = forward_terms(geo, count, stats_c, norm, width)
@@ -366,7 +370,11 @@
             acc[2 * group] += fold(piece)
             acc[2 * group + 1] += fold(piece * piece)
 
-    loop(geo.slabs, slab)
+    loop(1, slab)
+    net.open()
+    loop(4, lambda s: slab(s + 1))
+    net.turn(1)
+    loop(geo.slabs - 5, lambda s: slab(s + 5))
     net.turn(2)
     finish(net.own, acc, 4)
     net.run()
@@ -383,7 +391,7 @@
                 acc[2 * group + 1, :, c : c + step] += fold(piece * piece)
 
 
-def gather_taps(geo, live, zd, terms, full, taps):
+def gather_taps(geo, net, live, zd, terms, full, taps):
     width = zd.shape[1]
     blank = jnp.zeros((8, width), F32)
     full[:, 0:CELLS, :] = jnp.zeros((width // 128, CELLS, 128), F32)
@@ -413,18 +421,19 @@
                     picked, axis=0
                 ).astype(BF16)
 
-    loop(geo.slabs, slab)
+    loop(2, slab)
+    net.open()
+    loop(geo.slabs - 2, lambda s: slab(s + 2))
 
 
 def stage_e(
     geo, net, live, count, zd, stats_d, norm, weight_0, weight_1, weight_2, sub, conv, conv_s,
     stats_s, full, taps, acc, acc_s,
 ):
-    net.open()
     acc[...] = jnp.zeros(acc.shape, F32)
     acc_s[...] = jnp.zeros(acc_s.shape, F32)
     terms = forward_terms(geo, count, stats_d, norm, zd.shape[1])
-    gather_taps(geo, live, zd, terms, full, taps)
+    gather_taps(geo, net, live, zd, terms, full, taps)
     net.turn(1)
     step = 256
     third = weight_0.shape[1]
@@ -450,10 +459,12 @@
         part = c // step
         return short[part // 2, part % 2].reshape(step, short.shape[4])
 
-    half = conv_s.shape[1] // 2
-    small_product(geo, sub, pick, step, conv_s, acc_s, 0, half)
-    net.middle()
-    small_product(geo, sub, pick, step, conv_s, acc_s, half, 2 * half)
+    width = conv_s.shape[1]
+    small_product(geo, sub, pick, step, conv_s, acc_s, 0, width // 4)
+    net.step()
+    small_product(geo, sub, pick, step, conv_s, acc_s, width // 4, 5 * width // 8)
+    net.step()
+    small_product(geo, sub, pick, step, conv_s, acc_s, 5 * width // 8, width)
     finish(stats_s, acc_s, 4)
     net.end()
 
@@ -476,13 +487,14 @@
         act[at(s, geo.small), :] = jnp.concatenate(parts, axis=0).astype(BF16)
 
     loop(geo.slabs, slab)
+    net.side.step()
     half, step = weight.shape[0] // 2, 256
 
     def pick(c):
         return weight[c : c + step, :]
 
     small_product(geo, act, pick, step, conv, acc, 0, half)
-    net.side.middle()
+    net.side.step()
     small_product(geo, act, pick, step, conv, acc, half, 2 * half)
     net.side.end()
     finish(net.own, acc, 4)
@@ -560,7 +572,6 @@
     finish(net.own, acc, 6)
     net.begin()
     finish(pooled_sums, acc, 2, 6)
-    net.middle()
     net.end()
 
 
@@ -623,12 +634,16 @@
     for c in range(0, width, block):
         cols = slice(c, c + block)
         put_pieces(wgrad_s, c, tn(dzs[:, cols], sub[...]))
-    net.side.middle()
-    net.middle()
+        if c == width // 4:
+            net.step()
+    net.step()
     net.turn(1)
     for c in range(0, width, block):
         cols = slice(c, c + block)
         put_pieces(wgrad_f, c, tn(dzf[:, cols], act[...]))
+        if c == width // 4:
+            net.side.step()
+    net.side.step()
     net.turn(2)
     for c in range(0, sub.shape[1], block):
         cols = slice(c, c + block)
@@ -641,12 +656,11 @@
     geo, net, live, count, ze, stats_e, norm_e, back_e, sums_e, zd, stats_d, norm_d, weight_0, weight_1,
     weight_2, wgrad, back_d, ngrad, full, taps, dze, moved, parity, acc,
 ):
-    net.open()
     acc[...] = jnp.zeros(acc.shape, F32)
     width = ze.shape[1]
     terms_e = backward_terms(geo, count, stats_e, norm_e, sums_e, ngrad, width, True)
     terms_d = forward_terms(geo, count, stats_d, norm_d, width)
-    gather_taps(geo, live, zd, terms_d, full, taps)
+    gather_taps(geo, net, live, zd, terms_d, full, taps)
 
     def shift(s):
         value = small_back(geo, live, s, back_e, ze, terms_e, width, slice(0, width)).astype(F32)
@@ -703,9 +717,11 @@
     loop(geo.slabs, slab)
     finish(net.own, acc, 4)
     net.begin()
-    grads(0, 4)
-    net.middle()
-    grads(4, 9)
+    grads(0, 3)
+    net.step()
+    grads(3, 6)
+    net.step()
+    grads(6, 9)
     net.end()
 
 
@@ -727,8 +743,6 @@
     width = zc.shape[1]
     terms_d = backward_terms(geo, count, stats_d, norm_d, sums_d, ngrad, zd.shape[1])
     terms_c = forward_terms(geo, count, stats_c, norm_c, width)
-
-    net.open()
 
     def slab(s):
         wide_back(geo, live, s, back_d, zd, terms_d, dzd)
@@ -749,18 +763,18 @@
             acc[2 * group] += fold(piece)
             acc[2 * group + 1] += fold(piece * value)
 
-    third = geo.slabs // 3
-    loop(third, slab)
+    loop(1, slab)
+    net.open()
+    loop(4, lambda s: slab(s + 1))
     net.turn(1)
-    loop(geo.slabs - third, lambda s: slab(s + third))
+    loop(geo.slabs - 5, lambda s: slab(s + 5))
     net.turn(2)
     finish(net.own, acc, 4)
     block = 256
     net.begin()
     for c in range(0, dzd.shape[1], block):
         put_pieces(wgrad, c, tn(dzd[:, c : c + block], hid[...]))
-        if c == 0:
-            net.middle()
+        net.step()
     net.end()
 
 
@@ -772,8 +786,6 @@
     terms_c = backward_terms(geo, count, stats_c, norm_c, sums_c, ngrad, zc.shape[1])
     terms_b = forward_terms(geo, count, stats_b, norm_b, zb.shape[1])
     width = zb.shape[1]
-
-    net.open()
 
     def slab(s):
         wide_back(geo, live, s, joined, zc, terms_c, dzc)
@@ -793,17 +805,17 @@
             acc[2 * group] += fold(piece)
             acc[2 * group + 1] += fold(piece * value)
 
-    half = geo.slabs // 2
-    loop(half, slab)
-    net.turn(1)
-    loop(geo.slabs - half, lambda s: slab(s + half))
+    loop(1, slab)
+    net.open()
+    loop(geo.slabs - 1, lambda s: slab(s + 1))
     net.turn(2)
     finish(net.own, acc, 4)
     net.begin()
-    half = dzc.shape[1] // 2
-    put_pieces(wgrad, 0, tn(dzc[:, 0:half], act[...]))
-    net.middle()
-    put_pieces(wgrad, half, tn(dzc[:, half:], act[...]))
+    block = 256
+    for c in range(0, dzc.shape[1], block):
+        put_pieces(wgrad, c, tn(dzc[:, c : c + block], act[...]))
+        if c < 2 * block:
+            net.step()
     net.end()
 
 
@@ -831,8 +843,9 @@
             values.append((value + constant) * (geo.mask(size, group, width) * keep))
         spread_taps(geo, dtaps, s, values, True)
 
+    loop(2, fill)
     net.open()
-    loop(geo.slabs, fill)
+    loop(geo.slabs - 2, lambda s: fill(s + 2))
     net.turn(1)
     span = geo.halo - CELLS
     total[...] = jnp.zeros(total.shape, F32)
@@ -867,11 +880,13 @@
     loop(geo.slabs, slab)
     net.turn(2)
     finish(net.own, acc, 4)
-    half = geo.slabs // 2
+    part = geo.slabs // 3
     net.begin()
-    loop(half, grads)
-    net.middle()
-    loop(geo.slabs - half, lambda s: grads(s + half))
+    loop(part, grads)
+    net.step()
+    loop(part, lambda s: grads(s + part))
+    net.step()
+    loop(geo.slabs - 2 * part, lambda s: grads(s + 2 * part))
     put_pieces(wgrad, 0, total[...])
     net.end()
 
@@ -952,49 +967,82 @@
     return outs[:4], [item if turn else item.T for turn, item in zip(upright, outs[4:])]
 
 
+class Group:
+    def __init__(self, kind, reps, shards):
+        rep, shard = lax.axis_index("rep"), lax.axis_index("fsdp")
+        chip, core = shard // 2, lax.rem(shard, 2)
+        wide = reps // 2
+        low, high = lax.rem(rep, 2), rep // wide
+        first = core == 0
+        if kind == "core":
+            self.size, self.me = 2, core
+            self.address = lambda k: {"fsdp": chip * 2 + k}
+        elif kind == "chips":
+            self.size, self.me = shards // 2, chip
+            self.address = lambda k: {"fsdp": k * 2 + core}
+        elif kind == "shards":
+            self.size, self.me = shards, shard
+            self.address = lambda k: {"fsdp": k}
+        elif kind == "reps":
+            self.size, self.me = reps, rep
+            self.address = lambda k: {"rep": k}
+        elif kind == "near":
+            self.size, self.me = 2, jnp.where(first, low, high)
+            self.address = lambda k: {
+                "rep": jnp.where(first, rep - low + k, rep - high * wide + k * wide)
+            }
+        else:
+            self.size = wide
+            self.me = jnp.where(first, rep // 2, lax.rem(rep, wide))
+            self.address = lambda k: {"rep": jnp.where(first, k * 2 + low, high * wide + k)}
+
+    def other(self, hop):
+        return lax.rem(self.me + hop, self.size)
+
+
 class Sums:
-    def __init__(self, reps, shards, own, out, first, second, sems):
-        self.reps, self.shards = reps, shards
-        self.own, self.out, self.first, self.second = own, out, first, second
-        self.sems = sems
-        self.rep, self.shard = lax.axis_index("rep"), lax.axis_index("fsdp")
+    def __init__(self, reps, shards, own, out, buffers, sems):
+        self.own, self.out, self.buffers, self.sems = own, out, buffers, sems
+        self.groups = [Group(kind, reps, shards) for kind in ("core", "chips", "reps")]
+        self.phase = 0
         self.copies = []
 
-    def begin(self):
+    def send(self, source):
+        group, buffer = self.groups[self.phase], self.buffers[self.phase]
         self.copies = []
-        for hop in range(1, self.shards):
+        for hop in range(1, group.size):
             copy = pltpu.make_async_remote_copy(
-                self.own, self.first.at[self.shard], self.sems[0].at[hop], self.sems[1].at[hop],
-                device_id={"fsdp": lax.rem(self.shard + hop, self.shards)}, device_id_type=MESH,
+                source, buffer.at[group.me], self.sems[2 * self.phase].at[hop],
+                self.sems[2 * self.phase + 1].at[hop], device_id=group.address(group.other(hop)),
+                device_id_type=MESH,
             )
             copy.start()
             self.copies.append(copy)
-        self.first[self.shard] = self.own[...]
-
-    def middle(self):
+
+    def begin(self):
+        self.send(self.own)
+        self.buffers[0][self.groups[0].me] = self.own[...]
+
+    def total(self):
         for copy in self.copies:
             copy.wait()
-        total = self.first[0]
-        for k in range(1, self.shards):
-            total = total + self.first[k]
-        self.second[self.rep] = total
-        self.copies = []
-        for hop in range(1, self.reps):
-            place = self.second.at[self.rep]
-            copy = pltpu.make_async_remote_copy(
-                place, place, self.sems[2].at[hop], self.sems[3].at[hop],
-                device_id={"rep": lax.rem(self.rep + hop, self.reps)}, device_id_type=MESH,
-            )
-            copy.start()
-            self.copies.append(copy)
+        buffer = self.buffers[self.phase]
+        total = buffer[0]
+        for k in range(1, self.groups[self.phase].size):
+            total = total + buffer[k]
+        return total
+
+    def step(self):
+        total = self.total()
+        self.phase += 1
+        group, buffer = self.groups[self.phase], self.buffers[self.phase]
+        buffer[group.me] = total
+        self.send(buffer.at[group.me])
 
     def end(self):
-        for copy in self.copies:
-            copy.wait()
-        total = self.second[0]
-        for k in range(1, self.reps):
-            total = total + self.second[k]
-        self.out[...] = total
+        while self.phase < 2:
+            self.step()
+        self.out[...] = self.total()
 
 
 class Net:
@@ -1042,8 +1090,8 @@
         self.open()
         self.sums.begin()
 
-    def middle(self):
-        self.sums.middle()
+    def step(self):
+        self.sums.step()
 
     def end(self):
         self.sums.end()
@@ -1051,7 +1099,6 @@
 
     def run(self):
         self.begin()
-        self.middle()
         self.end()
 
     def close(self):
@@ -1061,88 +1108,71 @@
 
 
 class Job:
+    GROUPS = {
+        "pair": "core", "join": "core", "line": "chips", "spread": "chips", "all": "shards",
+        "share": "reps", "half": "near", "near": "near", "rest": "others", "others": "others",
+    }
+
     def __init__(self, kind, reps, shards, sources, out, held, send, recv):
-        self.kind, self.source, self.out, self.held = kind, sources[0], out, held
-        self.sources = sources
+        self.kind, self.sources, self.out, self.held = kind, sources, out, held
         self.send, self.recv = send, recv
         self.reps, self.chips = reps, shards // 2
         self.rep, shard = lax.axis_index("rep"), lax.axis_index("fsdp")
         self.chip, self.core = shard // 2, lax.rem(shard, 2)
-        if kind in ("pair", "join"):
-            self.members, self.me = 2, self.core
-            self.address = lambda k: {"fsdp": self.chip * 2 + k}
-        elif kind in ("line", "spread"):
-            self.members, self.me = self.chips, self.chip
-            self.address = lambda k: {"fsdp": k * 2 + self.core}
-        elif kind == "all":
-            self.members, self.me = shards, shard
-            self.address = lambda k: {"fsdp": k}
-        elif kind == "half":
-            wide = reps // 2
-            even = lax.rem(self.rep, 2) == 0
-            self.members, self.me = 2, 0
-            aside = jnp.where(even, self.rep + 1, self.rep - 1)
-            across = lax.rem(self.rep + wide, reps)
-            self.address = lambda k: {"rep": jnp.where(self.core == 0, aside, across)}
-        elif kind == "rest":
-            wide = reps // 2
-            low, high = lax.rem(self.rep, 2), self.rep // wide
-            first = self.core == 0
-            self.members = wide
-            self.me = jnp.where(first, self.rep // 2, lax.rem(self.rep, wide))
-            self.address = lambda k: {"rep": jnp.where(first, k * 2 + low, high * wide + k)}
-        else:
-            self.members, self.me = reps, self.rep
-            self.address = lambda k: {"rep": k}
+        self.group = Group(self.GROUPS[kind], reps, shards)
 
     def give(self, source, target, hop):
-        other = lax.rem(self.me + hop, self.members)
         k = len(self.copies)
         if hop == 0:
             copy = pltpu.make_async_copy(source, target, self.send.at[k])
         else:
             copy = pltpu.make_async_remote_copy(
                 source, target, self.send.at[k], self.recv.at[k],
-                device_id=self.address(other), device_id_type=MESH,
+                device_id=self.group.address(self.group.other(hop)), device_id_type=MESH,
             )
         copy.start()
         self.copies.append(copy)
 
     def start(self):
         self.copies = []
-        kind, out = self.kind, self.out
-        order = list(range(1, self.members)) + [0]
+        kind, out, source, group = self.kind, self.out, self.sources[0], self.group
+        order = list(range(1, group.size)) + [0]
+        wide = self.reps // 2
+        first = self.core == 0
         if kind == "spread":
+            for hop in order[:-1]:
+                self.give(source.at[self.rep], out.at[group.size - hop - 1], hop)
+        elif kind == "near":
+            self.give(source, out, 1)
+        elif kind == "others":
+            low, high = lax.rem(self.rep, 2), self.rep // wide
+            partner = jnp.where(
+                first, self.rep + 1 - 2 * low, self.rep + (1 - 2 * high) * wide
+            )
             for hop in order:
-                self.give(self.source.at[self.rep], out.at[self.chip], hop)
-        elif kind == "fan":
+                self.give(source, out.at[self.rep], hop)
+                self.give(self.sources[1], out.at[partner], hop)
+        elif kind == "join":
             for hop in order:
                 for step in range(1, self.chips):
                     chip = lax.rem(self.chip + step, self.chips)
-                    self.give(self.source.at[chip], out.at[chip, self.rep], hop)
-            self.give(self.sources[1], out.at[self.chip], 0)
-        elif kind == "join":
-            for hop in order:
-                for chip in range(self.chips):
-                    self.give(self.source.at[chip], out.at[chip, self.core], hop)
+                    self.give(source.at[:, step - 1], out.at[chip, self.core], hop)
+                self.give(self.sources[1], out.at[self.chip, self.core], hop)
         elif kind in ("all", "share"):
             for hop in order:
-                self.give(self.source, out.at[self.me], hop)
+                self.give(source, out.at[group.me], hop)
         elif kind == "half":
-            wide = self.reps // 2
-            first = self.core == 0
             low, high = lax.rem(self.rep, 2), self.rep // wide
             mine = jnp.where(first, low, high * wide)
             theirs = jnp.where(first, 1 - low, (1 - high) * wide)
             step = jnp.where(first, 2, 1)
             for k in range(wide):
-                self.give(self.source.at[theirs + k * step], self.held.at[1, k], 1)
+                self.give(source.at[theirs + k * step], self.held.at[1, k], 1)
             for k in range(wide):
-                self.give(self.source.at[mine + k * step], self.held.at[0, k], 0)
+                self.give(source.at[mine + k * step], self.held.at[0, k], 0)
         else:
             for hop in order:
-                other = lax.rem(self.me + hop, self.members)
-                self.give(self.source.at[other], self.held.at[self.me], hop)
+                self.give(source.at[group.other(hop)], self.held.at[group.me], hop)
 
     def finish(self):
         for copy in self.copies:
@@ -1150,6 +1180,7 @@
         held, out = self.held, self.out
         if held is None:
             return
+        members = held.shape[0]
         blocks = held.shape[1:-2]
 
         def one(index):
@@ -1157,7 +1188,7 @@
                 (index,) if blocks else ()
             )
             total = held[(0,) + place].astype(F32)
-            for k in range(1, self.members):
+            for k in range(1, members):
                 total = total + held[(k,) + place].astype(F32)
             out[place[::-1] if self.kind == "pair" else place] = total.astype(BF16)
 
@@ -1165,7 +1196,7 @@
             loop(blocks[0] * (blocks[1] if len(blocks) == 2 else 1), one)
         else:
             total = held[0].astype(F32)
-            for k in range(1, self.members):
+            for k in range(1, members):
                 total = total + held[k].astype(F32)
             out[...] = total.astype(BF16)
 
@@ -1173,11 +1204,13 @@
 def job_shapes(kind, reps, shards, shape):
     chips = shards // 2
     if kind == "spread":
-        return None, (chips,) + shape[1:], chips
-    if kind == "fan":
-        return None, (chips, reps) + shape[1:], reps * (chips - 1) + 1
+        return None, (chips - 1,) + shape[1:], chips
+    if kind == "near":
+        return None, shape, 1
+    if kind == "others":
+        return None, (reps,) + shape, reps
     if kind == "join":
-        return None, (chips, 2) + shape[1:], 2 * chips
+        return None, (chips, 2, reps) + shape[2:], 2 * chips
     if kind == "all":
         return None, (shards,) + shape, shards
     if kind == "pair":
@@ -1190,18 +1223,16 @@
 
 
 VMEM_CAP = 60 << 20
-FAR = ("spread", "fan")
+FAR = ("spread", "near", "others")
 
 
 def sums_scratch(reps, shards, shape, own):
-    return [pltpu.VMEM(shape, F32)] * own + [
-        pltpu.VMEM((shards,) + shape, F32),
-        pltpu.VMEM((reps,) + shape, F32),
-        pltpu.SemaphoreType.DMA((shards,)),
-        pltpu.SemaphoreType.DMA((shards,)),
-        pltpu.SemaphoreType.DMA((reps,)),
-        pltpu.SemaphoreType.DMA((reps,)),
-    ]
+    sizes = (2, shards // 2, reps)
+    return (
+        [pltpu.VMEM(shape, F32)] * own
+        + [pltpu.VMEM((size,) + shape, F32) for size in sizes]
+        + [pltpu.SemaphoreType.DMA((size,)) for size in sizes for unused in range(2)]
+    )
 
 
 def run(name, kernel, geo, reps, shards, number, live, operands, results, scratch, sums, jobs, side, far=()):
@@ -1262,11 +1293,11 @@
         beside, main = None, None
         place = own_results + len(jobs)
         if side is not None:
-            beside = Sums(reps, shards, refs[near + 1], outs[place], more[0], more[1], more[2:6])
-            more = more[6:]
+            beside = Sums(reps, shards, refs[near + 1], outs[place], more[0:3], more[3:9])
+            more = more[9:]
         if sums is not None:
-            main = Sums(reps, shards, more[0], outs[-1], more[1], more[2], more[3:7])
-            more = more[7:]
+            main = Sums(reps, shards, more[0], outs[-1], more[1:4], more[4:10])
+            more = more[10:]
         net = None
         if remote:
             plans = [job[2:] for job in jobs]
@@ -1353,10 +1384,7 @@
     def both(width):
         return ((2, width), F32)
 
-    (
-        packed, za, spread_a, fan_a, wa, spread_b, fan_b, wb, norms, unused, unused, wc,
-        unused, fan_d, spread_e0, spread_e1, sa,
-    ) = go(
+    more = go(
         "stage_a", stage_a, (global_views, local_views),
         [((big, channels), BF16), ((big, mid_1), BF16)],
         [
@@ -1365,46 +1393,56 @@
         ],
         mid_1, 8,
         jobs=(
-            ("spread", (ha,), 0, 1), ("fan", (0, ha), 1, 2), ("join", (1,), 2, 3),
-            ("spread", (hb,), 0, 2), ("fan", (3, hb), 2, 4), ("join", (4,), 4, None),
-            ("all", (own_norms(first_norms, second_norms),), 1, 4),
-            ("spread", (hc,), 0, 3), ("fan", (7, hc), 3, 4), ("join", (8,), 4, None),
-            ("spread", (hd,), 0, 3), ("fan", (10, hd), 3, 4),
-            ("spread", (he_0,), 3, 4), ("spread", (he_1,), 3, 4),
+            ("spread", (ha,), 0, 1), ("near", (0,), 1, 2), ("others", (0, 1), 2, 3),
+            ("join", (2, ha), 3, 4),
+            ("spread", (hb,), 0, 2), ("near", (4,), 2, 3), ("others", (4, 5), 3, 5),
+            ("join", (6, hb), 5, None),
+            ("spread", (hc,), 0, 3), ("near", (8,), 3, 5), ("others", (8, 9), 5, None),
+            ("spread", (hd,), 0, 3), ("near", (11,), 3, 5), ("others", (11, 12), 5, None),
+            ("all", (own_norms(first_norms, second_norms),), 1, 5),
+            ("spread", (he_0,), 3, 5), ("spread", (he_1,), 3, 5),
         ),
         far=(0, 1),
     )
-    count = sa
-    wa, wb, wc = rows_of(wa), rows_of(wb), rows_of(wc)
+    packed, za, wa, wb = more[0], more[1], more[2 + 3], more[2 + 7]
+    far_c, far_d, norms, spread_e0, spread_e1 = (more[2 + k] for k in (10, 13, 14, 15, 16))
+    sa = count = more[-1]
+    wa, wb = rows_of(wa), rows_of(wb)
     norms_1, norms_2 = all_norms(norms, first_norms, second_norms)
     na, nb, nc = norms_1[:, :mid_1], norms_1[:, mid_1 : 2 * mid_1], norms_1[:, 2 * mid_1 :]
     nd, ne = norms_2[:, :mid_2], norms_2[:, mid_2 : 2 * mid_2]
     nf, ns = norms_2[:, 2 * mid_2 : 2 * mid_2 + wide], norms_2[:, 2 * mid_2 + wide :]
-    zb, wd, fan_e0, fan_e1, spread_e2, spread_s, sb = go(
+    zb, wc, wd, unused, far_e0, unused, far_e1, spread_e2, spread_f, sb = go(
         "stage_b", stage_b, (count, za, sa, na, wb), [((big, mid_1), BF16)],
         [((geo.halo_total, 3 * mid_1), BF16), acc(mid_1)], mid_1,
         jobs=(
-            ("join", (fan_d,), 0, 2), ("fan", (spread_e0, he_0), 0, 2),
-            ("fan", (spread_e1, he_1), 0, 2), ("spread", (he_2,), 0, 2), ("spread", (hs,), 0, 2),
+            ("join", (far_c, hc), 0, 2), ("join", (far_d, hd), 0, 2),
+            ("near", (spread_e0,), 0, 1), ("others", (spread_e0, 2), 1, 2),
+            ("near", (spread_e1,), 0, 1), ("others", (spread_e1, 4), 1, 2),
+            ("spread", (he_2,), 0, 2), ("spread", (hf,), 0, 2),
         ),
     )
-    zc, we_0, we_1, fan_e2, spread_f, sc = go(
+    wc = rows_of(wc)
+    zc, we_0, we_1, unused, far_e2, spread_s, sc = go(
         "stage_c", stage_c, (count, zb, sb, nb, wc), [((big, channels), BF16)],
         [((geo.rows, mid_1), BF16), acc(channels)], channels,
         jobs=(
-            ("join", (fan_e0,), 0, 2), ("join", (fan_e1,), 0, 2),
-            ("fan", (spread_e2, he_2), 0, 2), ("spread", (hf,), 0, 2),
+            ("join", (far_e0, he_0), 0, 2), ("join", (far_e1, he_1), 0, 2),
+            ("near", (spread_e2,), 0, 1), ("others", (spread_e2, 2), 1, 2), ("spread", (hs,), 0, 2),
         ),
     )
     wd = rows_of(wd)
-    hid, zd, sub, we_2, fan_s, sd = go(
+    hid, zd, sub, we_2, unused, far_s, near_f, sd = go(
         "stage_d", stage_d, (count, zc, sc, nc, packed, wd),
         [((big, channels), BF16), ((big, mid_2), BF16), ((small, channels), BF16)],
         [((channels // 128, geo.rows, 128), F32), acc(mid_2)], mid_2,
-        jobs=(("join", (fan_e2,), 0, 2), ("fan", (spread_s, hs), 0, 2)),
+        jobs=(
+            ("join", (far_e2, he_2), 0, 2), ("near", (spread_s,), 0, 1),
+            ("others", (spread_s, 1), 1, 2), ("near", (spread_f,), 1, 2),
+        ),
     )
     we = tuple(rows_of(item) for item in (we_0, we_1, we_2))
-    ze, zs, local_s, ws, fan_f, wf, se = go(
+    ze, zs, local_s, ws, unused, wf, se = go(
         "stage_e", stage_e, (count, zd, sd, nd, *we, sub),
         [((small, mid_2), BF16), ((small, wide), BF16), stat(wide // 2)],
         [
@@ -1412,7 +1450,8 @@
         ],
         mid_2,
         jobs=(
-            ("join", (fan_s,), 0, 2), ("fan", (spread_f, hf), 0, 2), ("join", (1,), 2, None),
+            ("join", (far_s, hs), 0, 2), ("others", (spread_f, near_f), 0, 2),
+            ("join", (1, hf), 2, None),
         ),
     )
     wf, ws = rows_of(wf), rows_of(ws)

time: 529 us -> 526 us (level)
  Pallas kernels: 489 us -> 483 us
    pallas_call x13, Pallas kernels: 470 us -> 465 us  [run(): pl.pallas_call(whole, out_shape=[jax.ShapeDtypeStruct(shape, dtype) for s...]
    unnamed x38 -> x36, local copies, waits for them, and re-layouts: 16.9 us -> 16.9 us
where the time goes in v4:
time: 526 us; the launch traced here: 517 us
  Pallas kernels  483 us (92%)
  local copies, waits for them, and re-layouts  26.7 us (5%)
    pallas_call x13, Pallas kernels, run(): pl.pallas_call(whole, out_shape=[jax.ShapeDtypeStruct(shape, dtype) for s...  465 us
    pallas_call x1, Pallas kernels, run_last(): pl.pallas_call(functools.partial(last_kernel, geo, upright), grid=(geo.sl...  18.1 us
    unnamed x36, local copies, waits for them, and re-layouts  16.9 us

profile of v4, /device:TPU:0, one launch (start us, length us, event | category | flops | bytes accessed | tf_op | source)
XLA Modules:
  0.0 517.5 jit_solution(10050152884735397414)
XLA Ops:
  1.3 1.9 fusion.10
  3.2 0.0 copy-start.11
  3.2 0.0 copy-start.13
  3.2 1.6 copy.38
  4.8 3.6 copy.39.refs_2_
  8.4 0.0 copy-done.11
  8.4 0.0 copy-done.13
  8.4 0.1 reshape.117
  8.5 0.6 reshape.139.refs_9_
  9.1 0.0 copy-start.5
  9.1 41.7 %stage_a.1 = (bf16[3200,1024]{1,0:T(8,128)(2,1)}, bf16[3200,256]{1,0:T(8,128)(2,1)}, bf16[3,8,1024]{2,1,0:T(8,128)(2,1)}, bf16[3,8,1024]{2,1,0:T(8,128)(2,1)}, b...) custom-call(s32[1]{0:T(128)S(6)} %copy.50.refs_0_, ...), custom_call_target="tpu_custom_call" | custom-call | tf_op jit(solution)/shard_map/stage_a/pallas_call | solution.py:1309
  50.8 0.9 copy.47
  51.7 0.1 reshape.123
  51.8 0.1 reshape.124
  51.9 0.6 fusion.13
  52.5 0.0 copy-done.5
  52.5 0.8 copy.41
  53.3 0.0 copy-start.4
  53.3 40.0 %stage_b.1 = (bf16[3200,256]{1,0:T(8,128)(2,1)}, bf16[4,2,4,32,256]{4,3,2,1,0:T(8,128)(2,1)}, bf16[4,2,4,16,1024]{4,3,2,1,0:T(8,128)(2,1)}, bf16[3,16,1536]{2,1,...) custom-call(s32[1]{0:T(128)S(6)} %copy.50.refs_0_, ...), custom_call_target="tpu_custom_call" | custom-call | tf_op jit(solution)/shard_map/stage_b/pallas_call | solution.py:1309
  93.3 0.0 copy-done.4
  93.3 1.0 copy.42
  94.3 30.6 %stage_c.1 = (bf16[3200,1024]{1,0:T(8,128)(2,1)}, bf16[4,2,4,16,1536]{4,3,2,1,0:T(8,128)(2,1)}, bf16[4,2,4,16,1536]{4,3,2,1,0:T(8,128)(2,1)}, bf16[3,16,1536]{2,...) custom-call(s32[1]{0:T(128)S(6)} %copy.50.refs_0_, ...), custom_call_target="tpu_custom_call" | custom-call | tf_op jit(solution)/shard_map/stage_c/pallas_call | solution.py:1309
  124.9 0.6 slice.68.refs_4_.refs_11_
  125.5 51.8 %stage_d.1 = (bf16[3200,1024]{1,0:T(8,128)(2,1)}, bf16[3200,512]{1,0:T(8,128)(2,1)}, bf16[800,1024]{1,0:T(8,128)(2,1)}, bf16[4,2,4,16,1536]{4,3,2,1,0:T(8,128)(2...) custom-call(s32[1]{0:T(128)S(6)} %copy.50.refs_0_, ...), custom_call_target="tpu_custom_call" | custom-call | tf_op jit(solution)/shard_map/stage_d/pallas_call | solution.py:1309
  177.3 0.6 fusion.12
  177.9 31.1 %stage_e.1 = (bf16[800,512]{1,0:T(8,128)(2,1)}, bf16[800,2048]{1,0:T(8,128)(2,1)}, f32[8,1024]{1,0:T(8,128)}, bf16[4,2,4,64,1024]{4,3,2,1,0:T(8,128)(2,1)}, bf16...) custom-call(s32[1]{0:T(128)S(6)} %copy.50.refs_0_, ...), custom_call_target="tpu_custom_call" | custom-call | tf_op jit(solution)/shard_map/stage_e/pallas_call | solution.py:1309
  209.1 0.0 copy-start.3
  209.1 25.5 %stage_f.1 = (bf16[800,512]{1,0:T(8,128)(2,1)}, bf16[800,2048]{1,0:T(8,128)(2,1)}, f32[8,1024]{1,0:T(8,128)}, f32[8,1024]{1,0:T(8,128)}) custom-call(s32[1]{0:T(128)S(6)} %copy.50.refs_0_, f32[16,128]{1,0:T(8,128)} %get-tuple-element.118.refs_1_.refs_3_.refs_8_, bf16[800,512]{1,0:T(8,128)(2,1)} %get-tuple-element.147.refs_2_.refs_14_, ...), custom_call_target="tpu_custom_call" | custom-call | tf_op jit(solution)/shard_map/stage_f/pallas_call | solution.py:1309
  234.5 0.6 fusion.11
  235.2 0.0 copy-done.3
  235.2 1.6 copy.43.refs_9_
  236.7 26.5 %stage_out.1 = (bf16[10,7,7,2048]{3,2,1,0:T(8,128)(2,1)}, bf16[20,3,3,2048]{3,2,1,0:T(4,128)(2,1)}, bf16[800,2048]{1,0:T(8,128)(2,1)}, f32[8,512]{1,0:T(8,128)}, f32[24,512]{1,0:T(8,128)}) custom-call(s32[1]{0:T(128)S(6)} %copy.50.refs_0_, f32[16,128]{1,0:T(8,128)} %get-tuple-element.118.refs_1_.refs_3_.refs_8_, ...), custom_call_target="tpu_custom_call" | custom-call | tf_op jit(solution)/shard_map/stage_out/pallas_call | solution.py:1309
  263.3 33.4 %stage_f_back.1 = (bf16[2,4,4,64,512]{4,3,2,1,0:T(8,128)(2,1)}, bf16[2,4,4,64,1024]{4,3,2,1,0:T(8,128)(2,1)}, bf16[800,1024]{1,0:T(8,128)(2,1)}, bf16[800,512]{1...) custom-call(s32[1]{0:T(128)S(6)} %copy.50.refs_0_, ...), custom_call_target="tpu_custom_call" | custom-call | tf_op jit(solution)/shard_map/stage_f_back/pallas_call | solution.py:1309
  296.7 31.9 %stage_e_back.1 = (bf16[2,4,4,16,4608]{4,3,2,1,0:T(8,128)(2,1)}, bf16[3200,512]{1,0:T(8,128)(2,1)}, f32[2,512]{1,0:T(2,128)}, bf16[2,4,64,512]{3,2,1,0:T(8,128)(...) custom-call(s32[1]{0:T(128)S(6)} %copy.50.refs_0_, f32[16,128]{1,0:T(8,128)} %get-tuple-element.118.refs_1_.refs_3_.refs_8_, ...), custom_call_target="tpu_custom_call" | custom-call | tf_op jit(solution)/shard_map/stage_e_back/pallas_call | solution.py:1309
  328.6 0.0 copy-start.6
  328.6 0.0 copy-start.7
  328.6 0.0 copy-start.10
  328.6 43.5 %stage_d_back.1 = (bf16[2,4,4,16,1024]{4,3,2,1,0:T(8,128)(2,1)}, bf16[3200,1024]{1,0:T(8,128)(2,1)}, f32[2,512]{1,0:T(2,128)}, bf16[4,4,16,4608]{3,2,1,0:T(8,128...) custom-call(s32[1]{0:T(128)S(6)} %copy.50.refs_0_, ...), custom_call_target="tpu_custom_call" | custom-call | tf_op jit(solution)/shard_map/stage_d_back/pallas_call | solution.py:1309
  372.1 0.0 copy-done.6
  372.1 0.0 copy-done.7
  372.2 0.0 copy-done.10
  372.2 1.3 fusion.5
  373.5 36.1 %stage_c_back.1 = (bf16[2,4,4,32,256]{4,3,2,1,0:T(8,128)(2,1)}, bf16[3200,256]{1,0:T(8,128)(2,1)}, f32[2,1024]{1,0:T(2,128)}, bf16[4,4,16,1024]{3,2,1,0:T(8,128)...) custom-call(s32[1]{0:T(128)S(6)} %copy.50.refs_0_, ...), custom_call_target="tpu_custom_call" | custom-call | tf_op jit(solution)/shard_map/stage_c_back/pallas_call | solution.py:1309
  409.6 33.1 %stage_b_back.1 = (bf16[2,4,4,8,2304]{4,3,2,1,0:T(8,128)(2,1)}, bf16[3200,256]{1,0:T(8,128)(2,1)}, f32[2,256]{1,0:T(2,128)}, bf16[2,4,16,1024]{3,2,1,0:T(8,128)(...) custom-call(s32[1]{0:T(128)S(6)} %copy.50.refs_0_, ...), custom_call_target="tpu_custom_call" | custom-call | tf_op jit(solution)/shard_map/stage_b_back/pallas_call | solution.py:1309
  442.7 0.0 copy-start.9
  442.7 0.0 copy-start.12
  442.7 39.8 %stage_a_back.1 = (bf16[2,4,4,8,1024]{4,3,2,1,0:T(8,128)(2,1)}, bf16[3200,256]{1,0:T(8,128)(2,1)}, f32[2,256]{1,0:T(2,128)}, bf16[4,4,8,2304]{3,2,1,0:T(8,128)(2...) custom-call(s32[1]{0:T(128)S(6)} %copy.50.refs_0_, ...), custom_call_target="tpu_custom_call" | custom-call | tf_op jit(solution)/shard_map/stage_a_back/pallas_call | solution.py:1309
  482.6 0.0 copy-done.9
  482.6 0.0 copy-done.12
  482.6 1.3 fusion.9
  483.9 18.1 %last.1 = (f32[10,14,14,1024]{3,2,1,0:T(8,128)}, f32[20,6,6,1024]{3,2,1,0:T(8,128)}, bf16[10,14,14,1024]{3,2,1,0:T(8,128)(2,1)}, bf16[20,6,6,1024]{3,2,1,0:T(8,1...) custom-call(bf16[3200,1024]{1,0:T(8,128)(2,1)} %get-tuple-element.17, ...), custom_call_target="tpu_custom_call" | custom-call | tf_op jit(solution)/shard_map/last/pallas_call | solution.py:949
  502.0 0.0 copy-start.1
  502.0 5.8 %copy.46 = f32[20,6,6,1024]{3,0,2,1:T(8,128)} copy(f32[20,6,6,1024]{3,2,1,0:T(8,128)} %get-tuple-element.241) | data formatting | bytes 5898240
  507.9 0.0 copy-start.8
  507.9 0.0 copy-start.2
  507.9 0.0 copy-done.1
  507.9 2.1 copy.44
  509.9 1.2 slice.60
  511.8 0.0 copy-done.8
  511.8 0.6 sqrt_reduce_fusion
  513.0 0.0 copy-done.2
  513.1 1.5 copy.45
  514.5 0.0 copy-done
  514.5 1.4 copy.51
  (7 shorter events, 0.1 us)
Async XLA Ops:
  3.2 5.2 %copy-start.11 = (bf16[2,640]{1,0:T(2,128)(2,1)S(1)}, bf16[2,640]{1,0:T(2,128)(2,1)}, u32[]{:S(2)}) copy-start(bf16[2,640]{1,0:T(2,128)(2,1)} %param.25) | copy-start | bytes 7684
  3.2 5.2 %copy-start.13 = (bf16[2,192]{1,0:T(2,128)(2,1)S(1)}, bf16[2,192]{1,0:T(2,128)(2,1)}, u32[]{:S(2)}) copy-start(bf16[2,192]{1,0:T(2,128)(2,1)} %param.20) | copy-start | bytes 2308
  9.1 43.3 %copy-start.5 = (bf16[512,256]{1,0:T(8,128)(2,1)S(1)}, bf16[512,256]{1,0:T(8,128)(2,1)}, u32[]{:S(2)}) copy-start(bf16[512,256]{1,0:T(8,128)(2,1)} %param.23) | copy-start | bytes 786436
  53.3 40.0 %copy-start.4 = (bf16[1024,256]{1,0:T(8,128)(2,1)S(1)}, bf16[1024,256]{1,0:T(8,128)(2,1)}, u32[]{:S(2)}) copy-start(bf16[1024,256]{1,0:T(8,128)(2,1)} %param.24) | copy-start | bytes 1572868
  209.1 26.1 %copy-start.3 = (bf16[20,3,3,2048]{3,0,2,1:T(8,128)(2,1)S(1)}, bf16[20,3,3,2048]{3,0,2,1:T(8,128)(2,1)}, u32[]{:S(2)}) copy-start(bf16[20,3,3,2048]{3,0,2,1:T(8,128)(2,1)} %param.27) | copy-start | bytes 2211844
  328.6 43.6 %copy-start.6 = (f32[2,2048]{1,0:T(2,128)S(1)}, f32[2,2048]{1,0:T(2,128)}, u32[]{:S(2)}) copy-start(f32[2,2048]{1,0:T(2,128)} %get-tuple-element.217) | copy-start | bytes 49156
  328.6 43.6 %copy-start.7 = (f32[2,2048]{1,0:T(2,128)S(1)}, f32[2,2048]{1,0:T(2,128)}, u32[]{:S(2)}) copy-start(f32[2,2048]{1,0:T(2,128)} %get-tuple-element.218) | copy-start | bytes 49156
  328.6 43.6 %copy-start.10 = (f32[2,512]{1,0:T(2,128)S(1)}, f32[2,512]{1,0:T(2,128)}, u32[]{:S(2)}) copy-start(f32[2,512]{1,0:T(2,128)} %get-tuple-element.216) | copy-start | bytes 12292
  442.7 39.8 %copy-start.9 = (f32[2,1024]{1,0:T(2,128)S(1)}, f32[2,1024]{1,0:T(2,128)}, u32[]{:S(2)}) copy-start(f32[2,1024]{1,0:T(2,128)} %get-tuple-element.210) | copy-start | bytes 24580
  442.7 39.8 %copy-start.12 = (f32[2,256]{1,0:T(2,128)S(1)}, f32[2,256]{1,0:T(2,128)}, u32[]{:S(2)}) copy-start(f32[2,256]{1,0:T(2,128)} %get-tuple-element.209) | copy-start | bytes 6148
  502.0 5.9 %copy-start.1 = (bf16[20,6,6,1024]{3,2,1,0:T(8,128)(2,1)S(1)}, bf16[20,6,6,1024]{3,2,1,0:T(8,128)(2,1)}, u32[]{:S(2)}) copy-start(bf16[20,6,6,1024]{3,2,1,0:T(8,128)(2,1)} %get-tuple-element.237) | copy-start | bytes 4423684
  507.9 3.9 copy-start.8
  507.9 5.2 %copy-start.2 = (bf16[20,3,3,2048]{3,2,1,0:T(4,128)(2,1)S(1)}, bf16[20,3,3,2048]{3,2,1,0:T(4,128)(2,1)}, u32[]{:S(2)}) copy-start(bf16[20,3,3,2048]{3,2,1,0:T(4,128)(2,1)} %get-tuple-element.239) | copy-start | bytes 2211844
  507.9 6.7 %copy-start = (bf16[10,7,7,2048]{3,2,1,0:T(8,128)(2,1)S(1)}, bf16[10,7,7,2048]{3,2,1,0:T(8,128)(2,1)}, u32[]{:S(2)}) copy-start(bf16[10,7,7,2048]{3,2,1,0:T(8,128)(2,1)} %get-tuple-element.279) | copy-start | bytes 6021124

commit v5 on v4

--- a/solution.py
+++ b/solution.py
@@ -346,7 +346,8 @@
 
 
 def stage_d(
-    geo, net, live, count, zc, stats_c, norm, packed, weight, hid, conv, sub, full, acc,
+    geo, net, live, count, zc, stats_c, norm, packed, weight, short, hid, conv, sub, conv_s, stats_s,
+    full, acc, acc_s,
 ):
     acc[...] = jnp.zeros(acc.shape, F32)
     width = zc.shape[1]
@@ -377,7 +378,20 @@
     loop(geo.slabs - 5, lambda s: slab(s + 5))
     net.turn(2)
     finish(net.own, acc, 4)
-    net.run()
+    net.begin()
+    acc_s[...] = jnp.zeros(acc_s.shape, F32)
+    wide, step = short.shape[0], 256
+
+    def pick(c):
+        return short[c : c + step, :]
+
+    small_product(geo, sub, pick, step, conv_s, acc_s, 0, wide // 4)
+    net.step()
+    small_product(geo, sub, pick, step, conv_s, acc_s, wide // 4, 5 * wide // 8)
+    net.step()
+    small_product(geo, sub, pick, step, conv_s, acc_s, 5 * wide // 8, wide)
+    finish(stats_s, acc_s, 4)
+    net.end()
 
 
 def small_product(geo, left, pick, step, conv, acc, first, last):
@@ -427,17 +441,19 @@
 
 
 def stage_e(
-    geo, net, live, count, zd, stats_d, norm, weight_0, weight_1, weight_2, sub, conv, conv_s,
-    stats_s, full, taps, acc, acc_s,
+    geo, net, live, count, zd, stats_d, norm, weight_0, weight_1, weight_2, conv, full, taps,
+    acc,
 ):
     acc[...] = jnp.zeros(acc.shape, F32)
-    acc_s[...] = jnp.zeros(acc_s.shape, F32)
     terms = forward_terms(geo, count, stats_d, norm, zd.shape[1])
     gather_taps(geo, net, live, zd, terms, full, taps)
     net.turn(1)
+    net.side.begin()
     step = 256
     third = weight_0.shape[1]
     for c in range(0, weight_0.shape[0], step):
+        if c > 0:
+            net.side.step()
         result = nt(taps[:, 0:third], weight_0[c : c + step, :])
         result = result + nt(taps[:, third : 2 * third], weight_1[c : c + step, :])
         result = result + nt(taps[:, 2 * third :], weight_2[c : c + step, :])
@@ -449,29 +465,14 @@
                 piece = piece * (geo.small_mask(group, step) * keep)
                 acc[2 * group, :, c : c + step] += fold(piece)
                 acc[2 * group + 1, :, c : c + step] += fold(piece * piece)
+    net.side.step()
     net.turn(2)
+    net.side.end()
     finish(net.own, acc, 4)
-    net.begin()
-    short = net.job_out(0)
-    step = short.shape[2] * short.shape[3]
-
-    def pick(c):
-        part = c // step
-        return short[part // 2, part % 2].reshape(step, short.shape[4])
-
-    width = conv_s.shape[1]
-    small_product(geo, sub, pick, step, conv_s, acc_s, 0, width // 4)
-    net.step()
-    small_product(geo, sub, pick, step, conv_s, acc_s, width // 4, 5 * width // 8)
-    net.step()
-    small_product(geo, sub, pick, step, conv_s, acc_s, 5 * width // 8, width)
-    finish(stats_s, acc_s, 4)
-    net.end()
+    net.run()
 
 
 def stage_f(geo, net, live, count, ze, stats_e, norm, weight, act, conv, acc):
-    net.open()
-    net.side.begin()
     acc[...] = jnp.zeros(acc.shape, F32)
     width = ze.shape[1]
     terms = forward_terms(geo, count, stats_e, norm, width, True)
@@ -487,16 +488,14 @@
         act[at(s, geo.small), :] = jnp.concatenate(parts, axis=0).astype(BF16)
 
     loop(geo.slabs, slab)
-    net.side.step()
     half, step = weight.shape[0] // 2, 256
 
     def pick(c):
         return weight[c : c + step, :]
 
     small_product(geo, act, pick, step, conv, acc, 0, half)
-    net.side.step()
+    net.open()
     small_product(geo, act, pick, step, conv, acc, half, 2 * half)
-    net.side.end()
     finish(net.own, acc, 4)
     net.run()
 
@@ -888,27 +887,42 @@
     net.step()
     loop(geo.slabs - 2 * part, lambda s: grads(s + 2 * part))
     put_pieces(wgrad, 0, total[...])
+    net.turn(3)
     net.end()
 
 
 def stage_a_back(
-    geo, net, live, count, za, stats_a, norm_a, back_a, sums_a, packed, wgrad, dza, ngrad,
+    geo, net, live, count, za, stats_a, norm_a, back_a, sums_a, packed, joined, weight, wgrad, grad,
+    ngrad, dza,
 ):
+    terms_a = backward_terms(geo, count, stats_a, norm_a, sums_a, ngrad, za.shape[1])
+    loop(2, lambda s: wide_back(geo, live, s, back_a, za, terms_a, dza))
     net.open()
-    terms_a = backward_terms(geo, count, stats_a, norm_a, sums_a, ngrad, za.shape[1])
-    loop(geo.slabs, lambda s: wide_back(geo, live, s, back_a, za, terms_a, dza))
+    loop(geo.slabs - 2, lambda s: wide_back(geo, live, s + 2, back_a, za, terms_a, dza))
     put_pieces(wgrad, 0, tn(dza[...], packed[...]))
-    for number in range(1, 8):
-        net.turn(number)
+    net.turn(1)
+
+    def slab(s):
+        result = nn(dza[at(s, geo.rows), :], weight[...])
+        rows = at(s, geo.rows)
+        grad[rows, :] = (result + joined[rows, :].astype(F32)).astype(BF16)
+
+    part = geo.slabs // 3
+    for number in range(3):
+        begin = number * part
+        size = part if number < 2 else geo.slabs - begin
+        loop(size, lambda s: slab(s + begin))
+        net.turn(number + 2)
+    net.turn(5)
     net.close()
 
 
-def last_kernel(geo, upright, joined, dza, hid, weight, *refs):
+def last_kernel(geo, upright, grad, hid, *refs):
     count = len(upright)
     rows_in, refs = refs[:count], refs[count:]
     dxg, dxl, outg, outl = refs[:4]
     targets = refs[4:]
-    result = nn(dza[...], weight[...]) + joined[...].astype(F32)
+    result = grad[...].astype(F32)
     half = CELLS // 2
     for i in range(geo.hg):
         dxg[0, i] = result[i * CELLS : i * CELLS + geo.hg]
@@ -933,7 +947,7 @@
         write(k)
 
 
-def run_last(geo, joined, dza, hid, weight, parts, global_shape, local_shape):
+def run_last(geo, grad, hid, parts, global_shape, local_shape):
     def whole(shape):
         return pl.BlockSpec(shape, lambda s: (0,) * len(shape))
 
@@ -956,14 +970,13 @@
         ]
         + [jax.ShapeDtypeStruct(shape, F32) for shape in shapes],
         in_specs=[
-            pl.BlockSpec((geo.rows, item.shape[1]), lambda s: (s, 0)) for item in (joined, dza, hid)
+            pl.BlockSpec((geo.rows, item.shape[1]), lambda s: (s, 0)) for item in (grad, hid)
         ]
-        + [whole(weight.shape)]
         + [whole(part.shape) for part in parts],
         out_specs=views + views + [whole(shape) for shape in shapes],
         compiler_params=pltpu.CompilerParams(vmem_limit_bytes=VMEM_CAP),
         name="last",
-    )(joined, dza, hid, weight, *parts)
+    )(grad, hid, *parts)
     return outs[:4], [item if turn else item.T for turn, item in zip(upright, outs[4:])]
 
 
@@ -991,6 +1004,18 @@
             self.address = lambda k: {
                 "rep": jnp.where(first, rep - low + k, rep - high * wide + k * wide)
             }
+        elif kind == "cross":
+            self.size = wide * (shards // 2)
+            self.me = jnp.where(first, rep // 2, lax.rem(rep, wide)) * (shards // 2) + chip
+
+            def across(k):
+                far = k // (shards // 2)
+                return {
+                    "rep": jnp.where(first, far * 2 + low, high * wide + far),
+                    "fsdp": lax.rem(k, shards // 2) * 2 + core,
+                }
+
+            self.address = across
         else:
             self.size = wide
             self.me = jnp.where(first, rep // 2, lax.rem(rep, wide))
@@ -1062,11 +1087,21 @@
         for hop in range(1, self.reps):
             other = {"rep": lax.rem(rep + hop, self.reps)}
             pl.semaphore_signal(barrier, inc=1, device_id=other, device_id_type=MESH)
+        self.greeted = self.shards + self.reps - 2
+        if any(job.kind == "cross" for job in self.jobs):
+            group = Group("cross", self.reps, self.shards)
+            chips = self.shards // 2
+            for far in range(1, self.reps // 2):
+                for step in range(1, chips):
+                    other = lax.rem(group.me // chips + far, self.reps // 2) * chips
+                    other = group.address(other + lax.rem(group.me + step, chips))
+                    pl.semaphore_signal(barrier, inc=1, device_id=other, device_id_type=MESH)
+                    self.greeted += 1
 
     def open(self):
         if not self.opened:
             self.opened = True
-            pl.semaphore_wait(pltpu.get_barrier_semaphore(), self.shards + self.reps - 2)
+            pl.semaphore_wait(pltpu.get_barrier_semaphore(), self.greeted)
             self.turn(0)
 
     def turn(self, number):
@@ -1111,6 +1146,7 @@
     GROUPS = {
         "pair": "core", "join": "core", "line": "chips", "spread": "chips", "all": "shards",
         "share": "reps", "half": "near", "near": "near", "rest": "others", "others": "others",
+        "cross": "cross",
     }
 
     def __init__(self, kind, reps, shards, sources, out, held, send, recv):
@@ -1141,23 +1177,28 @@
         first = self.core == 0
         if kind == "spread":
             for hop in order[:-1]:
-                self.give(source.at[self.rep], out.at[group.size - hop - 1], hop)
+                self.give(source.at[self.rep], out.at[self.rep, group.size - hop - 1], hop)
         elif kind == "near":
-            self.give(source, out, 1)
+            self.give(out.at[self.rep], out.at[self.rep], 1)
         elif kind == "others":
             low, high = lax.rem(self.rep, 2), self.rep // wide
             partner = jnp.where(
                 first, self.rep + 1 - 2 * low, self.rep + (1 - 2 * high) * wide
             )
-            for hop in order:
-                self.give(source, out.at[self.rep], hop)
-                self.give(self.sources[1], out.at[partner], hop)
+            for hop in order[:-1]:
+                for place in (self.rep, partner):
+                    self.give(out.at[place], out.at[place], hop)
         elif kind == "join":
             for hop in order:
                 for step in range(1, self.chips):
                     chip = lax.rem(self.chip + step, self.chips)
                     self.give(source.at[:, step - 1], out.at[chip, self.core], hop)
                 self.give(self.sources[1], out.at[self.chip, self.core], hop)
+        elif kind == "cross":
+            for hop in order:
+                other = group.other(hop)
+                block = source.at[other // self.chips, lax.rem(other, self.chips)]
+                self.give(block, self.held.at[group.me], hop)
         elif kind in ("all", "share"):
             for hop in order:
                 self.give(source, out.at[group.me], hop)
@@ -1204,11 +1245,11 @@
 def job_shapes(kind, reps, shards, shape):
     chips = shards // 2
     if kind == "spread":
-        return None, (chips - 1,) + shape[1:], chips
-    if kind == "near":
-        return None, shape, 1
-    if kind == "others":
-        return None, (reps,) + shape, reps
+        return None, (reps, chips - 1) + shape[1:], chips
+    if kind in ("near", "others"):
+        return None, shape, reps
+    if kind == "cross":
+        return (shape[0] * shape[1],) + shape[2:], shape[2:], shape[0] * shape[1]
     if kind == "join":
         return None, (chips, 2, reps) + shape[2:], 2 * chips
     if kind == "all":
@@ -1242,6 +1283,8 @@
     extra = []
     arrays = []
     shapes = []
+    targets = []
+    kept = {}
     for kind, sources, start, end in jobs:
         source = sources[0]
         if isinstance(source, int):
@@ -1250,13 +1293,20 @@
             shape, dtype = results[int(source)]
         else:
             shape, dtype = source.shape, source.dtype
-        arrays += [item for item in sources if not isinstance(item, (int, str))]
         held, out, copies = job_shapes(kind, reps, shards, shape)
         shapes.append((out, dtype))
-        results.append(shapes[-1])
-        spaces.append(pltpu.HBM if kind in FAR else pltpu.VMEM)
         extra += [] if held is None else [pltpu.VMEM(held, BF16)]
         extra += [pltpu.SemaphoreType.DMA((copies,))] * 2
+        if kind in ("near", "others") and isinstance(source, int):
+            targets.append(targets[source])
+        else:
+            if kind in ("near", "others"):
+                kept[len(arrays)] = len(results)
+            targets.append(len(results))
+            results.append(shapes[-1])
+            spaces.append(pltpu.HBM if kind in FAR else pltpu.VMEM)
+        arrays += [item for item in sources if not isinstance(item, (int, str))]
+    own_or_job = len(results)
     operands = tuple(operands)
     near = len(operands)
     if side is not None:
@@ -1288,12 +1338,11 @@
                     refs_of.append(sources_in.pop(0))
             held = more.pop(0) if job_shapes(kind, reps, shards, refs_of[0].shape)[0] else None
             made.append(
-                Job(kind, reps, shards, refs_of, outs[own_results + k], held, more.pop(0), more.pop(0))
+                Job(kind, reps, shards, refs_of, outs[targets[k]], held, more.pop(0), more.pop(0))
             )
         beside, main = None, None
-        place = own_results + len(jobs)
         if side is not None:
-            beside = Sums(reps, shards, refs[near + 1], outs[place], more[0:3], more[3:9])
+            beside = Sums(reps, shards, refs[near + 1], outs[own_or_job], more[0:3], more[3:9])
             more = more[9:]
         if sums is not None:
             main = Sums(reps, shards, more[0], outs[-1], more[1:4], more[4:10])
@@ -1311,10 +1360,13 @@
         out_shape=[jax.ShapeDtypeStruct(shape, dtype) for shape, dtype in results],
         in_specs=[pl.BlockSpec(memory_space=pltpu.SMEM)]
         + [pl.BlockSpec(memory_space=pltpu.HBM if k in far else pltpu.VMEM) for k in range(len(operands))]
-        + [pl.BlockSpec(memory_space=pl.ANY)] * len(arrays),
+        + [
+            pl.BlockSpec(memory_space=pltpu.HBM if k in kept else pl.ANY) for k in range(len(arrays))
+        ],
         out_specs=[pl.BlockSpec(memory_space=space) for space in spaces],
         scratch_shapes=extra
         + [item if not isinstance(item, tuple) else pltpu.VMEM(*item) for item in scratch],
+        input_output_aliases={inputs + k: out for k, out in kept.items()},
         compiler_params=pltpu.CompilerParams(vmem_limit_bytes=VMEM_CAP, **params),
         name=name,
     )(live, *operands, *arrays)
@@ -1393,71 +1445,65 @@
         ],
         mid_1, 8,
         jobs=(
-            ("spread", (ha,), 0, 1), ("near", (0,), 1, 2), ("others", (0, 1), 2, 3),
-            ("join", (2, ha), 3, 4),
-            ("spread", (hb,), 0, 2), ("near", (4,), 2, 3), ("others", (4, 5), 3, 5),
-            ("join", (6, hb), 5, None),
-            ("spread", (hc,), 0, 3), ("near", (8,), 3, 5), ("others", (8, 9), 5, None),
-            ("spread", (hd,), 0, 3), ("near", (11,), 3, 5), ("others", (11, 12), 5, None),
-            ("all", (own_norms(first_norms, second_norms),), 1, 5),
-            ("spread", (he_0,), 3, 5), ("spread", (he_1,), 3, 5),
+            ("spread", (ha,), 0, 1), ("near", (0,), 1, 2), ("others", (0,), 2, 3),
+            ("join", (0, ha), 3, 4),
+            ("spread", (hb,), 0, 2), ("near", (4,), 2, 3), ("others", (4,), 3, 5),
+            ("join", (4, hb), 5, None),
+            ("spread", (hc,), 0, 3), ("near", (8,), 3, 5), ("others", (8,), 5, None),
+            ("spread", (hd,), 0, 3), ("near", (11,), 3, 5), ("others", (11,), 5, None),
+            ("all", (own_norms(first_norms, second_norms),), 1, 5), ("spread", (hs,), 3, 5),
         ),
         far=(0, 1),
     )
-    packed, za, wa, wb = more[0], more[1], more[2 + 3], more[2 + 7]
-    far_c, far_d, norms, spread_e0, spread_e1 = (more[2 + k] for k in (10, 13, 14, 15, 16))
-    sa = count = more[-1]
+    packed, za, unused, wa, unused, wb, far_c, far_d, norms, far_s, sa = more
+    count = sa
     wa, wb = rows_of(wa), rows_of(wb)
     norms_1, norms_2 = all_norms(norms, first_norms, second_norms)
     na, nb, nc = norms_1[:, :mid_1], norms_1[:, mid_1 : 2 * mid_1], norms_1[:, 2 * mid_1 :]
     nd, ne = norms_2[:, :mid_2], norms_2[:, mid_2 : 2 * mid_2]
     nf, ns = norms_2[:, 2 * mid_2 : 2 * mid_2 + wide], norms_2[:, 2 * mid_2 + wide :]
-    zb, wc, wd, unused, far_e0, unused, far_e1, spread_e2, spread_f, sb = go(
+    zb, wc, wd, far_s, far_e0, far_e1, far_e2, sb = go(
         "stage_b", stage_b, (count, za, sa, na, wb), [((big, mid_1), BF16)],
         [((geo.halo_total, 3 * mid_1), BF16), acc(mid_1)], mid_1,
         jobs=(
             ("join", (far_c, hc), 0, 2), ("join", (far_d, hd), 0, 2),
-            ("near", (spread_e0,), 0, 1), ("others", (spread_e0, 2), 1, 2),
-            ("near", (spread_e1,), 0, 1), ("others", (spread_e1, 4), 1, 2),
-            ("spread", (he_2,), 0, 2), ("spread", (hf,), 0, 2),
+            ("near", (far_s,), 0, 1), ("others", (2,), 1, 2),
+            ("spread", (he_0,), 0, 2), ("spread", (he_1,), 0, 2), ("spread", (he_2,), 0, 2),
         ),
     )
     wc = rows_of(wc)
-    zc, we_0, we_1, unused, far_e2, spread_s, sc = go(
+    zc, ws, far_e0, far_e1, far_f, sc = go(
         "stage_c", stage_c, (count, zb, sb, nb, wc), [((big, channels), BF16)],
         [((geo.rows, mid_1), BF16), acc(channels)], channels,
         jobs=(
+            ("join", (far_s, hs), 0, 2), ("near", (far_e0,), 0, 1), ("others", (1,), 1, 2),
+            ("near", (far_e1,), 0, 1), ("others", (3,), 1, 2), ("spread", (hf,), 0, 2),
+        ),
+    )
+    wd, ws = rows_of(wd), rows_of(ws)
+    hid, zd, sub, zs, local_s, we_0, we_1, far_e2, we_2, far_f, sd = go(
+        "stage_d", stage_d, (count, zc, sc, nc, packed, wd, ws),
+        [
+            ((big, channels), BF16), ((big, mid_2), BF16), ((small, channels), BF16),
+            ((small, wide), BF16), stat(wide // 2),
+        ],
+        [((channels // 128, geo.rows, 128), F32), acc(mid_2), acc(wide)], mid_2,
+        jobs=(
             ("join", (far_e0, he_0), 0, 2), ("join", (far_e1, he_1), 0, 2),
-            ("near", (spread_e2,), 0, 1), ("others", (spread_e2, 2), 1, 2), ("spread", (hs,), 0, 2),
+            ("near", (far_e2,), 0, 1), ("others", (2,), 1, 2), ("join", (2, he_2), 2, None),
+            ("near", (far_f,), 0, 1), ("others", (5,), 1, 2),
         ),
     )
-    wd = rows_of(wd)
-    hid, zd, sub, we_2, unused, far_s, near_f, sd = go(
-        "stage_d", stage_d, (count, zc, sc, nc, packed, wd),
-        [((big, channels), BF16), ((big, mid_2), BF16), ((small, channels), BF16)],
-        [((channels // 128, geo.rows, 128), F32), acc(mid_2)], mid_2,
-        jobs=(
-            ("join", (far_e2, he_2), 0, 2), ("near", (spread_s,), 0, 1),
-            ("others", (spread_s, 1), 1, 2), ("near", (spread_f,), 1, 2),
-        ),
-    )
     we = tuple(rows_of(item) for item in (we_0, we_1, we_2))
-    ze, zs, local_s, ws, unused, wf, se = go(
-        "stage_e", stage_e, (count, zd, sd, nd, *we, sub),
-        [((small, mid_2), BF16), ((small, wide), BF16), stat(wide // 2)],
-        [
-            ((mid_2 // 128, geo.halo, 128), F32), ((small, 9 * mid_2), BF16), acc(mid_2), acc(wide),
-        ],
-        mid_2,
-        jobs=(
-            ("join", (far_s, hs), 0, 2), ("others", (spread_f, near_f), 0, 2),
-            ("join", (1, hf), 2, None),
-        ),
-    )
-    wf, ws = rows_of(wf), rows_of(ws)
-    act_e, zf, ss, sf = go(
+    ze, wf, ss, se = go(
+        "stage_e", stage_e, (count, zd, sd, nd, *we), [((small, mid_2), BF16)],
+        [((mid_2 // 128, geo.halo, 128), F32), ((small, 9 * mid_2), BF16), acc(mid_2)], mid_2,
+        jobs=(("join", (far_f, hf), 0, 2),), side=local_s,
+    )
+    wf = rows_of(wf)
+    act_e, zf, sf = go(
         "stage_f", stage_f, (count, ze, se, ne, wf),
-        [((small, mid_2), BF16), ((small, wide), BF16)], [acc(wide)], wide, side=local_s,
+        [((small, mid_2), BF16), ((small, wide), BF16)], [acc(wide)], wide,
     )
     second_g, second_l, grad, local_pool, so = go(
         "stage_out", stage_out,
@@ -1514,7 +1560,7 @@
             ("line", (rest_s,), 0, 2),
         ),
     )
-    wgrad_b, back_a, ngrad_b, unused, rest_d, unused, half_c, line_e, out_f, out_s, qa = go(
+    wgrad_b, back_a, ngrad_b, unused, rest_d, unused, half_c, line_e, out_f, out_s, pair_b, qa = go(
         "stage_b_back", stage_b_back,
         (count, zb, sb, nb, back_b, qb, za, sa, na, wb),
         [pieces(mid_1, 9 * mid_1), ((big, mid_1), BF16), both(mid_1)],
@@ -1526,26 +1572,25 @@
         jobs=(
             ("half", (pair_d,), 0, 1), ("rest", (0,), 1, 2), ("pair", (wgrad_c,), 0, 1),
             ("half", (2,), 1, 2), ("line", (rest_e,), 0, 2), ("share", (line_f,), 0, 2),
-            ("share", (line_s,), 0, 2),
+            ("share", (line_s,), 0, 2), ("pair", ("0",), 3, None),
         ),
     )
     more = go(
-        "stage_a_back", stage_a_back, (count, za, sa, na, back_a, qa, packed),
-        [pieces(mid_1, channels), ((big, mid_1), BF16), both(mid_1)], [],
+        "stage_a_back", stage_a_back, (count, za, sa, na, back_a, qa, packed, joined, wa),
+        [pieces(mid_1, channels), ((big, channels), BF16), both(mid_1)], [((big, mid_1), BF16)],
         jobs=(
-            ("pair", (wgrad_b,), 0, 1), ("half", (0,), 1, 2), ("rest", (1,), 2, 3),
-            ("line", (2,), 3, 4), ("share", (3,), 4, None),
-            ("pair", ("0",), 1, 2), ("half", (5,), 2, 3), ("rest", (6,), 3, 4),
-            ("line", (7,), 4, 5), ("share", (8,), 5, None),
-            ("rest", (half_c,), 0, 1), ("line", (10,), 1, 2), ("share", (11,), 2, None),
-            ("line", (rest_d,), 0, 1), ("share", (13,), 1, None),
+            ("half", (pair_b,), 0, 1), ("cross", (0,), 1, 2), ("share", (1,), 2, None),
+            ("pair", ("0",), 1, 2), ("half", (3,), 2, 3), ("cross", (4,), 3, 4),
+            ("share", (5,), 4, None),
+            ("cross", (half_c,), 0, 1), ("share", (7,), 1, None),
+            ("line", (rest_d,), 0, 1), ("share", (9,), 1, None),
             ("share", (line_e,), 0, None),
         ),
     )
-    dza, ngrad_a = more[1], more[2]
-    out_b, out_a, out_c, out_d, out_e = (more[3 + k] for k in (4, 9, 12, 14, 15))
+    grad, ngrad_a = more[1], more[2]
+    out_b, out_a, out_c, out_d, out_e = (more[3 + k] for k in (2, 6, 8, 10, 11))
     (grad_g, grad_l, first_g, first_l), columns = run_last(
-        geo, joined, dza, hid, wa, (out_a, out_b, out_c, out_d, out_e, out_f, out_s),
+        geo, grad, hid, (out_a, out_b, out_c, out_d, out_e, out_f, out_s),
         global_views.shape, local_views.shape,
     )
     shard = lax.axis_index("fsdp")

time: 526 us -> 501 us (0.952)
  Pallas kernels: 483 us -> 459 us
    pallas_call x13, Pallas kernels: 465 us -> 444 us  [run(): pl.pallas_call(whole, out_shape=[jax.ShapeDtypeStruct(shape, dtype) for s...]
where the time goes in v5:
time: 501 us; the launch traced here: 494 us
  Pallas kernels  459 us (92%)
  local copies, waits for them, and re-layouts  26.6 us (5%)
    pallas_call x13, Pallas kernels, run(): pl.pallas_call(whole, out_shape=[jax.ShapeDtypeStruct(shape, dtype) for s...  444 us
    unnamed x36, local copies, waits for them, and re-layouts  16.9 us
    pallas_call x1, Pallas kernels, run_last(): pl.pallas_call(functools.partial(last_kernel, geo, upright), grid=(geo.sl...  15.8 us

profile of v5, /device:TPU:0, one launch (start us, length us, event | category | flops | bytes accessed | tf_op | source)
XLA Modules:
  0.0 493.7 jit_solution(16871370353986379249)
XLA Ops:
  1.3 0.0 copy-start.11
  1.3 0.0 copy-start.13
  1.3 2.1 copy.44
  3.4 1.6 copy.43
  4.9 3.6 copy.45.refs_2_
  8.5 0.0 copy-done.11
  8.5 0.0 copy-done.13
  8.5 0.1 reshape.117
  8.6 0.6 reshape.139.refs_9_
  9.2 0.0 copy-start.4
  9.2 44.0 %stage_a.1 = (bf16[3200,1024]{1,0:T(8,128)(2,1)}, bf16[3200,256]{1,0:T(8,128)(2,1)}, bf16[4,3,8,1024]{3,2,1,0:T(8,128)(2,1)}, bf16[4,2,4,8,1024]{4,3,2,1,0:T(8,1...) custom-call(s32[1]{0:T(128)S(6)} %copy.60.refs_0_, ...), custom_call_target="tpu_custom_call" | custom-call | tf_op jit(solution)/shard_map/stage_a/pallas_call | solution.py:1358
  53.3 0.9 copy.52
  54.1 0.1 reshape.123
  54.2 0.1 reshape.124
  54.3 0.6 fusion.13
  54.9 0.0 copy-done.4
  54.9 0.8 fusion.10
  55.7 0.0 copy-start.5
  55.7 32.1 %stage_b.1 = (bf16[3200,256]{1,0:T(8,128)(2,1)}, bf16[4,2,4,32,256]{4,3,2,1,0:T(8,128)(2,1)}, bf16[4,2,4,16,1024]{4,3,2,1,0:T(8,128)(2,1)}, bf16[4,3,64,1024]{3,...) custom-call(s32[1]{0:T(128)S(6)} %copy.60.refs_0_, ...), custom_call_target="tpu_custom_call", output_to_operand_aliasing={{3}: (10, {})} | custom-call | tf_op jit(solution)/shard_map/stage_b/pallas_call | solution.py:1358
  87.8 0.0 copy-done.5
  87.8 0.8 copy.47
  88.7 31.3 %stage_c.1 = (bf16[3200,1024]{1,0:T(8,128)(2,1)}, bf16[4,2,4,64,1024]{4,3,2,1,0:T(8,128)(2,1)}, bf16[4,3,16,1536]{3,2,1,0:T(8,128)(2,1)}, bf16[4,3,16,1536]{3,2,...) custom-call(s32[1]{0:T(128)S(6)} %copy.60.refs_0_, ...), custom_call_target="tpu_custom_call", output_to_operand_aliasing={{2}: (8, {}), {3}: (9, {})} | custom-call | tf_op jit(solution)/shard_map/stage_c/pallas_call | solution.py:1358
  119.9 0.6 slice.68.refs_4_.refs_11_
  120.5 40.4 %stage_d.1 = (bf16[3200,1024]{1,0:T(8,128)(2,1)}, bf16[3200,512]{1,0:T(8,128)(2,1)}, bf16[800,1024]{1,0:T(8,128)(2,1)}, bf16[800,2048]{1,0:T(8,128)(2,1)}, f32[8...) custom-call(s32[1]{0:T(128)S(6)} %copy.60.refs_0_, ...), custom_call_target="tpu_custom_call", output_to_operand_aliasing={{7}: (12, {}), {9}: (14, {})} | custom-call | tf_op jit(solution)/shard_map/stage_d/pallas_call | solution.py:1358
  161.0 0.6 fusion.12
  161.6 29.9 %stage_e.1 = (bf16[800,512]{1,0:T(8,128)(2,1)}, bf16[4,2,4,64,512]{4,3,2,1,0:T(8,128)(2,1)}, f32[8,1024]{1,0:T(8,128)}, f32[8,256]{1,0:T(8,128)}) custom-call(s32[1]{0:T(128)S(6)} %copy.60.refs_0_, f32[16,128]{1,0:T(8,128)} %get-tuple-element.117.refs_1_.refs_3_.refs_8_, bf16[3200,512]{1,0:T(8,128)(2,1)} %get-tuple-element.139.refs_2_.refs_7_, ...), custom_call_target="tpu_custom_call" | custom-call | tf_op jit(solution)/shard_map/stage_e/pallas_call | solution.py:1358
  191.5 0.0 copy-start.3
  191.5 15.8 %stage_f.1 = (bf16[800,512]{1,0:T(8,128)(2,1)}, bf16[800,2048]{1,0:T(8,128)(2,1)}, f32[8,1024]{1,0:T(8,128)}) custom-call(s32[1]{0:T(128)S(6)} %copy.60.refs_0_, f32[16,128]{1,0:T(8,128)} %get-tuple-element.117.refs_1_.refs_3_.refs_8_, bf16[800,512]{1,0:T(8,128)(2,1)} %get-tuple-element.146.refs_2_.refs_14_, f32[8,256]{1,0:T(8,128)} %get-tuple-element.147.refs_3_.refs_15_, ...), custom_call_target="tpu_custom_call" | custom-call | tf_op jit(solution)/shard_map/stage_f/pallas_call | solution.py:1358
  207.3 0.6 fusion.11
  207.9 0.0 copy-done.3
  207.9 1.6 copy.48.refs_9_
  209.5 26.5 %stage_out.1 = (bf16[10,7,7,2048]{3,2,1,0:T(8,128)(2,1)}, bf16[20,3,3,2048]{3,2,1,0:T(4,128)(2,1)}, bf16[800,2048]{1,0:T(8,128)(2,1)}, f32[8,512]{1,0:T(8,128)}, f32[24,512]{1,0:T(8,128)}) custom-call(s32[1]{0:T(128)S(6)} %copy.60.refs_0_, f32[16,128]{1,0:T(8,128)} %get-tuple-element.117.refs_1_.refs_3_.refs_8_, ...), custom_call_target="tpu_custom_call" | custom-call | tf_op jit(solution)/shard_map/stage_out/pallas_call | solution.py:1358
  236.0 33.7 %stage_f_back.1 = (bf16[2,4,4,64,512]{4,3,2,1,0:T(8,128)(2,1)}, bf16[2,4,4,64,1024]{4,3,2,1,0:T(8,128)(2,1)}, bf16[800,1024]{1,0:T(8,128)(2,1)}, bf16[800,512]{1...) custom-call(s32[1]{0:T(128)S(6)} %copy.60.refs_0_, ...), custom_call_target="tpu_custom_call" | custom-call | tf_op jit(solution)/shard_map/stage_f_back/pallas_call | solution.py:1358
  269.7 31.6 %stage_e_back.1 = (bf16[2,4,4,16,4608]{4,3,2,1,0:T(8,128)(2,1)}, bf16[3200,512]{1,0:T(8,128)(2,1)}, f32[2,512]{1,0:T(2,128)}, bf16[2,4,64,512]{3,2,1,0:T(8,128)(...) custom-call(s32[1]{0:T(128)S(6)} %copy.60.refs_0_, f32[16,128]{1,0:T(8,128)} %get-tuple-element.117.refs_1_.refs_3_.refs_8_, ...), custom_call_target="tpu_custom_call" | custom-call | tf_op jit(solution)/shard_map/stage_e_back/pallas_call | solution.py:1358
  301.3 0.0 copy-start.6
  301.3 0.0 copy-start.7
  301.3 0.0 copy-start.10
  301.4 43.5 %stage_d_back.1 = (bf16[2,4,4,16,1024]{4,3,2,1,0:T(8,128)(2,1)}, bf16[3200,1024]{1,0:T(8,128)(2,1)}, f32[2,512]{1,0:T(2,128)}, bf16[4,4,16,4608]{3,2,1,0:T(8,128...) custom-call(s32[1]{0:T(128)S(6)} %copy.60.refs_0_, ...), custom_call_target="tpu_custom_call" | custom-call | tf_op jit(solution)/shard_map/stage_d_back/pallas_call | solution.py:1358
  344.9 0.0 copy-done.6
  344.9 0.0 copy-done.7
  344.9 0.0 copy-done.10
  344.9 1.3 fusion.5
  346.2 36.1 %stage_c_back.1 = (bf16[2,4,4,32,256]{4,3,2,1,0:T(8,128)(2,1)}, bf16[3200,256]{1,0:T(8,128)(2,1)}, f32[2,1024]{1,0:T(2,128)}, bf16[4,4,16,1024]{3,2,1,0:T(8,128)...) custom-call(s32[1]{0:T(128)S(6)} %copy.60.refs_0_, ...), custom_call_target="tpu_custom_call" | custom-call | tf_op jit(solution)/shard_map/stage_c_back/pallas_call | solution.py:1358
  382.3 35.4 %stage_b_back.1 = (bf16[2,4,4,8,2304]{4,3,2,1,0:T(8,128)(2,1)}, bf16[3200,256]{1,0:T(8,128)(2,1)}, f32[2,256]{1,0:T(2,128)}, bf16[2,4,16,1024]{3,2,1,0:T(8,128)(...) custom-call(s32[1]{0:T(128)S(6)} %copy.60.refs_0_, ...), custom_call_target="tpu_custom_call" | custom-call | tf_op jit(solution)/shard_map/stage_b_back/pallas_call | solution.py:1358
  417.7 0.0 copy-start.9
  417.8 0.0 copy-start.12
  417.8 43.3 %stage_a_back.1 = (bf16[2,4,4,8,1024]{4,3,2,1,0:T(8,128)(2,1)}, bf16[3200,1024]{1,0:T(8,128)(2,1)}, f32[2,256]{1,0:T(2,128)}, bf16[2,4,8,2304]{3,2,1,0:T(8,128)(...) custom-call(s32[1]{0:T(128)S(6)} %copy.60.refs_0_, ...), custom_call_target="tpu_custom_call" | custom-call | tf_op jit(solution)/shard_map/stage_a_back/pallas_call | solution.py:1358
  461.1 0.0 copy-done.9
  461.1 0.0 copy-done.12
  461.1 1.3 fusion.9
  462.4 15.8 %last.1 = (f32[10,14,14,1024]{3,2,1,0:T(8,128)}, f32[20,6,6,1024]{3,2,1,0:T(8,128)}, bf16[10,14,14,1024]{3,2,1,0:T(8,128)(2,1)}, bf16[20,6,6,1024]{3,2,1,0:T(8,1...) custom-call(bf16[3200,1024]{1,0:T(8,128)(2,1)} %get-tuple-element.18, ...), custom_call_target="tpu_custom_call" | custom-call | tf_op jit(solution)/shard_map/last/pallas_call | solution.py:963
  478.2 0.0 copy-start.1
  478.2 5.8 %copy.51 = f32[20,6,6,1024]{3,0,2,1:T(8,128)} copy(f32[20,6,6,1024]{3,2,1,0:T(8,128)} %get-tuple-element.239) | data formatting | bytes 5898240
  484.0 0.0 copy-start.8
  484.0 0.0 copy-start.2
  484.0 0.0 copy-done.1
  484.0 2.1 copy.49
  486.1 1.2 slice.60
  487.9 0.0 copy-done.8
  488.0 0.6 sqrt_reduce_fusion
  489.2 0.0 copy-done.2
  489.2 1.5 copy.50
  490.7 0.0 copy-done
  490.7 1.4 copy.61
  (7 shorter events, 0.1 us)
Async XLA Ops:
  1.3 7.2 %copy-start.11 = (bf16[2,640]{1,0:T(2,128)(2,1)S(1)}, bf16[2,640]{1,0:T(2,128)(2,1)}, u32[]{:S(2)}) copy-start(bf16[2,640]{1,0:T(2,128)(2,1)} %param.25) | copy-start | bytes 7684
  1.3 7.2 %copy-start.13 = (bf16[2,192]{1,0:T(2,128)(2,1)S(1)}, bf16[2,192]{1,0:T(2,128)(2,1)}, u32[]{:S(2)}) copy-start(bf16[2,192]{1,0:T(2,128)(2,1)} %param.20) | copy-start | bytes 2308
  9.2 45.7 %copy-start.4 = (bf16[4608,64]{0,1:T(8,128)(2,1)S(1)}, bf16[4608,64]{0,1:T(8,128)(2,1)}, u32[]{:S(2)}) copy-start(bf16[4608,64]{0,1:T(8,128)(2,1)} %param.22) | copy-start | bytes 1769476
  55.7 32.1 %copy-start.5 = (bf16[512,256]{1,0:T(8,128)(2,1)S(1)}, bf16[512,256]{1,0:T(8,128)(2,1)}, u32[]{:S(2)}) copy-start(bf16[512,256]{1,0:T(8,128)(2,1)} %param.23) | copy-start | bytes 786436
  191.5 16.4 %copy-start.3 = (bf16[20,3,3,2048]{3,0,2,1:T(8,128)(2,1)S(1)}, bf16[20,3,3,2048]{3,0,2,1:T(8,128)(2,1)}, u32[]{:S(2)}) copy-start(bf16[20,3,3,2048]{3,0,2,1:T(8,128)(2,1)} %param.27) | copy-start | bytes 2211844
  301.3 43.6 %copy-start.6 = (f32[2,2048]{1,0:T(2,128)S(1)}, f32[2,2048]{1,0:T(2,128)}, u32[]{:S(2)}) copy-start(f32[2,2048]{1,0:T(2,128)} %get-tuple-element.215) | copy-start | bytes 49156
  301.3 43.6 %copy-start.7 = (f32[2,2048]{1,0:T(2,128)S(1)}, f32[2,2048]{1,0:T(2,128)}, u32[]{:S(2)}) copy-start(f32[2,2048]{1,0:T(2,128)} %get-tuple-element.216) | copy-start | bytes 49156
  301.3 43.6 %copy-start.10 = (f32[2,512]{1,0:T(2,128)S(1)}, f32[2,512]{1,0:T(2,128)}, u32[]{:S(2)}) copy-start(f32[2,512]{1,0:T(2,128)} %get-tuple-element.214) | copy-start | bytes 12292
  417.7 43.3 %copy-start.9 = (f32[2,1024]{1,0:T(2,128)S(1)}, f32[2,1024]{1,0:T(2,128)}, u32[]{:S(2)}) copy-start(f32[2,1024]{1,0:T(2,128)} %get-tuple-element.208) | copy-start | bytes 24580
  417.8 43.3 %copy-start.12 = (f32[2,256]{1,0:T(2,128)S(1)}, f32[2,256]{1,0:T(2,128)}, u32[]{:S(2)}) copy-start(f32[2,256]{1,0:T(2,128)} %get-tuple-element.207) | copy-start | bytes 6148
  478.2 5.9 %copy-start.1 = (bf16[20,6,6,1024]{3,2,1,0:T(8,128)(2,1)S(1)}, bf16[20,6,6,1024]{3,2,1,0:T(8,128)(2,1)}, u32[]{:S(2)}) copy-start(bf16[20,6,6,1024]{3,2,1,0:T(8,128)(2,1)} %get-tuple-element.235) | copy-start | bytes 4423684
  484.0 3.9 copy-start.8
  484.0 5.2 %copy-start.2 = (bf16[20,3,3,2048]{3,2,1,0:T(4,128)(2,1)S(1)}, bf16[20,3,3,2048]{3,2,1,0:T(4,128)(2,1)}, u32[]{:S(2)}) copy-start(bf16[20,3,3,2048]{3,2,1,0:T(4,128)(2,1)} %get-tuple-element.237) | copy-start | bytes 2211844
  484.0 6.7 %copy-start = (bf16[10,7,7,2048]{3,2,1,0:T(8,128)(2,1)S(1)}, bf16[10,7,7,2048]{3,2,1,0:T(8,128)(2,1)}, u32[]{:S(2)}) copy-start(bf16[10,7,7,2048]{3,2,1,0:T(8,128)(2,1)} %get-tuple-element.277) | copy-start | bytes 6021124
